TPU v7x, 32 devices: a whole 2x2x4 slice. The times are simulated.
32 devices in a mesh: dp: 8 (over z, x), tensor: 4 (over y, core).
Axes of the slice: x: 2, y: 2, z: 4, core: 2. Of those that a mesh axis runs over, the one named last changes fastest.
Arguments:
- inputs: bfloat16 [16, 1024, 1024], P('dp'), may hold values from -6 to 6
- segment_ids: int32 [16, 1024], P('dp'), may hold values from 0 to 7, never falling along the last dimension, each value on 1 to 512 neighbouring positions
- doc_offsets: int32 [16, 8], P('dp'), may hold values from 0 to 3071
- time_index: int32 [16], P('dp'), may hold values from 0 to 999
- w_qkv: bfloat16 [3, 1024, 1024], P(None, 'dp', 'tensor'), may hold values from -0.1875 to 0.1875
- w_out: bfloat16 [1024, 1024], P('tensor', 'dp'), may hold values from -0.75 to 0.75
- w_up: bfloat16 [1024, 4096], P('dp', 'tensor'), may hold values from -0.1875 to 0.1875
- w_down: bfloat16 [4096, 1024], P('tensor', 'dp'), may hold values from -0.09375 to 0.09375
- w_time: bfloat16 [256, 1024], P(None, 'dp'), may hold values from -0.375 to 0.375
- gain_attn: bfloat16 [1024], P('dp'), may hold values from 0.5 to 1.5
- gain_mlp: bfloat16 [1024], P('dp'), may hold values from 0.5 to 1.5
- cotangent: bfloat16 [16, 1024, 1024], P('dp'), may hold values from -6 to 6
Outputs:
- block_out: bfloat16 [16, 1024, 1024], P('dp', None, 'tensor')
- input_grad: float32 [16, 1024, 1024], P('dp', None, 'tensor')
- grad_qkv: float32 [3, 1024, 1024], P(None, 'dp', 'tensor')
- grad_out: float32 [1024, 1024], P('tensor', 'dp')
- grad_up: float32 [1024, 4096], P('dp', 'tensor')
- grad_down: float32 [4096, 1024], P('tensor', 'dp')
- grad_time: float32 [256, 1024], P(None, 'dp')
- grad_gain_attn: float32 [1024], P('dp')
- grad_gain_mlp: float32 [1024], P('dp')
Inputs may be any that keep to these rules, and one draw needn't show every extreme that they name: `segment_ids`: in each sequence the ids never fall, every id of 0 to 7 occurs, each document has 1 to 512 tokens and one has exactly 512.
All inputs are finite; a program needn't handle non-finite values.
Results may differ from a plain program's by a relative error of at most 0.022.
Values may be sent and summed in bfloat16 or wider, within the bound.
No kernel may reach another device: no remote copies, remote signals or barrier semaphores. Data moves between devices by JAX's collectives and lax.ppermute only.
A program may use at most 192 MiB of HBM per device.

v0:
```python
import functools
import math

import jax
import jax.numpy as jnp
from jax import lax
from jax.experimental import pallas as pl
from jax.experimental.pallas import tpu as pltpu
from jax.sharding import PartitionSpec as P

HEADS = 16
TEMB = 256
BLOCK = 256
LANES = 128
FINE = 64
eps = 1e-05
masked = -1000000000.0
f32 = jnp.float32
bf16 = jnp.bfloat16
VMEM = pl.BlockSpec(memory_space=pltpu.VMEM)
SMEM = pl.BlockSpec(memory_space=pltpu.SMEM)
ANY = pl.BlockSpec(memory_space=pl.ANY)
HBM = pl.BlockSpec(memory_space=pltpu.HBM)


def params(mebibytes):
    return pltpu.CompilerParams(vmem_limit_bytes=mebibytes * 1024 * 1024)


def freqs(width):
    half = width // 2
    return jnp.exp(-math.log(10000.0) * jnp.arange(half, dtype=f32) / half)


def sinusoid(values, width):
    angles = values[..., None] * freqs(width)
    return jnp.concatenate([jnp.sin(angles), jnp.cos(angles)], axis=-1)


def norm_parts(hidden):
    centre = jnp.mean(hidden, axis=-1, keepdims=True)
    centred = hidden - centre
    spread = jnp.mean(centred * centred, axis=-1, keepdims=True)
    inv = lax.rsqrt(spread + eps)
    return centred * inv, inv


def norm_back(unit, inv, gain, grad):
    scaled = grad * gain
    first = jnp.mean(scaled, axis=-1, keepdims=True)
    second = jnp.mean(scaled * unit, axis=-1, keepdims=True)
    return inv * (scaled - first - unit * second)


def positions(segs, offsets):
    seq_len = segs.shape[0]
    index = jnp.arange(seq_len, dtype=jnp.int32)
    member = segs[:, None] == jnp.arange(offsets.shape[0], dtype=jnp.int32)[None, :]
    starts = jnp.min(jnp.where(member, index[:, None], seq_len), axis=0)
    start_tok = jnp.sum(jnp.where(member, starts[None, :], 0), axis=1)
    offset_tok = jnp.sum(jnp.where(member, offsets[None, :], 0), axis=1)
    return offset_tok + index - start_tok


def dot(left, right, left_dim, right_dim):
    return lax.dot_general(
        left, right, (((left_dim,), (right_dim,)), ((), ())), preferred_element_type=f32
    )


def like(shape, dtype):
    return jax.ShapeDtypeStruct(shape, dtype)


def rows_at(block):
    return pl.ds(pl.multiple_of(block * BLOCK, BLOCK), BLOCK)


def exchanged(core, block, blocks):
    return lax.rem(block + core * (blocks // 2), blocks)


def call(kernel, name, mebibytes, flops, outs, args, scratch=(), after=(), stored=(), direct=()):
    count, first, total = len(args), len(args) + len(after), len(outs)

    def body(*refs):
        results = list(refs[first : first + total])
        token = refs[first + total]
        rest = refs[first + total + 1 :]
        sems = rest[-1]
        copies = []

        def store(k, rows=slice(None)):
            mine = rest[stored.index(k)]
            copies.append(
                pltpu.make_async_copy(mine.at[rows], refs[first + k].at[rows], sems.at[len(copies)])
            )
            copies[-1].start()

        for at, k in enumerate(stored):
            results[k] = rest[at]
        extra = rest[len(stored) : -1]
        if stored:
            kernel(*refs[:count], *results, *extra, store=store)
        else:
            kernel(*refs[:count], *results, *extra)
        token[...] = jnp.zeros(token.shape, token.dtype)
        for copy in copies:
            copy.wait()

    moved = sum(a.size * a.dtype.itemsize for a in args) + sum(
        math.prod(o.shape) * o.dtype.itemsize for o in outs
    )
    return pl.pallas_call(
        body,
        out_shape=(
            *(
                pltpu.HBM(o.shape, o.dtype) if k in stored else o for k, o in enumerate(outs)
            ),
            like((8, LANES), f32),
        ),
        in_specs=[SMEM]
        + [HBM if k in direct else VMEM for k in range(1, count)]
        + [ANY] * len(after),
        out_specs=tuple(HBM if k in stored else VMEM for k in range(total)) + (VMEM,),
        scratch_shapes=[pltpu.VMEM(outs[k].shape, outs[k].dtype) for k in stored]
        + list(scratch)
        + [pltpu.SemaphoreType.DMA((8,))],
        compiler_params=params(mebibytes),
        cost_estimate=pl.CostEstimate(
            flops=flops // 1024, bytes_accessed=moved // 1024, transcendentals=0
        ),
        name=name,
    )(
        *(
            pltpu.with_memory_space_constraint(a, pltpu.HBM) if k in direct else a
            for k, a in enumerate(args)
        ),
        *after,
    )


def load(given, held, sems):
    copies = [
        pltpu.make_async_copy(ref, mine, sems.at[k])
        for k, (ref, mine) in enumerate(zip(given, held, strict=True))
    ]
    for copy in copies:
        copy.start()
    return lambda: copies.pop(0).wait()


def held_like(arrays):
    return [*(pltpu.VMEM(a.shape, a.dtype) for a in arrays), pltpu.SemaphoreType.DMA((len(arrays),))]


def pieces(table):
    first = table.astype(bf16)
    rest = table - first.astype(f32)
    second = rest.astype(bf16)
    return jnp.concatenate([first, second, (rest - second.astype(f32)).astype(bf16)], axis=0)


def embed_kernel(seqs, meta, inputs, place, freq, *refs, store):
    outs, held, sems = refs[:seqs], refs[seqs], refs[seqs + 1]
    copies = [pltpu.make_async_copy(inputs.at[i], held.at[i], sems.at[i]) for i in range(seqs)]
    for copy in copies:
        copy.start()
    seq_len = inputs.shape[1]
    half = freq.shape[1]
    blocks = seq_len // BLOCK
    step = lax.broadcasted_iota(jnp.int32, (FINE, half), 0).astype(f32)
    angles = (step * (FINE * freq[...]), step * freq[...])
    coarse, fine = (pieces(jnp.concatenate([jnp.sin(t), jnp.cos(t)], axis=1)) for t in angles)
    entry = lax.rem(lax.broadcasted_iota(jnp.int32, (BLOCK, 3 * FINE), 1), FINE)
    for i in range(seqs):

        def add(block, _, i=i):
            source = rows_at(exchanged(meta[0], block, blocks))
            at = place[i, source, :]
            a = dot((entry == at // FINE).astype(bf16), coarse, 1, 0)
            b = dot((entry == lax.rem(at, FINE)).astype(bf16), fine, 1, 0)
            sin_a, cos_a, sin_b, cos_b = a[:, :half], a[:, half:], b[:, :half], b[:, half:]
            x = held[i, source, :].astype(f32)
            outs[i][rows_at(block), :half] = x[:, :half] + (sin_a * cos_b + cos_a * sin_b)
            outs[i][rows_at(block), half:] = x[:, half:] + (cos_a * cos_b - sin_a * sin_b)
            return 0

        copies[i].wait()
        lax.fori_loop(0, blocks, add, 0)
        store(i)


def embedded(meta, inputs, place):
    seqs, seq_len, width = inputs.shape
    return call(
        functools.partial(embed_kernel, seqs),
        "embed",
        18,
        200 * inputs.size,
        (like((seq_len, width), f32),) * seqs,
        (meta, inputs, place[:, :, None], freqs(width)[None]),
        [pltpu.VMEM(inputs.shape, bf16), pltpu.SemaphoreType.DMA((seqs,))],
        stored=tuple(range(seqs)),
        direct=(1,),
    )


def window(meta, block, blocks):
    first, last = meta[2 + block], meta[2 + blocks + block]
    low, high = jnp.int32(blocks), jnp.int32(0)
    for j in range(blocks):
        hit = (meta[2 + blocks + j] >= first) & (meta[2 + j] <= last)
        low = jnp.where(hit & (low == blocks), j, low)
        high = jnp.where(hit, j + 1, high)
    return low, high - low


def set_bias(bias, seg_col, seg_row, block, low, count):
    keys = jnp.concatenate([seg_row[pl.ds(low + j, 1), :] for j in range(count)], axis=1)
    bias[:, : count * BLOCK] = jnp.where(seg_col[rows_at(block), :] == keys, 0.0, masked)


def project_kernel(shard, meta, entered, cond, gain, w1, h0, n1, qkv, inv, store):
    blocks = entered.shape[0] // BLOCK
    for block in range(blocks):
        rows = slice(block * BLOCK, (block + 1) * BLOCK)
        h = entered[rows, :] + cond[...]
        unit, scale = norm_parts(h)
        if block < blocks // 2:
            h0[rows, :] = h
        normed = (unit * gain[...]).astype(bf16)
        n1[rows, :] = normed
        inv[rows, LANES - 1 :] = scale
        terms = dot(normed, w1[:, : 3 * shard], 1, 0)
        qkv[rows_at(exchanged(meta[0], block, blocks)), :] = terms.astype(bf16)
        if block < blocks // 2:
            store(0, rows)
        store(1, rows)


def projected(meta, entered, cond, gain, w1, shard, after):
    seq_len, width = entered.shape
    return call(
        functools.partial(project_kernel, shard),
        "project",
        18,
        6 * seq_len * width * shard,
        (
            like((seq_len // 2, width), f32),
            like((seq_len, width), bf16),
            like((seq_len, 3 * shard), bf16),
            like((seq_len, LANES), f32),
        ),
        (meta, entered, cond, gain, w1),
        after=after,
        stored=(0, 1),
    )


def attend_kernel(shard, scale, meta, qkv, inv, seg_col, seg_row, a, lse, bias):
    seq_len = qkv.shape[0]
    blocks = seq_len // BLOCK
    lse[:, LANES - 1 :] = inv[:, LANES - 1 :]
    even = lax.broadcasted_iota(jnp.int32, (BLOCK, LANES), 1) < LANES // 2

    def attend(block, _):
        own = rows_at(exchanged(meta[0], block, blocks))
        low, count = window(meta, block, blocks)
        for size in range(1, blocks + 1):

            @pl.when(count == size)
            def _(size=size):
                span = size * BLOCK
                keys = pl.ds(pl.multiple_of(low * BLOCK, BLOCK), span)
                set_bias(bias, seg_col, seg_row, block, low, size)
                for pair in range(shard // LANES):
                    at = pair * LANES
                    query = qkv[rows_at(block), at : at + LANES] * jnp.bfloat16(scale)
                    key = qkv[keys, shard + at : shard + at + LANES]
                    value = qkv[keys, 2 * shard + at : 2 * shard + at + LANES]
                    outs = []
                    for e in range(2):
                        picked = jnp.where(even == (e == 0), query, jnp.bfloat16(0))
                        scores = dot(picked, key, 1, 1) + bias[:, :span]
                        top = jnp.max(scores, axis=1, keepdims=True)
                        expo = jnp.exp(scores - top)
                        denom = jnp.sum(expo, axis=1, keepdims=True)
                        outs.append(dot(expo.astype(bf16), value, 1, 0) * (1.0 / denom))
                        head = 2 * pair + e
                        lse[rows_at(block), head : head + 1] = top + jnp.log(denom)
                    a[own, at : at + LANES] = jnp.where(even, outs[0], outs[1]).astype(bf16)

        return 0

    lax.fori_loop(0, blocks, attend, 0)


def attended(meta, qkv, inv, seg_col, seg_row, shard, scale, after):
    seq_len = qkv.shape[0]
    return call(
        functools.partial(attend_kernel, shard, scale),
        "attend",
        10,
        8 * seq_len * seq_len * shard,
        (like((seq_len, shard), bf16), like((seq_len, LANES), f32)),
        (meta, qkv, inv, seg_col, seg_row),
        [pltpu.VMEM((BLOCK, seq_len), f32)],
        after,
    )


def out_kernel(meta, count, *refs):
    mixed, weights, keep, send = refs[:count], refs[count : 2 * count], refs[-2], refs[-1]
    half = keep.shape[0]
    for at in range(0, half, BLOCK):
        for base, out in ((half, send), (0, keep)):
            term = 0.0
            for a, w in zip(mixed, weights, strict=True):
                term = term + dot(a[base + at : base + at + BLOCK, :], w[...], 1, 1)
            out[at : at + BLOCK, :] = term.astype(out.dtype)


def projected_out(meta, mixed, weights, after):
    seq_len, shard = mixed[0].shape
    width = weights[0].shape[0]
    return call(
        lambda m, *refs: out_kernel(m, len(mixed), *refs),
        "project_out",
        7,
        2 * seq_len * width * shard * len(mixed),
        (like((seq_len // 2, width), bf16),) * 2,
        (meta, *mixed, *weights),
        after=after,
    )


def middle_kernel(meta, h0, keep, got, gain, h1, n2, inv, store):
    for at in range(0, keep.shape[0], BLOCK):
        rows = slice(at, at + BLOCK)
        h = h0[rows, :] + (keep[rows, :].astype(f32) + got[rows, :].astype(f32))
        unit, scale = norm_parts(h)
        inv[rows, :1] = scale
        h1[rows, :] = h
        n2[rows, :] = (unit * gain[...]).astype(bf16)
    store(0)


def middle(meta, h0, keep, got, gain, after):
    return call(
        middle_kernel,
        "middle",
        10,
        20 * keep.size,
        (like(keep.shape, f32), like(keep.shape, bf16), like((keep.shape[0], LANES), f32)),
        (meta, h0, keep, got, gain),
        after=after,
        stored=(0,),
    )


def split_features(core, term, keep, send):
    groups, _, part = keep.shape
    for g in range(groups):
        first = term[:, 2 * g * part : (2 * g + 1) * part]
        second = term[:, (2 * g + 1) * part : (2 * g + 2) * part]
        keep[g] = jnp.where(core == 0, first, second)
        send[g] = jnp.where(core == 0, second, first)


def hidden_kernel(
    meta,
    n2_own,
    n2_other,
    cot,
    w2,
    h1,
    d_keep,
    d_send,
    grad,
    keep,
    send,
    act,
    d_hid,
    held,
    sems,
    store,
):
    ready = load([h1], [held], sems)
    hid = w2.shape[1] // 2
    half, width = n2_own.shape
    chips = keep.shape[0]
    chunk = min(512, hid)
    own = pl.multiple_of(meta[0] * half, BLOCK)
    other = pl.multiple_of((1 - meta[0]) * half, BLOCK)
    for first, base, n2, d_n2 in ((half, other, n2_other, d_send), (0, own, n2_own, d_keep)):
        if first == 0:
            ready()
        for at in range(0, half, BLOCK):
            rows = slice(at, at + BLOCK)
            mine = slice(first + at, first + at + BLOCK)
            d_out = cot[pl.ds(base + at, BLOCK), :]
            for col in range(0, hid, chunk):
                u = dot(n2[rows, :], w2[:, col : col + chunk], 1, 0)
                d_act = dot(d_out, w2[:, hid + col : hid + col + chunk], 1, 0)
                cdf = 0.5 + 0.5 * lax.erf(u * (0.5**0.5))
                act[mine, col : col + chunk] = (u * cdf).astype(bf16)
                slope = cdf + u * (jnp.exp(-0.5 * u * u) * (0.5 / math.pi) ** 0.5)
                d_hid[mine, col : col + chunk] = (d_act * slope).astype(bf16)
            d_n2[rows, :] = dot(d_hid[mine, :], w2[:, :hid], 1, 1).astype(bf16)
            term = dot(act[mine, :], w2[:, hid:], 1, 1)
            if first == 0:
                term = term + held[rows, :] * (1.0 / chips)
            split_features(
                meta[0], term.astype(bf16), keep.at[:, mine, :], send.at[:, mine, :]
            )
    store(3)
    store(4)
    for at in range(0, width, BLOCK):
        cols = slice(at, at + BLOCK)
        up = dot(n2_own[:, cols], d_hid[:half, :], 0, 0)
        up = up + dot(n2_other[:, cols], d_hid[half:, :], 0, 0)
        grad[cols, :hid] = up.astype(bf16)
        down = dot(cot[pl.ds(own, half), cols], act[:half, :], 0, 0)
        down = down + dot(cot[pl.ds(other, half), cols], act[half:, :], 0, 0)
        grad[cols, hid:] = down.astype(bf16)
        store(2, cols)


def hidden_layer(meta, n2, cot, w2, h1, chips, after):
    half, width = n2[0].shape
    hid = w2.shape[1] // 2
    split = like((chips, 2 * half, width // (2 * chips)), bf16)
    d_n2 = like((half, width), bf16)
    return call(
        hidden_kernel,
        "hidden_layer",
        28,
        24 * half * width * hid,
        (d_n2, d_n2, like((width, 2 * hid), bf16), split, split),
        (meta, *n2, cot, w2, h1),
        [*(pltpu.VMEM((2 * half, hid), bf16) for _ in range(2)), *held_like([h1])],
        after,
        (2, 3, 4),
        (5,),
    )


def middle_back_kernel(meta, low, got, n2, inv1, cot, gain, d_low, sums):
    half = n2.shape[0]
    base = pl.multiple_of(meta[0] * half, BLOCK)
    ungain = 1.0 / gain[...]
    total = jnp.zeros(sums.shape, f32)
    for at in range(0, half, BLOCK):
        rows = slice(at, at + BLOCK)
        d_n2 = low[rows, :].astype(f32) + got[rows, :].astype(f32)
        unit = n2[rows, :].astype(f32) * ungain
        total = total + jnp.sum(d_n2 * unit, axis=0, keepdims=True)
        d_h = norm_back(unit, inv1[rows, :1], gain[...], d_n2)
        d_h = d_h + cot[pl.ds(base + at, BLOCK), :].astype(f32)
        d_low[rows, :] = d_h.astype(bf16)
    sums[...] = total


def middle_back(meta, low, got, n2, inv1, cot, gain, after):
    return call(
        middle_back_kernel,
        "middle_back",
        12,
        30 * n2.size,
        (like(n2.shape, bf16), like((1, n2.shape[1]), f32)),
        (meta, low, got, n2, inv1, cot, gain),
        after=after,
    )


def attend_back_kernel(
    shard,
    scale,
    seq,
    seqs,
    n_seqs,
    meta,
    low_own,
    low_other,
    w1,
    qkv,
    a,
    lse,
    seg_col,
    seg_row,
    n1,
    gain,
    gain_sum,
    grads,
    keep,
    send,
    d_mix,
    total,
    bias,
    d_qkv,
    *loads,
    store,
):
    ready = load((qkv, lse, n1), loads[:-1], loads[-1])
    qkv, lse, n1 = loads[:-1]
    seq_len = a.shape[0]
    blocks = seq_len // BLOCK
    per = blocks // 2
    for block in range(per):
        w_out_t = w1[:, 3 * shard : 4 * shard]
        rows = slice(block * BLOCK, (block + 1) * BLOCK)
        d_mix[rows, :] = dot(low_own[rows, :], w_out_t, 1, 0).astype(bf16)
        after = slice((block + per) * BLOCK, (block + per + 1) * BLOCK)
        d_mix[after, :] = dot(low_other[rows, :], w_out_t, 1, 0).astype(bf16)
    ready()
    ready()
    total[...] = jnp.zeros(total.shape, f32)
    even = lax.broadcasted_iota(jnp.int32, (BLOCK, LANES), 1) < LANES // 2

    def attend(block, _):
        own = rows_at(exchanged(meta[0], block, blocks))
        low, count = window(meta, block, blocks)
        for size in range(1, blocks + 1):

            @pl.when(count == size)
            def _(size=size):
                span = size * BLOCK
                keys = pl.ds(pl.multiple_of(low * BLOCK, BLOCK), span)
                set_bias(bias, seg_col, seg_row, block, low, size)
                for pair in range(shard // LANES):
                    at = pair * LANES
                    query = qkv[rows_at(block), at : at + LANES] * jnp.bfloat16(scale)
                    key = qkv[keys, shard + at : shard + at + LANES]
                    value = qkv[keys, 2 * shard + at : 2 * shard + at + LANES]
                    grad = d_mix[own, at : at + LANES]
                    product = grad.astype(f32) * a[own, at : at + LANES].astype(f32)
                    d_query = []
                    d_key = d_value = 0.0
                    for e in range(2):
                        side = even == (e == 0)
                        picked = jnp.where(side, query, jnp.bfloat16(0))
                        picked_grad = jnp.where(side, grad, jnp.bfloat16(0))
                        delta = jnp.sum(jnp.where(side, product, 0.0), axis=1, keepdims=True)
                        head = 2 * pair + e
                        scores = dot(picked, key, 1, 1) + bias[:, :span]
                        probs = jnp.exp(scores - lse[rows_at(block), head : head + 1])
                        d_probs = dot(picked_grad, value, 1, 1)
                        d_scores = (probs * (d_probs - delta)).astype(bf16)
                        d_query.append(dot(d_scores, key, 1, 0))
                        d_key = d_key + dot(d_scores, picked, 0, 0)
                        d_value = d_value + dot(probs.astype(bf16), picked_grad, 0, 0)
                    total[keys, at : at + LANES] += d_key
                    total[keys, shard + at : shard + at + LANES] += d_value
                    d_qkv[own, at : at + LANES] = (
                        jnp.where(even, d_query[0], d_query[1]) * scale
                    ).astype(bf16)

        return 0

    lax.fori_loop(0, blocks, attend, 0)
    share = 1.0 / keep.shape[0]
    unit_sum = term_sum = jnp.zeros((1, n1.shape[1]), f32)
    ungain = 1.0 / gain[...]
    ready()
    for block in range(blocks):
        rows = slice(block * BLOCK, (block + 1) * BLOCK)
        d_qkv[rows, shard:] = total[rows_at(exchanged(meta[0], block, blocks)), :].astype(bf16)
        d_n1 = dot(d_qkv[rows, :], w1[:, : 3 * shard], 1, 1)
        unit = n1[rows, :].astype(f32) * ungain
        inv = lse[rows, LANES - 1 :]
        unit_sum = unit_sum + jnp.sum(d_n1 * unit, axis=0, keepdims=True)
        term = norm_back(unit, inv, gain[...], d_n1)
        if block < per:
            term = term + share * low_own[rows, :].astype(f32)
        term_sum = term_sum + jnp.sum(term, axis=0, keepdims=True)
        split_features(meta[0], term.astype(bf16), keep.at[:, rows, :], send.at[:, rows, :])
    row = lax.broadcasted_iota(jnp.int32, (LANES, n1.shape[1]), 0)
    table = jnp.where(row == meta[1] * seqs + seq, term_sum, 0.0)
    table = jnp.where(row == n_seqs, unit_sum, table)
    table = jnp.where(row == n_seqs + 1, gain_sum[...], table)
    grads[:, 4 * shard :] = table.T.astype(bf16)
    store(1)
    store(2)
    half = low_own.shape[0]
    for at in range(0, n1.shape[1], BLOCK):
        cols = slice(at, at + BLOCK)
        grads[cols, : 3 * shard] = dot(n1[:, cols], d_qkv[...], 0, 0).astype(bf16)
        proj = dot(low_own[:, cols], a[:half, :], 0, 0)
        proj = proj + dot(low_other[:, cols], a[half:, :], 0, 0)
        grads[cols, 3 * shard : 4 * shard] = proj.astype(bf16)
        store(0, cols)


def attended_back(
    meta, low, w1, kept, seg_col, seg_row, n1, gain, gain_sum, scale, groups, place, after
):
    qkv, a, lse = kept
    seq_len, shard = a.shape
    width = w1.shape[0]
    split = like((groups, seq_len, width // (2 * groups)), bf16)
    return call(
        functools.partial(attend_back_kernel, shard, scale, *place),
        "attend_back",
        36,
        16 * seq_len * width * shard + 20 * seq_len * seq_len * shard,
        (like((width, 4 * shard + LANES), bf16), split, split),
        (meta, *low, w1, qkv, a, lse, seg_col, seg_row, n1, gain, gain_sum),
        [
            pltpu.VMEM((seq_len, shard), bf16),
            pltpu.VMEM((seq_len, 2 * shard), f32),
            pltpu.VMEM((BLOCK, seq_len), f32),
            pltpu.VMEM((seq_len, 3 * shard), bf16),
            *held_like((qkv, lse, n1)),
        ],
        after,
        (0, 1, 2),
        (4, 6, 9),
    )


def assemble_kernel(spots, *refs):
    come, full, sems = refs[:-2], refs[-2], refs[-1]
    copies = []
    for k, ref in enumerate(come):
        rows = ref.shape[0]
        at = pl.ds(pl.multiple_of(spots[k], rows), rows)
        copies.append(pltpu.make_async_copy(ref, full.at[at, :], sems.at[k]))
    for copy in copies:
        copy.start()
    for copy in copies:
        copy.wait()


def assembled(spots, come):
    rows, cols = sum(c.shape[0] for c in come), come[0].shape[1]
    return pl.pallas_call(
        assemble_kernel,
        out_shape=like((rows, cols), come[0].dtype),
        in_specs=[SMEM] + [HBM] * len(come),
        out_specs=ANY,
        scratch_shapes=[pltpu.SemaphoreType.DMA((len(come),))],
        compiler_params=params(2),
        cost_estimate=pl.CostEstimate(
            flops=0, bytes_accessed=rows * cols // 16, transcendentals=0
        ),
        name="assemble",
    )(spots, *(pltpu.with_memory_space_constraint(c, pltpu.HBM) for c in come))


def pack_kernel(seqs, times, *refs):
    given, first, second, held, sems = refs[:6], refs[6], refs[7], refs[8:-1], refs[-1]
    copies = [
        pltpu.make_async_copy(ref, mine, sems.at[k])
        for k, (ref, mine) in enumerate(zip(given, held, strict=True))
    ]
    for copy in copies:
        copy.start()
    for copy in copies:
        copy.wait()
    w_qkv, w_out, w_time, w_up, w_down, gains = held
    shard = w_qkv.shape[2]
    rows = first.shape[0]
    for c in range(3):
        first[:, c * shard : (c + 1) * shard] = w_qkv[c]
    at = 3 * shard
    for block in (w_out, w_time):
        first[:, at : at + block.shape[0]] = block[...].astype(f32).T.astype(bf16)
        at += block.shape[0]
    row = lax.broadcasted_iota(jnp.int32, (LANES, rows), 0)
    marks = jnp.zeros((LANES, rows), f32)
    for k in range(2):
        marks = jnp.where(row == k, gains[k : k + 1, :].astype(f32), marks)
    for i in range(seqs):
        for k, part in enumerate((times[i] // 32, lax.rem(times[i], 32))):
            marks = jnp.where(row == 2 + 2 * i + k, part.astype(f32), marks)
    first[:, at:] = marks.T.astype(bf16)
    hid = w_up.shape[1]
    second[:, :hid] = w_up[...]
    second[:, hid:] = w_down[...].astype(f32).T.astype(bf16)


def packed(times, *given):
    w_qkv, w_out, w_time, w_up, _, _ = given
    rows = w_up.shape[0]
    cols = 3 * w_qkv.shape[2] + w_out.shape[0] + w_time.shape[0] + LANES
    return call(
        functools.partial(pack_kernel, times.shape[0]),
        "pack",
        8,
        0,
        (like((rows, cols), bf16), like((rows, 2 * w_up.shape[1]), bf16)),
        (times, *given),
        [*(pltpu.VMEM(g.shape, g.dtype) for g in given), pltpu.SemaphoreType.DMA((len(given),))],
        direct=tuple(range(1, 1 + len(given))),
    )


class Ring:
    def __init__(self, n):
        self.n = n
        me = lax.axis_index("dp")
        spot = jnp.where(me & 1 == 0, me >> 1, n - 1 - (me >> 1))
        order = list(range(0, n, 2)) + list(range(n - 1, 0, -2))
        self.right = [(order[p], order[(p + 1) % n]) for p in range(n)]
        self.left = [(b, a) for a, b in self.right]

        def at(offset):
            there = spot + offset
            there = jnp.where(there >= n, there - n, jnp.where(there < 0, there + n, there))
            return jnp.where(there < n // 2, 2 * there, 2 * (n - 1 - there) + 1)

        self.near = tuple(at(k) for k in range(1 - n // 2, n // 2 + 1))

    def at(self, offset):
        return self.near[offset + self.n // 2 - 1]

    def gather(self, block):
        n, rows = self.n, block.shape[0]
        come, spots = [block], [self.at(0) * rows]
        from_left = from_right = block
        waited = yield ()
        for hop in range(1, n // 2):
            from_left = lax.ppermute(from_left, "dp", self.right)
            from_right = lax.ppermute(from_right, "dp", self.left)
            waited = yield (from_left, from_right), waited
            (from_left, from_right), waited = gate((from_left, from_right), waited)
            come += [from_left, from_right]
            spots += [self.at(-hop) * rows, self.at(hop) * rows]
        come.append(lax.ppermute(from_left[: rows // 2], "dp", self.right))
        come.append(lax.ppermute(from_right[rows // 2 :], "dp", self.left))
        farthest = self.at(n // 2) * rows
        spots += [farthest, farthest + rows // 2]
        yield tuple(come[-2:]), waited
        yield assembled(jnp.stack(spots).astype(jnp.int32), come)

    def scatter(self, terms):
        n, rows = self.n, terms[0].shape[0] // self.n

        def whole(offset, at, size):
            parts = [
                lax.dynamic_slice_in_dim(t, self.at(offset) * rows + at, size, 0) for t in terms
            ]
            return sum(p.astype(f32) for p in parts)

        def part(offset, at=0, size=rows):
            return whole(offset, at, size).astype(bf16)

        def plus(run, offset, at=0, size=rows):
            return (run.astype(f32) + whole(offset, at, size)).astype(bf16)

        half = rows // 2
        right, left = part(n // 2, 0, half), part(n // 2, half, half)
        for hop in range(1, n // 2 + 1):
            right = lax.ppermute(right, "dp", self.right)
            left = lax.ppermute(left, "dp", self.left)
            waited = yield (right, left)
            (right, left), _ = gate((right, left), waited)
            if hop == 1:
                rest = n // 2 - 1
                right = jnp.concatenate([plus(right, rest, 0, half), part(rest, half, half)])
                left = jnp.concatenate([part(-rest, 0, half), plus(left, -rest, half, half)])
            elif hop < n // 2:
                right = plus(right, n // 2 - hop)
                left = plus(left, hop - n // 2)
        yield whole(0, 0, rows) + right.astype(f32) + left.astype(f32)


def butterfly(value, axis, bit, n):
    return lax.ppermute(value, axis, [(i, i ^ bit) for i in range(n)])


def gate(values, waited):
    return lax.optimization_barrier((values, tuple(waited)))


def swap(value, bit, n):
    return lax.ppermute(value, "tensor", [(i, i ^ bit) for i in range(n)])


def to_features(keep, got, n, waited, pieces=1):
    chip = lax.axis_index("tensor") // 2
    half = keep.shape[1] // 2
    (keep, got), _ = gate((keep, got), waited)
    got = jnp.concatenate([got[:, half:], got[:, :half]], axis=1)
    kept, came = keep, [got]
    bit = 1
    while 2 * bit < n:
        value = kept.astype(f32) + jnp.concatenate(came, axis=1).astype(f32)
        value = value.reshape((-1, 2) + keep.shape[1:])
        mine = (chip // bit) % 2
        kept = lax.dynamic_index_in_dim(value, mine, 1, keepdims=False)
        sent = lax.dynamic_index_in_dim(value, 1 - mine, 1, keepdims=False).astype(bf16)
        bit *= 2
        parts = pieces if 2 * bit >= n else 1
        came = [swap(p, bit, n) for p in jnp.split(sent, parts, axis=1)]
    return kept, came


def shards(
    inputs,
    segment_ids,
    doc_offsets,
    time_index,
    w_qkv,
    w_out,
    w_up,
    w_down,
    w_time,
    gain_attn,
    gain_mlp,
    cotangent,
):
    n_dp = lax.axis_size("dp")
    n_tensor = lax.axis_size("tensor")
    me_dp = lax.axis_index("dp")
    core = lax.axis_index("tensor") % 2
    chips = n_tensor // 2
    seqs_dev, seq_len, width = inputs.shape
    half = seq_len // 2
    blocks = seq_len // BLOCK
    shard = width // n_tensor
    scale = (width // HEADS) ** (-0.5)
    hidden_dev = w_up.shape[1]
    rows = width // n_dp
    n_seqs = n_dp * seqs_dev
    ring = Ring(n_dp)
    seqs = range(seqs_dev)

    metas, seg_cols, seg_rows, places = [], [], [], []
    for i in seqs:
        ids = segment_ids[i]
        metas.append(
            jnp.concatenate(
                [
                    jnp.stack([core, me_dp]).astype(jnp.int32),
                    ids[::BLOCK],
                    ids[BLOCK - 1 :: BLOCK],
                ]
            )
        )
        seg_cols.append(ids[:, None])
        seg_rows.append(ids.reshape(blocks, BLOCK))
        places.append(positions(ids, doc_offsets[i]))
    w1_part, w2_part, _ = packed(
        time_index, w_qkv, w_out, w_time, w_up, w_down, jnp.stack([gain_attn, gain_mlp])
    )
    *entered, _ = embedded(metas[0], inputs, jnp.stack(places))
    cot = [cotangent[i] for i in seqs]
    gather1 = ring.gather(w1_part)
    next(gather1)
    brought, passed = [gather1.send(())[0]], []
    beside = [(*seg_cols, *seg_rows, *cot, *ring.near, *metas), tuple(entered)]
    while not isinstance(w1 := gather1.send(beside.pop(0) if beside else ()), jax.Array):
        brought.append(w1[0])
        passed.append(w1[1])
    early, entered = passed[:2]
    seg_cols, seg_rows, cot = (early[k * seqs_dev : (k + 1) * seqs_dev] for k in range(3))
    ring.near = early[3 * seqs_dev : -seqs_dev]
    metas = early[-seqs_dev:]
    w2_part, _ = gate(w2_part, brought[-2][:1])
    gather2 = ring.gather(w2_part)
    next(gather2)
    brought2 = [gather2.send(())[0]]
    small = w1[:, 4 * shard :]
    temb = sinusoid(time_index.astype(f32), TEMB)
    cond = jnp.sum(temb[:, None, :] * small[None, :, :TEMB].astype(f32), axis=2)
    attn_g = small[:, TEMB].astype(f32)[None]
    mlp_g = small[:, TEMB + 1].astype(f32)[None]
    def exchange_core(value):
        return swap(value, 1, n_tensor)

    def gather_chips(value):
        values = [value]
        bit = 2
        while bit < n_tensor:
            values = values + [swap(v, bit, n_tensor) for v in values]
            bit *= 2
        return values

    def sum_chips(value):
        bit = 2
        low, got = value.astype(bf16), jnp.zeros_like(value, bf16)
        while bit < n_tensor:
            low = (low.astype(f32) + got.astype(f32)).astype(bf16)
            got = swap(low, bit, n_tensor)
            bit *= 2
        return low, got

    h0, n1, kept, h1, inv1, n2 = [], [], [], [], [], []
    w_outs = gather_chips(w1[:, 3 * shard : 4 * shard])
    while not isinstance(w2 := gather2.send(()), jax.Array):
        brought2.append(w2[0])
    brought2 = brought2[-4:]
    after = ()
    for i in seqs:
        h, n, qkv, inv, token = projected(
            metas[i], entered[i], cond[i : i + 1], attn_g, w1, shard, after
        )
        a, lse, token = attended(
            metas[i],
            qkv,
            inv,
            seg_cols[i],
            seg_rows[i],
            shard,
            scale,
            (token, *(brought2[i] if i < 2 else ())),
        )
        after = (token, *w_outs[1:])
        h0.append(h)
        n1.append(n)
        kept.append((qkv, a, lse))
    mixes = [gather_chips(k[1]) for k in kept]
    outs, terms, d_n2, grad2, downs = [], [], [], [], []
    share = 1.0 / chips
    final = seqs_dev - 1

    def out_of(i, after):
        keep, send, token = projected_out(metas[i], mixes[i], w_outs, after)
        outs.append((keep, exchange_core(send)))
        return token

    def middle_of(i, after):
        h, own, inv, token = middle(metas[i], h0[i], *outs[i], mlp_g, after)
        inv1.append(inv)
        h1.append(h)
        n2.append((own, exchange_core(own)))
        return token

    def hidden_of(i, after):
        d_keep, d_send, grad, keep, send, token = hidden_layer(
            metas[i], n2[i], cot[i], w2, h1[i], chips, after
        )
        grad2.append(grad)
        terms.append((d_keep, exchange_core(d_send)))
        downs.append((keep, exchange_core(send)))
        return token

    def sum_of(i, after):
        (keep, got), _ = gate(terms[i], after)
        d_n2.append(sum_chips(keep.astype(f32) + got.astype(f32)))
        return d_n2[i][0]

    for i in seqs:
        token = out_of(i, (token, *(brought2[2] if i == 0 else ())))
    for i in seqs:
        token = middle_of(i, (token, *(brought2[3] if i == 0 else ())))
    for i in seqs:
        token = hidden_of(i, (token,))
        if i < final:
            token = sum_of(i, (token,))
    grad2, _ = gate(grad2, (got for _, got in d_n2))
    sum2 = ring.scatter(grad2)
    hops2 = next(sum2)
    gain_sums, to_inputs, lows = [], [], []

    def middle_back_of(i, after):
        low, gain_sum, token = middle_back(
            metas[i], *d_n2[i], n2[i][0], inv1[i], cot[i], mlp_g, after
        )
        lows.append((low, exchange_core(low)))
        gain_sums.append(gain_sum * share)
        return token

    token = middle_back_of(0, (token,))
    if final:
        token = sum_of(final, (token,))
    hops2 = sum2.send((token,))
    grad1 = []
    for i in seqs:
        grad, keep, send, token = attended_back(
            metas[i],
            lows[i],
            w1,
            kept[i],
            seg_cols[i],
            seg_rows[i],
            n1[i],
            attn_g,
            gain_sums[i],
            scale,
            chips,
            (i, seqs_dev, n_seqs),
            (token,),
        )
        grad1.append(grad)
        to_inputs.append((keep, exchange_core(send)))
        hops2 = sum2.send((token,))
        if i < final:
            token = middle_back_of(i + 1, (token,))
            block_out = [to_features(*pair, n_tensor, (token,)) for pair in downs]
    side = [to_features(*pair, n_tensor, (token,), 2) for pair in to_inputs]
    grad1, _ = gate(grad1, (got for _, came in block_out for got in came))
    sum1 = ring.scatter(grad1)
    hops1 = next(sum1)
    came = side[final][1]
    sent = [got for _, came in side for got in came]
    window = 0
    while not isinstance(hops1, jax.Array):
        latest = hops1
        hops1 = sum1.send((sent.pop(0),) if len(sent) > len(came) else ())
        window += 1
        if window == 1:
            block_out, _ = gate(block_out, latest)
        if window == 2:
            hops2 = sum2.send(latest)
        if window == 3:
            side[0], _ = gate(side[0], latest)
    while not isinstance(hops2, jax.Array):
        hops2 = sum2.send(())
    share1, share2 = hops1, hops2
    sums = share1[:, 4 * shard :]
    bit = 1
    while bit < n_tensor:
        sums = sums + butterfly(sums, "tensor", bit, n_tensor)
        bit *= 2
    small, _ = gate(small, (token,))
    marks = small[::rows, TEMB + 2 : TEMB + 2 + 2 * seqs_dev].astype(f32)
    times = (marks[:, 0::2] * 32 + marks[:, 1::2]).reshape(n_seqs)
    block_out, input_grad = (
        [kept + jnp.concatenate(came, axis=1).astype(f32) for kept, came in pairs]
        for pairs in (block_out, side)
    )
    block_out = jnp.concatenate(block_out).astype(bf16)
    input_grad = jnp.concatenate(input_grad)
    factor = float(n_seqs * seq_len) ** (-0.5)
    temb_all = sinusoid(times, TEMB)
    grad_time = (
        jnp.einsum("st,ds->td", temb_all, sums[:, :n_seqs], precision=lax.Precision.HIGHEST)
        * factor
    )

    def natural(value):
        return jnp.roll(value, core * half, axis=1)

    cols = 3 * shard
    return (
        natural(block_out),
        natural(input_grad),
        jnp.stack([share1[:, c * shard : (c + 1) * shard] for c in range(3)]) * factor,
        share1[:, cols : cols + shard].T * factor,
        share2[:, :hidden_dev] * factor,
        share2[:, hidden_dev:].T * factor,
        grad_time,
        sums[:, n_seqs] * factor,
        sums[:, n_seqs + 1] * factor,
    )


def solution(mesh):
    in_specs = (
        P("dp", None, None),
        P("dp", None),
        P("dp", None),
        P("dp"),
        P(None, "dp", "tensor"),
        P("tensor", "dp"),
        P("dp", "tensor"),
        P("tensor", "dp"),
        P(None, "dp"),
        P("dp"),
        P("dp"),
        P("dp", None, None),
    )
    out_specs = (
        P("dp", None, "tensor"),
        P("dp", None, "tensor"),
        P(None, "dp", "tensor"),
        P("tensor", "dp"),
        P("dp", "tensor"),
        P("tensor", "dp"),
        P(None, "dp"),
        P("dp"),
        P("dp"),
    )
    return jax.shard_map(shards, mesh=mesh, in_specs=in_specs, out_specs=out_specs, check_vma=False)
```

profile of v0, /device:TPU:0, one launch (start us, length us, event | category | flops | bytes accessed | tf_op | source)
XLA Modules:
  0.0 313.8 jit_solution(10681454090775190721)
XLA Ops:
  2.5 2.6 pack.1
  5.1 3.1 collective-permute-start
  10.7 4.7 %slice_bitcast_fusion = (bf16[1024,1024]{1,0:T(8,128)(2,1)}, bf16[1024,1024]{1,0:T(8,128)(2,1)}) fusion(bf16[2,1024,1024]{2,1,0:T(8,128)(2,1)} %param.23), kind=kLoop, calls=%fused_computation.18 | loop fusion | bytes 8388608 | tf_op jit(solution)/shard_map/squeeze | solution.py:849
  16.5 1.5 collective-permute-done.1.refs_2_
  18.1 1.6 collective-permute-start.2
  20.6 9.8 %embed.1 = (f32[1024,1024]{1,0:T(8,128)}, f32[1024,1024]{1,0:T(8,128)}, f32[8,128]{1,0:T(8,128)}) custom-call(s32[10]{0:T(128)S(1)} %get-tuple-element.139.refs_0_, bf16[2,1024,1024]{2,1,0:T(8,128)(2,1)} %refs_1_.3, s32[2,1024,1]{2,1,0:T(8,128)S(1)} %copy.30.refs_2_, f32[1,512]{1,0:T(1,128)S(1)} %multiply_exponential_fusion.refs_3_), custom_call_target="tpu_custom_call" | custom-call | flops 409600 | bytes 12298 | tf_op jit(solution)/shard_map/embed/pallas_call | solution.py:114
  30.4 1.6 collective-permute-start.4
  32.5 6.5 %collective-permute-done.4.refs_5_ = bf16[128,1408]{1,0:T(8,128)(2,1)S(1)} collective-permute-done((bf16[128,1408]{1,0:T(8,128)(2,1)S(1)}, bf16[128,1408]{1,0:T(8,128)(2,1)S(1)}, u32[]{:S(2)}, u32[]{:S(2)}) %collective-permute-start.4) | collective-permute-done | bytes 360480 | tf_op jit(solution)/shard_map/ppermute | solution.py:724
  39.0 1.6 collective-permute-start.8
  41.1 1.6 collective-permute-start.6
  44.5 9.4 %collective-permute-done.6.refs_7_ = bf16[64,1408]{1,0:T(8,128)(2,1)S(1)} collective-permute-done((bf16[64,1408]{1,0:T(8,128)(2,1)S(1)}, bf16[64,1408]{1,0:T(8,128)(2,1)S(1)}, u32[]{:S(2)}, u32[]{:S(2)}) %collective-permute-start.6) | collective-permute-done | bytes 180256 | tf_op jit(solution)/shard_map/ppermute | solution.py:730
  55.4 2.4 assemble.2.refs_4_.refs_3_
  57.8 1.6 collective-permute-start.12
  60.4 1.6 collective-permute-start.11
  62.7 3.4 %project.2 = (f32[512,1024]{1,0:T(8,128)}, bf16[1024,1024]{1,0:T(8,128)(2,1)}, bf16[1024,768]{1,0:T(8,128)(2,1)S(1)}, f32[1024,128]{1,0:T(8,128)S(1)}, f32[8,128]{1,0:T(8,128)S(1)}) custom-call(s32[10]{0:T(128)S(1)} %get-tuple-element.139.refs_0_, f32[1024,1024]{1,0:T(8,128)S(1)} %copy-done.12, f32[1,1024]{1,0:T(1,128)S(1)} %get-tuple-element.347.refs_2_, ...), custom_call_target="tpu_custom_call" | custom-call | flops 1572864 | bytes 13064 | tf_op jit(solution)/shard_map/project/pallas_call | solution.py:114
  66.2 9.0 %attend.2 = (bf16[1024,256]{1,0:T(8,128)(2,1)}, f32[1024,128]{1,0:T(8,128)S(1)}, f32[8,128]{1,0:T(8,128)S(1)}) custom-call(s32[10]{0:T(128)S(1)} %get-tuple-element.139.refs_0_, bf16[1024,768]{1,0:T(8,128)(2,1)S(1)} %get-tuple-element.150.refs_1_.refs_4_, f32[1024,128]{1,0:T(8,128)S(1)} %get-tuple-element.151.refs_2_, s32[1024,1]{1,0:T(8,128)S(1)} %copy-done.9, ...), custom_call_target="tpu_custom_call" | custom-call | flops 2097152 | bytes 3080 | tf_op jit(solution)/shard_map/attend/pallas_call | solution.py:114
  77.6 1.6 collective-permute-start.14
  80.9 2.2 copy-done.11
  83.1 3.4 %project.3 = (f32[512,1024]{1,0:T(8,128)}, bf16[1024,1024]{1,0:T(8,128)(2,1)}, bf16[1024,768]{1,0:T(8,128)(2,1)S(1)}, f32[1024,128]{1,0:T(8,128)S(1)}, f32[8,128]{1,0:T(8,128)S(1)}) custom-call(s32[10]{0:T(128)S(1)} %get-tuple-element.158.refs_0_, f32[1024,1024]{1,0:T(8,128)S(1)} %copy-done.11, f32[1,1024]{1,0:T(1,128)S(1)} %get-tuple-element.346.refs_2_, ...), custom_call_target="tpu_custom_call" | custom-call | flops 1572864 | bytes 13064 | tf_op jit(solution)/shard_map/project/pallas_call | solution.py:114
  86.5 8.1 %attend.3 = (bf16[1024,256]{1,0:T(8,128)(2,1)S(1)}, f32[1024,128]{1,0:T(8,128)S(1)}, f32[8,128]{1,0:T(8,128)S(1)}) custom-call(s32[10]{0:T(128)S(1)} %get-tuple-element.158.refs_0_, bf16[1024,768]{1,0:T(8,128)(2,1)S(1)} %get-tuple-element.161.refs_1_.refs_4_, f32[1024,128]{1,0:T(8,128)S(1)} %get-tuple-element.162.refs_2_, s32[1024,1]{1,0:T(8,128)S(1)} %copy-done.7, ...), custom_call_target="tpu_custom_call" | custom-call | flops 2097152 | bytes 3080 | tf_op jit(solution)/shard_map/attend/pallas_call | solution.py:114
  95.5 2.9 project_out.2
  98.5 1.6 collective-permute-start.17
  102.1 2.3 collective-permute-start.19
  104.3 8.5 %collective-permute-done.17.refs_2_ = bf16[1024,256]{1,0:T(8,128)(2,1)S(1)} collective-permute-done((bf16[1024,256]{1,0:T(8,128)(2,1)S(1)}, bf16[1024,256]{1,0:T(8,128)(2,1)S(1)}, u32[]{:S(2)}, u32[]{:S(2)}) %collective-permute-start.17) | collective-permute-done | bytes 524320 | tf_op jit(solution)/shard_map/ppermute | solution.py:778
  112.8 3.1 project_out.3
  117.0 3.3 %middle.2 = (f32[512,1024]{1,0:T(8,128)}, bf16[512,1024]{1,0:T(8,128)(2,1)}, f32[512,128]{1,0:T(8,128)S(1)}, f32[8,128]{1,0:T(8,128)S(1)}) custom-call(s32[10]{0:T(128)S(1)} %get-tuple-element.139.refs_0_, f32[512,1024]{1,0:T(8,128)S(1)} %copy-done.17, bf16[512,1024]{1,0:T(8,128)(2,1)S(1)} %get-tuple-element.171.refs_2_, ...), custom_call_target="tpu_custom_call" | custom-call | flops 10240 | bytes 7428 | tf_op jit(solution)/shard_map/middle/pallas_call | solution.py:114
  120.9 3.0 assemble.3.refs_4_
  124.1 3.1 %middle.3 = (f32[512,1024]{1,0:T(8,128)}, bf16[512,1024]{1,0:T(8,128)(2,1)S(1)}, f32[512,128]{1,0:T(8,128)S(1)}, f32[8,128]{1,0:T(8,128)S(1)}) custom-call(s32[10]{0:T(128)S(1)} %get-tuple-element.158.refs_0_, f32[512,1024]{1,0:T(8,128)S(1)} %copy-done.18, bf16[512,1024]{1,0:T(8,128)(2,1)S(1)} %copy-done.22, ...), custom_call_target="tpu_custom_call" | custom-call | flops 10240 | bytes 7428 | tf_op jit(solution)/shard_map/middle/pallas_call | solution.py:114
  127.2 18.1 %hidden_layer.2 = (bf16[512,1024]{1,0:T(8,128)(2,1)S(1)}, bf16[512,1024]{1,0:T(8,128)(2,1)S(1)}, bf16[1024,2048]{1,0:T(8,128)(2,1)}, bf16[2,1024,256]{2,1,0:T(8,...) custom-call(s32[10]{0:T(128)S(1)} %get-tuple-element.139.refs_0_, ...), custom_call_target="tpu_custom_call" | custom-call | flops 12582912 | bytes 18432 | tf_op jit(solution)/shard_map/hidden_layer/pallas_call | solution.py:114
  146.0 2.1 collective-permute-done.24
  148.1 1.4 add_convert_fusion.1.refs_6_.refs_1_
  149.5 1.5 collective-permute-start.27
  151.0 18.2 %hidden_layer.3 = (bf16[512,1024]{1,0:T(8,128)(2,1)S(1)}, bf16[512,1024]{1,0:T(8,128)(2,1)}, bf16[1024,2048]{1,0:T(8,128)(2,1)}, bf16[2,1024,256]{2,1,0:T(8,128)...) custom-call(s32[10]{0:T(128)S(1)} %get-tuple-element.158.refs_0_, ...), custom_call_target="tpu_custom_call" | custom-call | flops 12582912 | bytes 18432 | tf_op jit(solution)/shard_map/hidden_layer/pallas_call | solution.py:114
  170.7 4.3 %collective-permute-done.27.refs_2_ = bf16[512,1024]{1,0:T(8,128)(2,1)} collective-permute-done((bf16[512,1024]{1,0:T(8,128)(2,1)}, bf16[512,1024]{1,0:T(8,128)(2,1)}, u32[]{:S(2)}, u32[]{:S(2)}) %collective-permute-start.27) | collective-permute-done | bytes 1048608 | tf_op jit(solution)/shard_map/ppermute | solution.py:778
  175.0 1.6 copy-done.2
  176.6 4.1 %middle_back.2 = (bf16[512,1024]{1,0:T(8,128)(2,1)S(1)}, f32[1,1024]{1,0:T(1,128)S(1)}, f32[8,128]{1,0:T(8,128)}) custom-call(s32[10]{0:T(128)S(1)} %get-tuple-element.139.refs_0_, bf16[512,1024]{1,0:T(8,128)(2,1)} %add_convert_fusion.1.refs_6_.refs_1_, bf16[512,1024]{1,0:T(8,128)(2,1)} %collective-permute-done.27.refs_2_, ...), custom_call_target="tpu_custom_call" | custom-call | flops 15360 | bytes 6408 | tf_op jit(solution)/shard_map/middle_back/pallas_call | solution.py:114
  180.9 1.3 add_convert_fusion.16
  182.2 2.0 collective-permute-start.48
  184.2 1.6 add_convert_fusion.refs_12_.refs_1_
  185.9 1.6 collective-permute-start.26
  187.4 3.4 %collective-permute-done.47 = bf16[64,2048]{1,0:T(8,128)(2,1)S(1)} collective-permute-done((bf16[64,2048]{1,0:T(8,128)(2,1)S(1)}, bf16[64,2048]{1,0:T(8,128)(2,1)S(1)}, u32[]{:S(2)}, u32[]{:S(2)}) %collective-permute-start.47) | collective-permute-done | bytes 262176 | tf_op jit(solution)/shard_map/ppermute | solution.py:755
  190.9 1.7 add_convert_fusion.13
  192.7 1.7 collective-permute-start.50
  195.1 21.0 %attend_back.2 = (bf16[1024,1152]{1,0:T(8,128)(2,1)}, bf16[2,1024,256]{2,1,0:T(8,128)(2,1)}, bf16[2,1024,256]{2,1,0:T(8,128)(2,1)}, f32[8,128]{1,0:T(8,128)S(1)}) custom-call(s32[10]{0:T(128)S(1)} %get-tuple-element.139.refs_0_, bf16[512,1024]{1,0:T(8,128)(2,1)S(1)} %get-tuple-element.210.refs_1_, bf16[512,1024]{1,0:T(8,128)(2,1)S(1)} %collective-permute-done.28.refs_2_, ...), custom_call_target="tpu_custom_call" | custom-call | flops 9437184 | bytes 13840 | tf_op jit(solution)/shard_map/attend_back/pallas_call | solution.py:114
  216.1 2.1 middle_back.3
  220.5 1.5 collective-permute-start.31
  223.8 2.7 add_convert_fusion.4
  230.7 21.3 %attend_back.3 = (bf16[1024,1152]{1,0:T(8,128)(2,1)}, bf16[2,1024,256]{2,1,0:T(8,128)(2,1)}, bf16[2,1024,256]{2,1,0:T(8,128)(2,1)}, f32[8,128]{1,0:T(8,128)}) custom-call(s32[10]{0:T(128)S(1)} %get-tuple-element.158.refs_0_, bf16[512,1024]{1,0:T(8,128)(2,1)S(1)} %get-tuple-element.223.refs_1_, bf16[512,1024]{1,0:T(8,128)(2,1)S(1)} %collective-permute-done.32.refs_2_, ...), custom_call_target="tpu_custom_call" | custom-call | flops 9437184 | bytes 13840 | tf_op jit(solution)/shard_map/attend_back/pallas_call | solution.py:114
  254.8 1.5 collective-permute-start.36
  257.6 2.0 collective-permute-start.34
  260.3 2.5 add_convert_fusion.2
  264.1 2.0 collective-permute-start.54
  267.8 1.9 collective-permute-start.38
  270.8 2.6 fusion.4
  273.4 8.7 %collective-permute-done.39 = bf16[128,1152]{1,0:T(8,128)(2,1)S(1)} collective-permute-done((bf16[128,1152]{1,0:T(8,128)(2,1)S(1)}, bf16[128,1152]{1,0:T(8,128)(2,1)S(1)}, u32[]{:S(2)}, u32[]{:S(2)}) %collective-permute-start.39) | collective-permute-done | bytes 294944 | tf_op jit(solution)/shard_map/ppermute | solution.py:756
  283.0 1.4 collective-permute-start.41
  284.4 1.5 convert_add_fusion.4
  289.7 1.4 add_convert_fusion.8
  291.2 1.8 collective-permute-start.45
  295.8 1.8 collective-permute-start.43
  298.0 1.7 collective-permute-done.46
  304.1 2.1 collective-permute-start.56
  306.1 1.7 maximum_multiply_fusion
  311.6 2.0 fusion.1
  (268 shorter events, 56.7 us)
Async XLA Ops:
  5.1 35.5 %copy-start.25 = (bf16[128,2048]{1,0:T(8,128)(2,1)}, bf16[128,2048]{1,0:T(8,128)(2,1)S(1)}, u32[]{:S(2)}) copy-start(bf16[128,2048]{1,0:T(8,128)(2,1)S(1)} %get-tuple-element.156.refs_0_) | copy-start | bytes 1572868
  5.1 11.4 %collective-permute-start = (bf16[128,1408]{1,0:T(8,128)(2,1)S(1)}, bf16[128,1408]{1,0:T(8,128)(2,1)S(1)}, u32[]{:S(2)}, u32[]{:S(2)}) collective-permute-start(bf16[128,1408]{1,0:T(8,128)(2,1)S(1)} %get-tuple-element.138.refs_0_), channel_id=1, source_target_pairs={{0,8},{8,16},{16,24},{24,28},{28,20},{20,12},{12,4},{4,0},{1,9},{9... | collective-permute-start | bytes 1081352 | tf_op jit(solution)/shard_map/ppermute | solution.py:724
  8.2 9.9 %collective-permute-start.1 = (bf16[128,1408]{1,0:T(8,128)(2,1)S(1)}, bf16[128,1408]{1,0:T(8,128)(2,1)S(1)}, u32[]{:S(2)}, u32[]{:S(2)}) collective-permute-start(bf16[128,1408]{1,0:T(8,128)(2,1)S(1)} %get-tuple-element.138.refs_0_), channel_id=1, source_target_pairs={{8,0},{16,8},{24,16},{28,24},{20,28},{12,20},{4,12},{0,4},{9,1},{1... | collective-permute-start | bytes 1081352 | tf_op jit(solution)/shard_map/ppermute | solution.py:725
  18.1 12.3 %collective-permute-start.2 = (bf16[128,1408]{1,0:T(8,128)(2,1)S(1)}, bf16[128,1408]{1,0:T(8,128)(2,1)S(1)}, u32[]{:S(2)}, u32[]{:S(2)}) collective-permute-start(bf16[128,1408]{1,0:T(8,128)(2,1)S(1)} %collective-permute-done.refs_1_), channel_id=1, source_target_pairs={{0,8},{8,16},{16,24},{24,28},{28,20},{20,12},{12,4},{4,0},{1,9},{9... | collective-permute-start | bytes 1081352 | tf_op jit(solution)/shard_map/ppermute | solution.py:724
  19.7 10.7 %collective-permute-start.3 = (bf16[128,1408]{1,0:T(8,128)(2,1)S(1)}, bf16[128,1408]{1,0:T(8,128)(2,1)S(1)}, u32[]{:S(2)}, u32[]{:S(2)}) collective-permute-start(bf16[128,1408]{1,0:T(8,128)(2,1)S(1)} %collective-permute-done.1.refs_2_), channel_id=1, source_target_pairs={{8,0},{16,8},{24,16},{28,24},{20,28},{12,20},{4,12},{0,4},{9,1},{1... | collective-permute-start | bytes 1081352 | tf_op jit(solution)/shard_map/ppermute | solution.py:725
  30.4 23.6 %copy-start.46 = (bf16[128,1408]{1,0:T(8,128)(2,1)}, bf16[128,1408]{1,0:T(8,128)(2,1)S(1)}, u32[]{:S(2)}) copy-start(bf16[128,1408]{1,0:T(8,128)(2,1)S(1)} %collective-permute-done.2.refs_3_) | copy-start | bytes 1081348
  30.4 23.6 %copy-start.47 = (bf16[128,1408]{1,0:T(8,128)(2,1)}, bf16[128,1408]{1,0:T(8,128)(2,1)S(1)}, u32[]{:S(2)}) copy-start(bf16[128,1408]{1,0:T(8,128)(2,1)S(1)} %collective-permute-done.3.refs_4_) | copy-start | bytes 1081348
  30.4 8.6 %collective-permute-start.4 = (bf16[128,1408]{1,0:T(8,128)(2,1)S(1)}, bf16[128,1408]{1,0:T(8,128)(2,1)S(1)}, u32[]{:S(2)}, u32[]{:S(2)}) collective-permute-start(bf16[128,1408]{1,0:T(8,128)(2,1)S(1)} %collective-permute-done.2.refs_3_), channel_id=1, source_target_pairs={{0,8},{8,16},{16,24},{24,28},{28,20},{20,12},{12,4},{4,0},{1,9},{9... | collective-permute-start | bytes 1081352 | tf_op jit(solution)/shard_map/ppermute | solution.py:724
  32.0 9.0 %collective-permute-start.5 = (bf16[128,1408]{1,0:T(8,128)(2,1)S(1)}, bf16[128,1408]{1,0:T(8,128)(2,1)S(1)}, u32[]{:S(2)}, u32[]{:S(2)}) collective-permute-start(bf16[128,1408]{1,0:T(8,128)(2,1)S(1)} %collective-permute-done.3.refs_4_), channel_id=1, source_target_pairs={{8,0},{16,8},{24,16},{28,24},{20,28},{12,20},{4,12},{0,4},{9,1},{1... | collective-permute-start | bytes 1081352 | tf_op jit(solution)/shard_map/ppermute | solution.py:725
  39.0 18.7 %collective-permute-start.8 = (bf16[128,2048]{1,0:T(8,128)(2,1)S(1)}, bf16[128,2048]{1,0:T(8,128)(2,1)}, u32[]{:S(2)}, u32[]{:S(2)}) collective-permute-start(bf16[128,2048]{1,0:T(8,128)(2,1)S(1)} %get-tuple-element.156.refs_0_), channel_id=1, source_target_pairs={{0,8},{8,16},{16,24},{24,28},{28,20},{20,12},{12,4},{4,0},{1,9},{9... | collective-permute-start | bytes 1572872 | tf_op jit(solution)/shard_map/ppermute | solution.py:724
  40.6 17.1 %collective-permute-start.9 = (bf16[128,2048]{1,0:T(8,128)(2,1)S(1)}, bf16[128,2048]{1,0:T(8,128)(2,1)}, u32[]{:S(2)}, u32[]{:S(2)}) collective-permute-start(bf16[128,2048]{1,0:T(8,128)(2,1)S(1)} %get-tuple-element.156.refs_0_), channel_id=1, source_target_pairs={{8,0},{16,8},{24,16},{28,24},{20,28},{12,20},{4,12},{0,4},{9,1},{1... | collective-permute-start | bytes 1572872 | tf_op jit(solution)/shard_map/ppermute | solution.py:725
  41.1 12.8 %collective-permute-start.6 = (bf16[64,1408]{1,0:T(8,128)(2,1)S(1)}, bf16[64,1408]{1,0:T(8,128)(2,1)S(1)}, u32[]{:S(2)}, u32[]{:S(2)}) collective-permute-start(bf16[64,1408]{1,0:T(8,128)(2,1)S(1)} %slice.139), channel_id=1, source_target_pairs={{0,8},{8,16},{16,24},{24,28},{28,20},{20,12},{12,4},{4,0},{1,9},{9... | collective-permute-start | bytes 540680 | tf_op jit(solution)/shard_map/ppermute | solution.py:730
  42.8 12.6 %collective-permute-start.7 = (bf16[64,1408]{1,0:T(8,128)(2,1)S(1)}, bf16[64,1408]{1,0:T(8,128)(2,1)}, u32[]{:S(2)}, u32[]{:S(2)}) collective-permute-start(bf16[64,1408]{1,0:T(8,128)(2,1)S(1)} %slice.140), channel_id=1, source_target_pairs={{8,0},{16,8},{24,16},{28,24},{20,28},{12,20},{4,12},{0,4},{9,1},{1... | collective-permute-start | bytes 540680 | tf_op jit(solution)/shard_map/ppermute | solution.py:731
  57.7 172.9 %copy-start = (bf16[1024,1408]{1,0:T(8,128)(2,1)}, bf16[1024,1408]{1,0:T(8,128)(2,1)S(1)}, u32[]{:S(2)}) copy-start(bf16[1024,1408]{1,0:T(8,128)(2,1)S(1)} %assemble.2.refs_4_.refs_3_) | copy-start | bytes 8650756
  57.8 19.9 %collective-permute-start.12 = (bf16[128,2048]{1,0:T(8,128)(2,1)}, bf16[128,2048]{1,0:T(8,128)(2,1)}, u32[]{:S(2)}, u32[]{:S(2)}) collective-permute-start(bf16[128,2048]{1,0:T(8,128)(2,1)} %collective-permute-done.8.refs_6_.refs_1_), channel_id=1, source_target_pairs={{0,8},{8,16},{16,24},{24,28},{28,20},{20,12},{12,4},{4,0},{1,9},{9... | collective-permute-start | bytes 1572872 | tf_op jit(solution)/shard_map/ppermute | solution.py:724
  59.4 18.2 %collective-permute-start.13 = (bf16[128,2048]{1,0:T(8,128)(2,1)}, bf16[128,2048]{1,0:T(8,128)(2,1)}, u32[]{:S(2)}, u32[]{:S(2)}) collective-permute-start(bf16[128,2048]{1,0:T(8,128)(2,1)} %collective-permute-done.9.refs_7_.refs_2_), channel_id=1, source_target_pairs={{8,0},{16,8},{24,16},{28,24},{20,28},{12,20},{4,12},{0,4},{9,1},{1... | collective-permute-start | bytes 1572872 | tf_op jit(solution)/shard_map/ppermute | solution.py:725
  60.4 20.5 %collective-permute-start.11 = (bf16[1024,256]{1,0:T(8,128)(2,1)S(1)}, bf16[1024,256]{1,0:T(8,128)(2,1)}, u32[]{:S(2)}, u32[]{:S(2)}) collective-permute-start(bf16[1024,256]{1,0:T(8,128)(2,1)S(1)} %get-tuple-element.326.refs_3_), channel_id=1, source_target_pairs={{0,2},{1,3},{2,0},{3,1},{4,6},{5,7},{6,4},{7,5},{8,10},{9,11},{10,... | collective-permute-start | bytes 1572872 | tf_op jit(solution)/shard_map/ppermute | solution.py:778
  77.1 18.3 %collective-permute-start.10 = (bf16[1024,256]{1,0:T(8,128)(2,1)}, bf16[1024,256]{1,0:T(8,128)(2,1)}, u32[]{:S(2)}, u32[]{:S(2)}) collective-permute-start(bf16[1024,256]{1,0:T(8,128)(2,1)} %get-tuple-element.157.refs_1_.refs_5_), channel_id=1, source_target_pairs={{0,2},{1,3},{2,0},{3,1},{4,6},{5,7},{6,4},{7,5},{8,10},{9,11},{10,... | collective-permute-start | bytes 1572872 | tf_op jit(solution)/shard_map/ppermute | solution.py:778
  77.6 17.8 %collective-permute-start.14 = (bf16[128,2048]{1,0:T(8,128)(2,1)}, bf16[128,2048]{1,0:T(8,128)(2,1)}, u32[]{:S(2)}, u32[]{:S(2)}) collective-permute-start(bf16[128,2048]{1,0:T(8,128)(2,1)} %collective-permute-done.12.refs_6_.refs_3_), channel_id=1, source_target_pairs={{0,8},{8,16},{16,24},{24,28},{28,20},{20,12},{12,4},{4,0},{1,9},{9... | collective-permute-start | bytes 1572872 | tf_op jit(solution)/shard_map/ppermute | solution.py:724
  79.2 16.3 %collective-permute-start.15 = (bf16[128,2048]{1,0:T(8,128)(2,1)}, bf16[128,2048]{1,0:T(8,128)(2,1)}, u32[]{:S(2)}, u32[]{:S(2)}) collective-permute-start(bf16[128,2048]{1,0:T(8,128)(2,1)} %collective-permute-done.13.refs_7_.refs_4_), channel_id=1, source_target_pairs={{8,0},{16,8},{24,16},{28,24},{20,28},{12,20},{4,12},{0,4},{9,1},{1... | collective-permute-start | bytes 1572872 | tf_op jit(solution)/shard_map/ppermute | solution.py:725
  98.4 18.5 %collective-permute-start.16 = (bf16[512,1024]{1,0:T(8,128)(2,1)S(1)}, bf16[512,1024]{1,0:T(8,128)(2,1)S(1)}, u32[]{:S(2)}, u32[]{:S(2)}) collective-permute-start(bf16[512,1024]{1,0:T(8,128)(2,1)S(1)} %get-tuple-element.172), channel_id=1, source_target_pairs={{0,1},{1,0},{2,3},{3,2},{4,5},{5,4},{6,7},{7,6},{8,9},{9,8},{10,11... | collective-permute-start | bytes 3145736 | tf_op jit(solution)/shard_map/ppermute | solution.py:778
  98.5 14.3 %collective-permute-start.17 = (bf16[1024,256]{1,0:T(8,128)(2,1)S(1)}, bf16[1024,256]{1,0:T(8,128)(2,1)S(1)}, u32[]{:S(2)}, u32[]{:S(2)}) collective-permute-start(bf16[1024,256]{1,0:T(8,128)(2,1)S(1)} %get-tuple-element.173.refs_1_.refs_5_), channel_id=1, source_target_pairs={{0,2},{1,3},{2,0},{3,1},{4,6},{5,7},{6,4},{7,5},{8,10},{9,11},{10,... | collective-permute-start | bytes 1572872 | tf_op jit(solution)/shard_map/ppermute | solution.py:778
  101.0 15.9 %collective-permute-start.18 = (bf16[64,2048]{1,0:T(8,128)(2,1)S(1)}, bf16[64,2048]{1,0:T(8,128)(2,1)S(1)}, u32[]{:S(2)}, u32[]{:S(2)}) collective-permute-start(bf16[64,2048]{1,0:T(8,128)(2,1)S(1)} %slice.147), channel_id=1, source_target_pairs={{0,8},{8,16},{16,24},{24,28},{28,20},{20,12},{12,4},{4,0},{1,9},{9... | collective-permute-start | bytes 786440 | tf_op jit(solution)/shard_map/ppermute | solution.py:730
  102.1 14.9 %collective-permute-start.19 = (bf16[64,2048]{1,0:T(8,128)(2,1)S(1)}, bf16[64,2048]{1,0:T(8,128)(2,1)S(1)}, u32[]{:S(2)}, u32[]{:S(2)}) collective-permute-start(bf16[64,2048]{1,0:T(8,128)(2,1)S(1)} %slice.148), channel_id=1, source_target_pairs={{8,0},{16,8},{24,16},{28,24},{20,28},{12,20},{4,12},{0,4},{9,1},{1... | collective-permute-start | bytes 786440 | tf_op jit(solution)/shard_map/ppermute | solution.py:731
  116.9 7.1 %collective-permute-start.21 = (bf16[512,1024]{1,0:T(8,128)(2,1)}, bf16[512,1024]{1,0:T(8,128)(2,1)}, u32[]{:S(2)}, u32[]{:S(2)}) collective-permute-start(bf16[512,1024]{1,0:T(8,128)(2,1)} %get-tuple-element.191), channel_id=1, source_target_pairs={{0,1},{1,0},{2,3},{3,2},{4,5},{5,4},{6,7},{7,6},{8,9},{9,8},{10,11... | collective-permute-start | bytes 3145736 | tf_op jit(solution)/shard_map/ppermute | solution.py:778
  120.3 6.9 %collective-permute-start.20 = (bf16[512,1024]{1,0:T(8,128)(2,1)}, bf16[512,1024]{1,0:T(8,128)(2,1)}, u32[]{:S(2)}, u32[]{:S(2)}) collective-permute-start(bf16[512,1024]{1,0:T(8,128)(2,1)} %get-tuple-element.178.refs_1_.refs_3_), channel_id=1, source_target_pairs={{0,1},{1,0},{2,3},{3,2},{4,5},{5,4},{6,7},{7,6},{8,9},{9,8},{10,11... | collective-permute-start | bytes 3145736 | tf_op jit(solution)/shard_map/ppermute | solution.py:778
  127.2 23.8 %copy-start.13 = (bf16[512,1024]{1,0:T(8,128)(2,1)}, bf16[512,1024]{1,0:T(8,128)(2,1)S(1)}, u32[]{:S(2)}) copy-start(bf16[512,1024]{1,0:T(8,128)(2,1)S(1)} %get-tuple-element.196.refs_1_.refs_3_) | copy-start | bytes 3145732
  145.4 2.7 collective-permute-start.24
  145.5 5.5 %collective-permute-start.23 = (bf16[512,1024]{1,0:T(8,128)(2,1)S(1)}, bf16[512,1024]{1,0:T(8,128)(2,1)S(1)}, u32[]{:S(2)}, u32[]{:S(2)}) collective-permute-start(bf16[512,1024]{1,0:T(8,128)(2,1)S(1)} %get-tuple-element.196.refs_1_.refs_3_), channel_id=1, source_target_pairs={{0,1},{1,0},{2,3},{3,2},{4,5},{5,4},{6,7},{7,6},{8,9},{9,8},{10,11... | collective-permute-start | bytes 3145736 | tf_op jit(solution)/shard_map/ppermute | solution.py:778
  149.5 25.5 %collective-permute-start.27 = (bf16[512,1024]{1,0:T(8,128)(2,1)}, bf16[512,1024]{1,0:T(8,128)(2,1)}, u32[]{:S(2)}, u32[]{:S(2)}) collective-permute-start(bf16[512,1024]{1,0:T(8,128)(2,1)} %add_convert_fusion.1.refs_6_.refs_1_), channel_id=1, source_target_pairs={{0,2},{1,3},{2,0},{3,1},{4,6},{5,7},{6,4},{7,5},{8,10},{9,11},{10,... | collective-permute-start | bytes 3145736 | tf_op jit(solution)/shard_map/ppermute | solution.py:778
  170.2 10.6 %collective-permute-start.25 = (bf16[512,1024]{1,0:T(8,128)(2,1)}, bf16[512,1024]{1,0:T(8,128)(2,1)}, u32[]{:S(2)}, u32[]{:S(2)}) collective-permute-start(bf16[512,1024]{1,0:T(8,128)(2,1)} %get-tuple-element.204), channel_id=1, source_target_pairs={{0,1},{1,0},{2,3},{3,2},{4,5},{5,4},{6,7},{7,6},{8,9},{9,8},{10,11... | collective-permute-start | bytes 3145736 | tf_op jit(solution)/shard_map/ppermute | solution.py:778
  170.2 48.1 %collective-permute-start.30 = (bf16[2,1024,256]{2,1,0:T(8,128)(2,1)}, bf16[2,1024,256]{2,1,0:T(8,128)(2,1)S(1)}, u32[]{:S(2)}, u32[]{:S(2)}) collective-permute-start(bf16[2,1024,256]{2,1,0:T(8,128)(2,1)} %get-tuple-element.219), channel_id=1, source_target_pairs={{0,1},{1,0},{2,3},{3,2},{4,5},{5,4},{6,7},{7,6},{8,9},{9,8},{10,11... | collective-permute-start | bytes 3145736 | tf_op jit(solution)/shard_map/ppermute | solution.py:778
  180.8 13.6 %collective-permute-start.28 = (bf16[512,1024]{1,0:T(8,128)(2,1)S(1)}, bf16[512,1024]{1,0:T(8,128)(2,1)S(1)}, u32[]{:S(2)}, u32[]{:S(2)}) collective-permute-start(bf16[512,1024]{1,0:T(8,128)(2,1)S(1)} %get-tuple-element.210.refs_1_), channel_id=1, source_target_pairs={{0,1},{1,0},{2,3},{3,2},{4,5},{5,4},{6,7},{7,6},{8,9},{9,8},{10,11... | collective-permute-start | bytes 3145736 | tf_op jit(solution)/shard_map/ppermute | solution.py:778
  182.2 8.7 %collective-permute-start.47 = (bf16[64,2048]{1,0:T(8,128)(2,1)S(1)}, bf16[64,2048]{1,0:T(8,128)(2,1)S(1)}, u32[]{:S(2)}, u32[]{:S(2)}) collective-permute-start(bf16[64,2048]{1,0:T(8,128)(2,1)S(1)} %get-tuple-element.313), channel_id=1, source_target_pairs={{0,8},{8,16},{16,24},{24,28},{28,20},{20,12},{12,4},{4,0},{1,9},{9... | collective-permute-start | bytes 786440 | tf_op jit(solution)/shard_map/ppermute | solution.py:755
  182.2 8.7 %collective-permute-start.48 = (bf16[64,2048]{1,0:T(8,128)(2,1)S(1)}, bf16[64,2048]{1,0:T(8,128)(2,1)S(1)}, u32[]{:S(2)}, u32[]{:S(2)}) collective-permute-start(bf16[64,2048]{1,0:T(8,128)(2,1)S(1)} %get-tuple-element.312), channel_id=1, source_target_pairs={{8,0},{16,8},{24,16},{28,24},{20,28},{12,20},{4,12},{0,4},{9,1},{1... | collective-permute-start | bytes 786440 | tf_op jit(solution)/shard_map/ppermute | solution.py:756
  185.9 30.2 %collective-permute-start.26 = (bf16[512,1024]{1,0:T(8,128)(2,1)S(1)}, bf16[512,1024]{1,0:T(8,128)(2,1)S(1)}, u32[]{:S(2)}, u32[]{:S(2)}) collective-permute-start(bf16[512,1024]{1,0:T(8,128)(2,1)S(1)} %add_convert_fusion.refs_12_.refs_1_), channel_id=1, source_target_pairs={{0,2},{1,3},{2,0},{3,1},{4,6},{5,7},{6,4},{7,5},{8,10},{9,11},{10,... | collective-permute-start | bytes 3145736 | tf_op jit(solution)/shard_map/ppermute | solution.py:778
  190.9 29.7 %collective-permute-start.22 = (bf16[2,1024,256]{2,1,0:T(8,128)(2,1)S(1)}, bf16[2,1024,256]{2,1,0:T(8,128)(2,1)S(1)}, u32[]{:S(2)}, u32[]{:S(2)}) collective-permute-start(bf16[2,1024,256]{2,1,0:T(8,128)(2,1)S(1)} %copy-done.51), channel_id=1, source_target_pairs={{0,1},{1,0},{2,3},{3,2},{4,5},{5,4},{6,7},{7,6},{8,9},{9,8},{10,11... | collective-permute-start | bytes 3145736 | tf_op jit(solution)/shard_map/ppermute | solution.py:778
  192.7 30.6 %collective-permute-start.50 = (bf16[128,2048]{1,0:T(8,128)(2,1)S(1)}, bf16[128,2048]{1,0:T(8,128)(2,1)S(1)}, u32[]{:S(2)}, u32[]{:S(2)}) collective-permute-start(bf16[128,2048]{1,0:T(8,128)(2,1)S(1)} %pad_maximum_fusion.1), channel_id=1, source_target_pairs={{8,0},{16,8},{24,16},{28,24},{20,28},{12,20},{4,12},{0,4},{9,1},{1... | collective-permute-start | bytes 1572872 | tf_op jit(solution)/shard_map/ppermute | solution.py:756
  194.4 29.4 %collective-permute-start.49 = (bf16[128,2048]{1,0:T(8,128)(2,1)S(1)}, bf16[128,2048]{1,0:T(8,128)(2,1)S(1)}, u32[]{:S(2)}, u32[]{:S(2)}) collective-permute-start(bf16[128,2048]{1,0:T(8,128)(2,1)S(1)} %pad_maximum_fusion), channel_id=1, source_target_pairs={{0,8},{8,16},{16,24},{24,28},{28,20},{20,12},{12,4},{4,0},{1,9},{9... | collective-permute-start | bytes 1572872 | tf_op jit(solution)/shard_map/ppermute | solution.py:755
  195.1 21.0 %copy-start.4 = (bf16[1024,1024]{1,0:T(8,128)(2,1)S(1)}, bf16[1024,1024]{1,0:T(8,128)(2,1)}, u32[]{:S(2)}) copy-start(bf16[1024,1024]{1,0:T(8,128)(2,1)} %get-tuple-element.197.refs_3_.refs_5_) | copy-start | bytes 6291460
  195.1 21.0 %copy-start.14 = (bf16[512,1024]{1,0:T(8,128)(2,1)S(1)}, bf16[512,1024]{1,0:T(8,128)(2,1)}, u32[]{:S(2)}) copy-start(bf16[512,1024]{1,0:T(8,128)(2,1)} %copy-done.13) | copy-start | bytes 3145732
  218.2 11.5 %collective-permute-start.32 = (bf16[512,1024]{1,0:T(8,128)(2,1)S(1)}, bf16[512,1024]{1,0:T(8,128)(2,1)S(1)}, u32[]{:S(2)}, u32[]{:S(2)}) collective-permute-start(bf16[512,1024]{1,0:T(8,128)(2,1)S(1)} %get-tuple-element.223.refs_1_), channel_id=1, source_target_pairs={{0,1},{1,0},{2,3},{3,2},{4,5},{5,4},{6,7},{7,6},{8,9},{9,8},{10,11... | collective-permute-start | bytes 3145736 | tf_op jit(solution)/shard_map/ppermute | solution.py:778
  218.3 33.8 %collective-permute-start.35 = (bf16[2,1024,256]{2,1,0:T(8,128)(2,1)S(1)}, bf16[2,1024,256]{2,1,0:T(8,128)(2,1)S(1)}, u32[]{:S(2)}, u32[]{:S(2)}) collective-permute-start(bf16[2,1024,256]{2,1,0:T(8,128)(2,1)S(1)} %copy-done.52), channel_id=1, source_target_pairs={{0,1},{1,0},{2,3},{3,2},{4,5},{5,4},{6,7},{7,6},{8,9},{9,8},{10,11... | collective-permute-start | bytes 3145736 | tf_op jit(solution)/shard_map/ppermute | solution.py:778
  220.5 35.8 %collective-permute-start.31 = (bf16[1,1024,256]{2,1,0:T(8,128)(2,1)}, bf16[1,1024,256]{2,1,0:T(8,128)(2,1)}, u32[]{:S(2)}, u32[]{:S(2)}) collective-permute-start(bf16[1,1024,256]{2,1,0:T(8,128)(2,1)} %dynamic-slice_convert_fusion.2), channel_id=1, source_target_pairs={{0,2},{1,3},{2,0},{3,1},{4,6},{5,7},{6,4},{7,5},{8,10},{9,11},{10,... | collective-permute-start | bytes 1572872 | tf_op jit(solution)/shard_map/ppermute | solution.py:778
  223.3 33.1 %collective-permute-start.29 = (bf16[1,1024,256]{2,1,0:T(8,128)(2,1)}, bf16[1,1024,256]{2,1,0:T(8,128)(2,1)}, u32[]{:S(2)}, u32[]{:S(2)}) collective-permute-start(bf16[1,1024,256]{2,1,0:T(8,128)(2,1)} %dynamic-slice_convert_fusion.3), channel_id=1, source_target_pairs={{0,2},{1,3},{2,0},{3,1},{4,6},{5,7},{6,4},{7,5},{8,10},{9,11},{10,... | collective-permute-start | bytes 1572872 | tf_op jit(solution)/shard_map/ppermute | solution.py:778
  226.5 33.3 %collective-permute-start.51 = (bf16[128,2048]{1,0:T(8,128)(2,1)}, bf16[128,2048]{1,0:T(8,128)(2,1)}, u32[]{:S(2)}, u32[]{:S(2)}) collective-permute-start(bf16[128,2048]{1,0:T(8,128)(2,1)} %get-tuple-element.307), channel_id=1, source_target_pairs={{0,8},{8,16},{16,24},{24,28},{28,20},{20,12},{12,4},{4,0},{1,9},{9... | collective-permute-start | bytes 1572872 | tf_op jit(solution)/shard_map/ppermute | solution.py:755
  229.7 30.6 %collective-permute-start.52 = (bf16[128,2048]{1,0:T(8,128)(2,1)}, bf16[128,2048]{1,0:T(8,128)(2,1)}, u32[]{:S(2)}, u32[]{:S(2)}) collective-permute-start(bf16[128,2048]{1,0:T(8,128)(2,1)} %get-tuple-element.306), channel_id=1, source_target_pairs={{8,0},{16,8},{24,16},{28,24},{20,28},{12,20},{4,12},{0,4},{9,1},{1... | collective-permute-start | bytes 1572872 | tf_op jit(solution)/shard_map/ppermute | solution.py:756
  254.8 12.4 %collective-permute-start.36 = (bf16[1,512,256]{2,1,0:T(8,128)(2,1)S(1)}, bf16[1,512,256]{2,1,0:T(8,128)(2,1)S(1)}, u32[]{:S(2)}, u32[]{:S(2)}) collective-permute-start(bf16[1,512,256]{2,1,0:T(8,128)(2,1)S(1)} %get-tuple-element.345), channel_id=1, source_target_pairs={{0,2},{1,3},{2,0},{3,1},{4,6},{5,7},{6,4},{7,5},{8,10},{9,11},{10,... | collective-permute-start | bytes 786440 | tf_op jit(solution)/shard_map/ppermute | solution.py:778
  257.6 6.5 %collective-permute-start.33 = (bf16[64,1152]{1,0:T(8,128)(2,1)S(1)}, bf16[64,1152]{1,0:T(8,128)(2,1)S(1)}, u32[]{:S(2)}, u32[]{:S(2)}) collective-permute-start(bf16[64,1152]{1,0:T(8,128)(2,1)S(1)} %get-tuple-element.323), channel_id=1, source_target_pairs={{0,8},{8,16},{16,24},{24,28},{28,20},{20,12},{12,4},{4,0},{1,9},{9... | collective-permute-start | bytes 442376 | tf_op jit(solution)/shard_map/ppermute | solution.py:755
  257.6 8.4 %collective-permute-start.34 = (bf16[64,1152]{1,0:T(8,128)(2,1)S(1)}, bf16[64,1152]{1,0:T(8,128)(2,1)S(1)}, u32[]{:S(2)}, u32[]{:S(2)}) collective-permute-start(bf16[64,1152]{1,0:T(8,128)(2,1)S(1)} %get-tuple-element.322), channel_id=1, source_target_pairs={{8,0},{16,8},{24,16},{28,24},{20,28},{12,20},{4,12},{0,4},{9,1},{1... | collective-permute-start | bytes 442376 | tf_op jit(solution)/shard_map/ppermute | solution.py:756
  259.8 13.6 %collective-permute-start.37 = (bf16[1,512,256]{2,1,0:T(8,128)(2,1)S(1)}, bf16[1,512,256]{2,1,0:T(8,128)(2,1)S(1)}, u32[]{:S(2)}, u32[]{:S(2)}) collective-permute-start(bf16[1,512,256]{2,1,0:T(8,128)(2,1)S(1)} %get-tuple-element.344), channel_id=1, source_target_pairs={{0,2},{1,3},{2,0},{3,1},{4,6},{5,7},{6,4},{7,5},{8,10},{9,11},{10,... | collective-permute-start | bytes 786440 | tf_op jit(solution)/shard_map/ppermute | solution.py:778
  262.9 21.6 %collective-permute-start.53 = (bf16[128,2048]{1,0:T(8,128)(2,1)S(1)}, bf16[128,2048]{1,0:T(8,128)(2,1)S(1)}, u32[]{:S(2)}, u32[]{:S(2)}) collective-permute-start(bf16[128,2048]{1,0:T(8,128)(2,1)S(1)} %get-tuple-element.305), channel_id=1, source_target_pairs={{0,8},{8,16},{16,24},{24,28},{28,20},{20,12},{12,4},{4,0},{1,9},{9... | collective-permute-start | bytes 1572872 | tf_op jit(solution)/shard_map/ppermute | solution.py:755
  264.1 20.4 %collective-permute-start.54 = (bf16[128,2048]{1,0:T(8,128)(2,1)S(1)}, bf16[128,2048]{1,0:T(8,128)(2,1)S(1)}, u32[]{:S(2)}, u32[]{:S(2)}) collective-permute-start(bf16[128,2048]{1,0:T(8,128)(2,1)S(1)} %get-tuple-element.304), channel_id=1, source_target_pairs={{8,0},{16,8},{24,16},{28,24},{20,28},{12,20},{4,12},{0,4},{9,1},{1... | collective-permute-start | bytes 1572872 | tf_op jit(solution)/shard_map/ppermute | solution.py:756
  267.5 14.6 %collective-permute-start.39 = (bf16[128,1152]{1,0:T(8,128)(2,1)S(1)}, bf16[128,1152]{1,0:T(8,128)(2,1)S(1)}, u32[]{:S(2)}, u32[]{:S(2)}) collective-permute-start(bf16[128,1152]{1,0:T(8,128)(2,1)S(1)} %pad_maximum_fusion.3), channel_id=1, source_target_pairs={{8,0},{16,8},{24,16},{28,24},{20,28},{12,20},{4,12},{0,4},{9,1},{1... | collective-permute-start | bytes 884744 | tf_op jit(solution)/shard_map/ppermute | solution.py:756
  267.8 14.4 %collective-permute-start.38 = (bf16[128,1152]{1,0:T(8,128)(2,1)S(1)}, bf16[128,1152]{1,0:T(8,128)(2,1)S(1)}, u32[]{:S(2)}, u32[]{:S(2)}) collective-permute-start(bf16[128,1152]{1,0:T(8,128)(2,1)S(1)} %pad_maximum_fusion.2), channel_id=1, source_target_pairs={{0,8},{8,16},{16,24},{24,28},{28,20},{20,12},{12,4},{4,0},{1,9},{9... | collective-permute-start | bytes 884744 | tf_op jit(solution)/shard_map/ppermute | solution.py:755
  273.4 20.0 %collective-permute-start.42 = (bf16[2,1024,256]{2,1,0:T(8,128)(2,1)}, bf16[2,1024,256]{2,1,0:T(8,128)(2,1)}, u32[]{:S(2)}, u32[]{:S(2)}) collective-permute-start(bf16[2,1024,256]{2,1,0:T(8,128)(2,1)} %get-tuple-element.247), channel_id=1, source_target_pairs={{0,1},{1,0},{2,3},{3,2},{4,5},{5,4},{6,7},{7,6},{8,9},{9,8},{10,11... | collective-permute-start | bytes 3145736 | tf_op jit(solution)/shard_map/ppermute | solution.py:778
  282.3 6.8 %collective-permute-start.40 = (bf16[128,1152]{1,0:T(8,128)(2,1)S(1)}, bf16[128,1152]{1,0:T(8,128)(2,1)S(1)}, u32[]{:S(2)}, u32[]{:S(2)}) collective-permute-start(bf16[128,1152]{1,0:T(8,128)(2,1)S(1)} %get-tuple-element.317), channel_id=1, source_target_pairs={{0,8},{8,16},{16,24},{24,28},{28,20},{20,12},{12,4},{4,0},{1,9},{9... | collective-permute-start | bytes 884744 | tf_op jit(solution)/shard_map/ppermute | solution.py:755
  283.0 6.7 %collective-permute-start.41 = (bf16[128,1152]{1,0:T(8,128)(2,1)S(1)}, bf16[128,1152]{1,0:T(8,128)(2,1)S(1)}, u32[]{:S(2)}, u32[]{:S(2)}) collective-permute-start(bf16[128,1152]{1,0:T(8,128)(2,1)S(1)} %get-tuple-element.316), channel_id=1, source_target_pairs={{8,0},{16,8},{24,16},{28,24},{20,28},{12,20},{4,12},{0,4},{9,1},{1... | collective-permute-start | bytes 884744 | tf_op jit(solution)/shard_map/ppermute | solution.py:756
  291.2 6.8 %collective-permute-start.45 = (bf16[128,1152]{1,0:T(8,128)(2,1)S(1)}, bf16[128,1152]{1,0:T(8,128)(2,1)S(1)}, u32[]{:S(2)}, u32[]{:S(2)}) collective-permute-start(bf16[128,1152]{1,0:T(8,128)(2,1)S(1)} %get-tuple-element.315), channel_id=1, source_target_pairs={{0,8},{8,16},{16,24},{24,28},{28,20},{20,12},{12,4},{4,0},{1,9},{9... | collective-permute-start | bytes 884744 | tf_op jit(solution)/shard_map/ppermute | solution.py:755
  293.0 6.7 %collective-permute-start.46 = (bf16[128,1152]{1,0:T(8,128)(2,1)S(1)}, bf16[128,1152]{1,0:T(8,128)(2,1)S(1)}, u32[]{:S(2)}, u32[]{:S(2)}) collective-permute-start(bf16[128,1152]{1,0:T(8,128)(2,1)S(1)} %get-tuple-element.314), channel_id=1, source_target_pairs={{8,0},{16,8},{24,16},{28,24},{20,28},{12,20},{4,12},{0,4},{9,1},{1... | collective-permute-start | bytes 884744 | tf_op jit(solution)/shard_map/ppermute | solution.py:756
  295.8 14.7 %collective-permute-start.43 = (bf16[1,512,256]{2,1,0:T(8,128)(2,1)}, bf16[1,512,256]{2,1,0:T(8,128)(2,1)}, u32[]{:S(2)}, u32[]{:S(2)}) collective-permute-start(bf16[1,512,256]{2,1,0:T(8,128)(2,1)} %get-tuple-element.342), channel_id=1, source_target_pairs={{0,2},{1,3},{2,0},{3,1},{4,6},{5,7},{6,4},{7,5},{8,10},{9,11},{10,... | collective-permute-start | bytes 786440 | tf_op jit(solution)/shard_map/ppermute | solution.py:778
  297.7 12.9 %collective-permute-start.44 = (bf16[1,512,256]{2,1,0:T(8,128)(2,1)}, bf16[1,512,256]{2,1,0:T(8,128)(2,1)}, u32[]{:S(2)}, u32[]{:S(2)}) collective-permute-start(bf16[1,512,256]{2,1,0:T(8,128)(2,1)} %get-tuple-element.343), channel_id=1, source_target_pairs={{0,2},{1,3},{2,0},{3,1},{4,6},{5,7},{6,4},{7,5},{8,10},{9,11},{10,... | collective-permute-start | bytes 786440 | tf_op jit(solution)/shard_map/ppermute | solution.py:778
  301.6 1.6 collective-permute-start.55
  304.1 4.7 %collective-permute-start.56 = (f32[128,128]{1,0:T(8,128)S(1)}, f32[128,128]{1,0:T(8,128)S(1)}, u32[]{:S(2)}, u32[]{:S(2)}) collective-permute-start(f32[128,128]{1,0:T(8,128)S(1)} %slice_add_fusion), channel_id=1, source_target_pairs={{0,2},{1,3},{2,0},{3,1},{4,6},{5,7},{6,4},{7,5},{8,10},{9,11},{10,... | collective-permute-start | bytes 196616 | tf_op jit(solution)/shard_map/ppermute | solution.py:770
  (47 other events, 234.1 us)
where the time goes:
time: 319 us; the launch traced here: 314 us
  Pallas kernels  139 us (44%)
  starting transfers between devices  52.6 us (16%)
  waiting for transfers between devices  51.3 us (16%)
  local copies, waits for them, and re-layouts  34 us (11%)
  other arithmetic  33.8 us (11%)
    pallas_call x16, Pallas kernels, call(): pl.pallas_call(body, out_shape=(*(pltpu.HBM(o.shape, o.dtype) if k in sto...  134 us
    ppermute x23, starting transfers between devices, swap(): return lax.ppermute(value, 'tensor', [(i, i ^ bit) for i in range(n)])  15.3 us
    ppermute x23, waiting for transfers between devices, swap(): return lax.ppermute(value, 'tensor', [(i, i ^ bit) for i in range(n)])  15 us
    unnamed x108, local copies, waits for them, and re-layouts  13.6 us
    ppermute x8, waiting for transfers between devices, scatter(): left = lax.ppermute(left, 'dp', self.left)  11.1 us
    ppermute x6, starting transfers between devices, gather(): from_left = lax.ppermute(from_left, 'dp', self.right)  11 us
    ppermute x8, starting transfers between devices, scatter(): left = lax.ppermute(left, 'dp', self.left)  10.6 us
    ppermute x2, waiting for transfers between devices, gather(): come.append(lax.ppermute(from_left[:rows // 2], 'dp', self.right))  9.42 us
  transfers between devices with their start and end apart: 57, of which 16 were waited for; matrix products, arithmetic and copies ran while one was open for 17% of the time, Pallas kernels for 37%

commit v1 on v0

--- a/solution.py
+++ b/solution.py
@@ -368,34 +368,19 @@
         send[g] = jnp.where(core == 0, second, first)
 
 
-def hidden_kernel(
-    meta,
-    n2_own,
-    n2_other,
-    cot,
-    w2,
-    h1,
-    d_keep,
-    d_send,
-    grad,
-    keep,
-    send,
-    act,
-    d_hid,
-    held,
-    sems,
-    store,
-):
-    ready = load([h1], [held], sems)
-    hid = w2.shape[1] // 2
-    half, width = n2_own.shape
-    chips = keep.shape[0]
-    chunk = min(512, hid)
+def halves_of(meta, half):
     own = pl.multiple_of(meta[0] * half, BLOCK)
     other = pl.multiple_of((1 - meta[0]) * half, BLOCK)
-    for first, base, n2, d_n2 in ((half, other, n2_other, d_send), (0, own, n2_own, d_keep)):
-        if first == 0:
-            ready()
+    return ((half, other), (0, own))
+
+
+def hidden_start(meta, n2_own, n2_other, cot, w2, d_keep, d_send, act, d_hid):
+    hid = w2.shape[1] // 2
+    half = n2_own.shape[0]
+    chunk = min(1024, hid)
+    for (first, base), n2, d_n2 in zip(
+        halves_of(meta, half), (n2_other, n2_own), (d_send, d_keep), strict=True
+    ):
         for at in range(0, half, BLOCK):
             rows = slice(at, at + BLOCK)
             mine = slice(first + at, first + at + BLOCK)
@@ -408,14 +393,27 @@
                 slope = cdf + u * (jnp.exp(-0.5 * u * u) * (0.5 / math.pi) ** 0.5)
                 d_hid[mine, col : col + chunk] = (d_act * slope).astype(bf16)
             d_n2[rows, :] = dot(d_hid[mine, :], w2[:, :hid], 1, 1).astype(bf16)
+
+
+def hidden_end(
+    meta, n2_own, n2_other, cot, w2, h1, act, d_hid, grad, keep, send, held, sems, store, outs
+):
+    ready = load([h1], [held], sems)
+    hid = w2.shape[1] // 2
+    half, width = n2_own.shape
+    chips = keep.shape[0]
+    (_, other), (_, own) = halves_of(meta, half)
+    for first in (half, 0):
+        if first == 0:
+            ready()
+        for at in range(0, half, BLOCK):
+            mine = slice(first + at, first + at + BLOCK)
             term = dot(act[mine, :], w2[:, hid:], 1, 1)
             if first == 0:
-                term = term + held[rows, :] * (1.0 / chips)
-            split_features(
-                meta[0], term.astype(bf16), keep.at[:, mine, :], send.at[:, mine, :]
-            )
-    store(3)
-    store(4)
+                term = term + held[mine, :] * (1.0 / chips)
+            split_features(meta[0], term.astype(bf16), keep.at[:, mine, :], send.at[:, mine, :])
+    store(outs + 1)
+    store(outs + 2)
     for at in range(0, width, BLOCK):
         cols = slice(at, at + BLOCK)
         up = dot(n2_own[:, cols], d_hid[:half, :], 0, 0)
@@ -424,24 +422,58 @@
         down = dot(cot[pl.ds(own, half), cols], act[:half, :], 0, 0)
         down = down + dot(cot[pl.ds(other, half), cols], act[half:, :], 0, 0)
         grad[cols, hid:] = down.astype(bf16)
-        store(2, cols)
-
-
-def hidden_layer(meta, n2, cot, w2, h1, chips, after):
+        store(outs, cols)
+
+
+def hidden_layer(meta, n2, cot, w2, h1, chips, after, part=None):
     half, width = n2[0].shape
     hid = w2.shape[1] // 2
     split = like((chips, 2 * half, width // (2 * chips)), bf16)
     d_n2 = like((half, width), bf16)
+    kept = like((2 * half, hid), bf16)
+    late = (like((width, 2 * hid), bf16), split, split)
+    if part is None:
+
+        def kernel(meta, own, other, cot, w2, h1, *refs, store):
+            (d_keep, d_send, *ends), act, d_hid, held, sems = refs[:5], *refs[5:]
+            hidden_start(meta, own, other, cot, w2, d_keep, d_send, act, d_hid)
+            hidden_end(
+                meta, own, other, cot, w2, h1, act, d_hid, *ends, held, sems, store, 2
+            )
+
+        scratch = [*(pltpu.VMEM(kept.shape, bf16) for _ in range(2)), *held_like([h1])]
+        return call(
+            kernel,
+            "hidden_layer",
+            28,
+            24 * half * width * hid,
+            (d_n2, d_n2, *late),
+            (meta, *n2, cot, w2, h1),
+            scratch,
+            after,
+            (2, 3, 4),
+            (5,),
+        )
+    if part == ():
+        return call(
+            hidden_start,
+            "hidden_start",
+            20,
+            12 * half * width * hid,
+            (d_n2, d_n2, kept, kept),
+            (meta, *n2, cot, w2),
+            after=after,
+        )
     return call(
-        hidden_kernel,
-        "hidden_layer",
+        lambda *refs, store: hidden_end(*refs, store, 0),
+        "hidden_end",
         28,
-        24 * half * width * hid,
-        (d_n2, d_n2, like((width, 2 * hid), bf16), split, split),
-        (meta, *n2, cot, w2, h1),
-        [*(pltpu.VMEM((2 * half, hid), bf16) for _ in range(2)), *held_like([h1])],
+        12 * half * width * hid,
+        late,
+        (meta, *n2, cot, w2, h1, *part),
+        held_like([h1]),
         after,
-        (2, 3, 4),
+        (0, 1, 2),
         (5,),
     )
 
@@ -929,11 +961,22 @@
         return token
 
     def hidden_of(i, after):
-        d_keep, d_send, grad, keep, send, token = hidden_layer(
-            metas[i], n2[i], cot[i], w2, h1[i], chips, after
-        )
+        given = (metas[i], n2[i], cot[i], w2, h1[i], chips)
+        if i < final:
+            d_keep, d_send, *rest, token = hidden_layer(*given, after, ())
+        else:
+            d_keep, d_send, *rest, token = hidden_layer(*given, after)
+        terms.append((d_keep, exchange_core(d_send)))
+        return token, rest
+
+    def rest_of(i, rest, after):
+        token = after[0]
+        if i < final:
+            *rest, token = hidden_layer(
+                metas[i], n2[i], cot[i], w2, h1[i], chips, after, tuple(rest)
+            )
+        grad, keep, send = rest
         grad2.append(grad)
-        terms.append((d_keep, exchange_core(d_send)))
         downs.append((keep, exchange_core(send)))
         return token
 
@@ -947,9 +990,10 @@
     for i in seqs:
         token = middle_of(i, (token, *(brought2[3] if i == 0 else ())))
     for i in seqs:
-        token = hidden_of(i, (token,))
+        token, rest = hidden_of(i, (token,))
         if i < final:
             token = sum_of(i, (token,))
+        token = rest_of(i, rest, (token,))
     grad2, _ = gate(grad2, (got for _, got in d_n2))
     sum2 = ring.scatter(grad2)
     hops2 = next(sum2)

time: 319 us -> 317 us (level)
  Pallas kernels: 139 us -> 133 us
  starting transfers between devices: 52.6 us -> 57.5 us
    ppermute x8, starting transfers between devices: 6.32 us -> 18 us  [scatter(): right = lax.ppermute(right, 'dp', self.right)]
    ppermute x8, starting transfers between devices: 10.6 us -> 3.97 us  [scatter(): left = lax.ppermute(left, 'dp', self.left)]
    pallas_call x16 -> x17, Pallas kernels: 134 us -> 127 us  [call(): pl.pallas_call(body, out_shape=(*(pltpu.HBM(o.shape, o.dtype) if k in sto...]
    ppermute x23, waiting for transfers between devices: 15 us -> 9.12 us  [swap(): return lax.ppermute(value, 'tensor', [(i, i ^ bit) for i in range(n)])]
    ppermute x2, starting transfers between devices: 1.69 us -> 5.26 us  [gather(): come.append(lax.ppermute(from_left[:rows // 2], 'dp', self.right))]
  transfers between devices with their start and end apart: 57 -> 57, of which waited for: 16 -> 15; matrix products, arithmetic and copies ran while one was open for 17% -> 17% of each run, Pallas kernels for 37% -> 38%
where the time goes in v1:
time: 317 us; the launch traced here: 312 us
  Pallas kernels  133 us (42%)
  starting transfers between devices  57.5 us (18%)
  waiting for transfers between devices  50.8 us (16%)
  local copies, waits for them, and re-layouts  34 us (11%)
  other arithmetic  33.8 us (11%)
    pallas_call x17, Pallas kernels, call(): pl.pallas_call(body, out_shape=(*(pltpu.HBM(o.shape, o.dtype) if k in sto...  127 us
    ppermute x8, starting transfers between devices, scatter(): right = lax.ppermute(right, 'dp', self.right)  18 us
    ppermute x23, starting transfers between devices, swap(): return lax.ppermute(value, 'tensor', [(i, i ^ bit) for i in range(n)])  14.2 us
    ppermute x8, waiting for transfers between devices, scatter(): left = lax.ppermute(left, 'dp', self.left)  14.1 us
    unnamed x108, local copies, waits for them, and re-layouts  13.7 us
    ppermute x6, starting transfers between devices, gather(): from_left = lax.ppermute(from_left, 'dp', self.right)  12.7 us
    ppermute x2, waiting for transfers between devices, gather(): come.append(lax.ppermute(from_left[:rows // 2], 'dp', self.right))  9.42 us
    ppermute x23, waiting for transfers between devices, swap(): return lax.ppermute(value, 'tensor', [(i, i ^ bit) for i in range(n)])  9.12 us
  transfers between devices with their start and end apart: 57, of which 15 were waited for; matrix products, arithmetic and copies ran while one was open for 17% of the time, Pallas kernels for 38%

profile of v1, /device:TPU:0, one launch (start us, length us, event | category | flops | bytes accessed | tf_op | source)
XLA Modules:
  0.0 312.0 jit_solution(11585056572345514732)
XLA Ops:
  2.5 2.6 pack.1
  5.1 3.1 collective-permute-start
  10.7 4.7 %slice_bitcast_fusion = (bf16[1024,1024]{1,0:T(8,128)(2,1)}, bf16[1024,1024]{1,0:T(8,128)(2,1)}) fusion(bf16[2,1024,1024]{2,1,0:T(8,128)(2,1)} %param.23), kind=kLoop, calls=%fused_computation.18 | loop fusion | bytes 8388608 | tf_op jit(solution)/shard_map/squeeze | solution.py:881
  16.5 1.5 collective-permute-done.1.refs_2_
  18.1 1.6 collective-permute-start.2
  20.6 9.8 %embed.1 = (f32[1024,1024]{1,0:T(8,128)}, f32[1024,1024]{1,0:T(8,128)}, f32[8,128]{1,0:T(8,128)}) custom-call(s32[10]{0:T(128)S(1)} %get-tuple-element.142.refs_0_, bf16[2,1024,1024]{2,1,0:T(8,128)(2,1)} %refs_1_.3, s32[2,1024,1]{2,1,0:T(8,128)S(1)} %copy.30.refs_2_, f32[1,512]{1,0:T(1,128)S(1)} %multiply_exponential_fusion.refs_3_), custom_call_target="tpu_custom_call" | custom-call | flops 409600 | bytes 12298 | tf_op jit(solution)/shard_map/embed/pallas_call | solution.py:114
  30.4 1.6 collective-permute-start.4
  32.5 6.5 %collective-permute-done.4.refs_5_ = bf16[128,1408]{1,0:T(8,128)(2,1)S(1)} collective-permute-done((bf16[128,1408]{1,0:T(8,128)(2,1)S(1)}, bf16[128,1408]{1,0:T(8,128)(2,1)S(1)}, u32[]{:S(2)}, u32[]{:S(2)}) %collective-permute-start.4) | collective-permute-done | bytes 360480 | tf_op jit(solution)/shard_map/ppermute | solution.py:756
  39.0 1.6 collective-permute-start.8
  41.1 1.6 collective-permute-start.6
  44.6 9.4 %collective-permute-done.6.refs_7_ = bf16[64,1408]{1,0:T(8,128)(2,1)S(1)} collective-permute-done((bf16[64,1408]{1,0:T(8,128)(2,1)S(1)}, bf16[64,1408]{1,0:T(8,128)(2,1)S(1)}, u32[]{:S(2)}, u32[]{:S(2)}) %collective-permute-start.6) | collective-permute-done | bytes 180256 | tf_op jit(solution)/shard_map/ppermute | solution.py:762
  55.4 2.4 assemble.2.refs_4_.refs_3_
  57.8 1.6 collective-permute-start.12
  60.4 1.6 collective-permute-start.11
  62.7 3.5 %project.2 = (f32[512,1024]{1,0:T(8,128)}, bf16[1024,1024]{1,0:T(8,128)(2,1)}, bf16[1024,768]{1,0:T(8,128)(2,1)S(1)}, f32[1024,128]{1,0:T(8,128)S(1)}, f32[8,128]{1,0:T(8,128)S(1)}) custom-call(s32[10]{0:T(128)S(1)} %get-tuple-element.142.refs_0_, f32[1024,1024]{1,0:T(8,128)S(1)} %copy-done.12, f32[1,1024]{1,0:T(1,128)S(1)} %get-tuple-element.353.refs_2_, ...), custom_call_target="tpu_custom_call" | custom-call | flops 1572864 | bytes 13064 | tf_op jit(solution)/shard_map/project/pallas_call | solution.py:114
  66.2 7.4 %attend.2 = (bf16[1024,256]{1,0:T(8,128)(2,1)}, f32[1024,128]{1,0:T(8,128)S(1)}, f32[8,128]{1,0:T(8,128)S(1)}) custom-call(s32[10]{0:T(128)S(1)} %get-tuple-element.142.refs_0_, bf16[1024,768]{1,0:T(8,128)(2,1)S(1)} %get-tuple-element.153.refs_1_.refs_4_, f32[1024,128]{1,0:T(8,128)S(1)} %get-tuple-element.154.refs_2_, s32[1024,1]{1,0:T(8,128)S(1)} %copy-done.9, ...), custom_call_target="tpu_custom_call" | custom-call | flops 2097152 | bytes 3080 | tf_op jit(solution)/shard_map/attend/pallas_call | solution.py:114
  76.1 3.2 %collective-permute-start.14 = (bf16[128,2048]{1,0:T(8,128)(2,1)}, bf16[128,2048]{1,0:T(8,128)(2,1)}, u32[]{:S(2)}, u32[]{:S(2)}) collective-permute-start(bf16[128,2048]{1,0:T(8,128)(2,1)} %collective-permute-done.12.refs_6_.refs_3_), channel_id=1, source_target_pairs={{0,8},{8,16},{16,24},{24,28},{28,20},{20,12},{12,4},{4,0},{1,9},{9... | collective-permute-start | bytes 1572872 | tf_op jit(solution)/shard_map/ppermute | solution.py:756
  80.5 2.2 copy-done.11
  82.7 3.4 %project.3 = (f32[512,1024]{1,0:T(8,128)}, bf16[1024,1024]{1,0:T(8,128)(2,1)}, bf16[1024,768]{1,0:T(8,128)(2,1)S(1)}, f32[1024,128]{1,0:T(8,128)S(1)}, f32[8,128]{1,0:T(8,128)S(1)}) custom-call(s32[10]{0:T(128)S(1)} %get-tuple-element.161.refs_0_, f32[1024,1024]{1,0:T(8,128)S(1)} %copy-done.11, f32[1,1024]{1,0:T(1,128)S(1)} %get-tuple-element.352.refs_2_, ...), custom_call_target="tpu_custom_call" | custom-call | flops 1572864 | bytes 13064 | tf_op jit(solution)/shard_map/project/pallas_call | solution.py:114
  86.1 6.5 %attend.3 = (bf16[1024,256]{1,0:T(8,128)(2,1)S(1)}, f32[1024,128]{1,0:T(8,128)S(1)}, f32[8,128]{1,0:T(8,128)S(1)}) custom-call(s32[10]{0:T(128)S(1)} %get-tuple-element.161.refs_0_, bf16[1024,768]{1,0:T(8,128)(2,1)S(1)} %get-tuple-element.164.refs_1_.refs_4_, f32[1024,128]{1,0:T(8,128)S(1)} %get-tuple-element.165.refs_2_, s32[1024,1]{1,0:T(8,128)S(1)} %copy-done.7, ...), custom_call_target="tpu_custom_call" | custom-call | flops 2097152 | bytes 3080 | tf_op jit(solution)/shard_map/attend/pallas_call | solution.py:114
  93.5 2.9 project_out.2
  96.5 1.6 collective-permute-start.17
  99.0 3.6 %collective-permute-start.18 = (bf16[64,2048]{1,0:T(8,128)(2,1)S(1)}, bf16[64,2048]{1,0:T(8,128)(2,1)S(1)}, u32[]{:S(2)}, u32[]{:S(2)}) collective-permute-start(bf16[64,2048]{1,0:T(8,128)(2,1)S(1)} %slice.147), channel_id=1, source_target_pairs={{0,8},{8,16},{16,24},{24,28},{28,20},{20,12},{12,4},{4,0},{1,9},{9... | collective-permute-start | bytes 786440 | tf_op jit(solution)/shard_map/ppermute | solution.py:762
  103.9 6.9 %collective-permute-done.17.refs_2_ = bf16[1024,256]{1,0:T(8,128)(2,1)S(1)} collective-permute-done((bf16[1024,256]{1,0:T(8,128)(2,1)S(1)}, bf16[1024,256]{1,0:T(8,128)(2,1)S(1)}, u32[]{:S(2)}, u32[]{:S(2)}) %collective-permute-start.17) | collective-permute-done | bytes 524320 | tf_op jit(solution)/shard_map/ppermute | solution.py:810
  110.8 3.1 project_out.3
  115.0 3.3 %middle.2 = (f32[512,1024]{1,0:T(8,128)}, bf16[512,1024]{1,0:T(8,128)(2,1)}, f32[512,128]{1,0:T(8,128)S(1)}, f32[8,128]{1,0:T(8,128)S(1)}) custom-call(s32[10]{0:T(128)S(1)} %get-tuple-element.142.refs_0_, f32[512,1024]{1,0:T(8,128)S(1)} %copy-done.17, bf16[512,1024]{1,0:T(8,128)(2,1)S(1)} %get-tuple-element.174.refs_2_, ...), custom_call_target="tpu_custom_call" | custom-call | flops 10240 | bytes 7428 | tf_op jit(solution)/shard_map/middle/pallas_call | solution.py:114
  119.0 3.0 assemble.3.refs_4_
  122.1 3.2 %middle.3 = (f32[512,1024]{1,0:T(8,128)}, bf16[512,1024]{1,0:T(8,128)(2,1)S(1)}, f32[512,128]{1,0:T(8,128)S(1)}, f32[8,128]{1,0:T(8,128)S(1)}) custom-call(s32[10]{0:T(128)S(1)} %get-tuple-element.161.refs_0_, f32[512,1024]{1,0:T(8,128)S(1)} %copy-done.18, bf16[512,1024]{1,0:T(8,128)(2,1)S(1)} %copy-done.22, ...), custom_call_target="tpu_custom_call" | custom-call | flops 10240 | bytes 7428 | tf_op jit(solution)/shard_map/middle/pallas_call | solution.py:114
  125.3 9.8 %hidden_start.1 = (bf16[512,1024]{1,0:T(8,128)(2,1)S(1)}, bf16[512,1024]{1,0:T(8,128)(2,1)S(1)}, bf16[1024,1024]{1,0:T(8,128)(2,1)S(1)}, bf16[1024,1024]{1,0:T(8,128)(2,1)S(1)}, f32[8,128]{1,0:T(8,128)}) custom-call(s32[10]{0:T(128)S(1)} %get-tuple-element.142.refs_0_, bf16[512,1024]{1,0:T(8,128)(2,1)} %get-tuple-element.181.refs_1_.refs_3_, ...), custom_call_target="tpu_custom_call" | custom-call | flops 6291456 | bytes 14336 | tf_op jit(solution)/shard_map/hidden_start/pallas_call | solution.py:114
  135.7 2.1 collective-permute-done.22
  137.8 1.4 add_convert_fusion.1.refs_8_.refs_1_
  139.2 1.5 collective-permute-start.27
  140.7 10.6 %hidden_end.1 = (bf16[1024,2048]{1,0:T(8,128)(2,1)}, bf16[2,1024,256]{2,1,0:T(8,128)(2,1)}, bf16[2,1024,256]{2,1,0:T(8,128)(2,1)}, f32[8,128]{1,0:T(8,128)S(1)}) custom-call(s32[10]{0:T(128)S(1)} %get-tuple-element.142.refs_0_, bf16[512,1024]{1,0:T(8,128)(2,1)} %get-tuple-element.181.refs_1_.refs_3_, bf16[512,1024]{1,0:T(8,128)(2,1)} %collective-permute-done.20.refs_2_, ...), custom_call_target="tpu_custom_call" | custom-call | flops 6291456 | bytes 20480 | tf_op jit(solution)/shard_map/hidden_end/pallas_call | solution.py:114
  151.4 16.7 %hidden_layer.1 = (bf16[512,1024]{1,0:T(8,128)(2,1)S(1)}, bf16[512,1024]{1,0:T(8,128)(2,1)}, bf16[1024,2048]{1,0:T(8,128)(2,1)}, bf16[2,1024,256]{2,1,0:T(8,128)...) custom-call(s32[10]{0:T(128)S(1)} %get-tuple-element.161.refs_0_, ...), custom_call_target="tpu_custom_call" | custom-call | flops 12582912 | bytes 18432 | tf_op jit(solution)/shard_map/hidden_layer/pallas_call | solution.py:114
  169.6 1.6 copy-done.2
  171.2 4.1 %middle_back.2 = (bf16[512,1024]{1,0:T(8,128)(2,1)S(1)}, f32[1,1024]{1,0:T(1,128)S(1)}, f32[8,128]{1,0:T(8,128)}) custom-call(s32[10]{0:T(128)S(1)} %get-tuple-element.142.refs_0_, bf16[512,1024]{1,0:T(8,128)(2,1)} %add_convert_fusion.1.refs_8_.refs_1_, bf16[512,1024]{1,0:T(8,128)(2,1)} %collective-permute-done.27.refs_2_, ...), custom_call_target="tpu_custom_call" | custom-call | flops 15360 | bytes 6408 | tf_op jit(solution)/shard_map/middle_back/pallas_call | solution.py:114
  175.5 1.3 add_convert_fusion.16
  176.8 3.6 %collective-permute-start.47 = (bf16[64,2048]{1,0:T(8,128)(2,1)S(1)}, bf16[64,2048]{1,0:T(8,128)(2,1)S(1)}, u32[]{:S(2)}, u32[]{:S(2)}) collective-permute-start(bf16[64,2048]{1,0:T(8,128)(2,1)S(1)} %get-tuple-element.319), channel_id=1, source_target_pairs={{0,8},{8,16},{16,24},{24,28},{28,20},{20,12},{12,4},{4,0},{1,9},{9... | collective-permute-start | bytes 786440 | tf_op jit(solution)/shard_map/ppermute | solution.py:787
  180.4 1.6 add_convert_fusion.refs_12_.refs_1_
  182.6 4.0 %collective-permute-done.47 = bf16[64,2048]{1,0:T(8,128)(2,1)S(1)} collective-permute-done((bf16[64,2048]{1,0:T(8,128)(2,1)S(1)}, bf16[64,2048]{1,0:T(8,128)(2,1)S(1)}, u32[]{:S(2)}, u32[]{:S(2)}) %collective-permute-start.47) | collective-permute-done | bytes 262176 | tf_op jit(solution)/shard_map/ppermute | solution.py:787
  186.6 2.2 collective-permute-done.48
  188.8 1.6 add_convert_fusion.13
  190.8 2.0 collective-permute-start.49
  192.8 18.4 %attend_back.2 = (bf16[1024,1152]{1,0:T(8,128)(2,1)}, bf16[2,1024,256]{2,1,0:T(8,128)(2,1)}, bf16[2,1024,256]{2,1,0:T(8,128)(2,1)}, f32[8,128]{1,0:T(8,128)S(1)}) custom-call(s32[10]{0:T(128)S(1)} %get-tuple-element.142.refs_0_, bf16[512,1024]{1,0:T(8,128)(2,1)S(1)} %get-tuple-element.216.refs_1_, bf16[512,1024]{1,0:T(8,128)(2,1)S(1)} %collective-permute-done.28.refs_2_, ...), custom_call_target="tpu_custom_call" | custom-call | flops 9437184 | bytes 13840 | tf_op jit(solution)/shard_map/attend_back/pallas_call | solution.py:114
  211.3 2.1 middle_back.3
  217.5 1.5 collective-permute-start.29
  219.0 2.8 add_convert_fusion.4
  221.8 4.1 %collective-permute-start.51 = (bf16[128,2048]{1,0:T(8,128)(2,1)}, bf16[128,2048]{1,0:T(8,128)(2,1)}, u32[]{:S(2)}, u32[]{:S(2)}) collective-permute-start(bf16[128,2048]{1,0:T(8,128)(2,1)} %get-tuple-element.313), channel_id=1, source_target_pairs={{0,8},{8,16},{16,24},{24,28},{28,20},{20,12},{12,4},{4,0},{1,9},{9... | collective-permute-start | bytes 1572872 | tf_op jit(solution)/shard_map/ppermute | solution.py:787
  228.0 19.9 %attend_back.3 = (bf16[1024,1152]{1,0:T(8,128)(2,1)}, bf16[2,1024,256]{2,1,0:T(8,128)(2,1)}, bf16[2,1024,256]{2,1,0:T(8,128)(2,1)}, f32[8,128]{1,0:T(8,128)}) custom-call(s32[10]{0:T(128)S(1)} %get-tuple-element.161.refs_0_, bf16[512,1024]{1,0:T(8,128)(2,1)S(1)} %get-tuple-element.229.refs_1_, bf16[512,1024]{1,0:T(8,128)(2,1)S(1)} %collective-permute-done.32.refs_2_, ...), custom_call_target="tpu_custom_call" | custom-call | flops 9437184 | bytes 13840 | tf_op jit(solution)/shard_map/attend_back/pallas_call | solution.py:114
  252.4 3.5 %collective-permute-start.33 = (bf16[64,1152]{1,0:T(8,128)(2,1)S(1)}, bf16[64,1152]{1,0:T(8,128)(2,1)S(1)}, u32[]{:S(2)}, u32[]{:S(2)}) collective-permute-start(bf16[64,1152]{1,0:T(8,128)(2,1)S(1)} %get-tuple-element.329), channel_id=1, source_target_pairs={{0,8},{8,16},{16,24},{24,28},{28,20},{20,12},{12,4},{4,0},{1,9},{9... | collective-permute-start | bytes 442376 | tf_op jit(solution)/shard_map/ppermute | solution.py:787
  256.0 1.6 collective-permute-start.37
  257.7 2.5 add_convert_fusion.2
  260.2 2.1 collective-permute-start.53
  265.7 1.3 collective-permute-start.38
  268.2 2.6 fusion.4
  270.8 10.2 %collective-permute-done.39 = bf16[128,1152]{1,0:T(8,128)(2,1)S(1)} collective-permute-done((bf16[128,1152]{1,0:T(8,128)(2,1)S(1)}, bf16[128,1152]{1,0:T(8,128)(2,1)S(1)}, u32[]{:S(2)}, u32[]{:S(2)}) %collective-permute-start.39) | collective-permute-done | bytes 294944 | tf_op jit(solution)/shard_map/ppermute | solution.py:788
  283.3 1.5 convert_add_fusion.4
  286.7 1.5 collective-permute-done.40
  289.5 1.4 add_convert_fusion.8
  291.4 1.6 collective-permute-start.46
  295.8 1.8 collective-permute-start.44
  302.8 1.7 maximum_multiply_fusion
  304.4 2.5 collective-permute-done.56
  309.8 2.0 fusion.1
  (269 shorter events, 55.6 us)
Async XLA Ops:
  5.1 35.5 %copy-start.25 = (bf16[128,2048]{1,0:T(8,128)(2,1)}, bf16[128,2048]{1,0:T(8,128)(2,1)S(1)}, u32[]{:S(2)}) copy-start(bf16[128,2048]{1,0:T(8,128)(2,1)S(1)} %get-tuple-element.159.refs_0_) | copy-start | bytes 1572868
  5.1 11.4 %collective-permute-start = (bf16[128,1408]{1,0:T(8,128)(2,1)S(1)}, bf16[128,1408]{1,0:T(8,128)(2,1)S(1)}, u32[]{:S(2)}, u32[]{:S(2)}) collective-permute-start(bf16[128,1408]{1,0:T(8,128)(2,1)S(1)} %get-tuple-element.141.refs_0_), channel_id=1, source_target_pairs={{0,8},{8,16},{16,24},{24,28},{28,20},{20,12},{12,4},{4,0},{1,9},{9... | collective-permute-start | bytes 1081352 | tf_op jit(solution)/shard_map/ppermute | solution.py:756
  8.2 9.9 %collective-permute-start.1 = (bf16[128,1408]{1,0:T(8,128)(2,1)S(1)}, bf16[128,1408]{1,0:T(8,128)(2,1)S(1)}, u32[]{:S(2)}, u32[]{:S(2)}) collective-permute-start(bf16[128,1408]{1,0:T(8,128)(2,1)S(1)} %get-tuple-element.141.refs_0_), channel_id=1, source_target_pairs={{8,0},{16,8},{24,16},{28,24},{20,28},{12,20},{4,12},{0,4},{9,1},{1... | collective-permute-start | bytes 1081352 | tf_op jit(solution)/shard_map/ppermute | solution.py:757
  18.1 12.3 %collective-permute-start.2 = (bf16[128,1408]{1,0:T(8,128)(2,1)S(1)}, bf16[128,1408]{1,0:T(8,128)(2,1)S(1)}, u32[]{:S(2)}, u32[]{:S(2)}) collective-permute-start(bf16[128,1408]{1,0:T(8,128)(2,1)S(1)} %collective-permute-done.refs_1_), channel_id=1, source_target_pairs={{0,8},{8,16},{16,24},{24,28},{28,20},{20,12},{12,4},{4,0},{1,9},{9... | collective-permute-start | bytes 1081352 | tf_op jit(solution)/shard_map/ppermute | solution.py:756
  19.7 10.7 %collective-permute-start.3 = (bf16[128,1408]{1,0:T(8,128)(2,1)S(1)}, bf16[128,1408]{1,0:T(8,128)(2,1)S(1)}, u32[]{:S(2)}, u32[]{:S(2)}) collective-permute-start(bf16[128,1408]{1,0:T(8,128)(2,1)S(1)} %collective-permute-done.1.refs_2_), channel_id=1, source_target_pairs={{8,0},{16,8},{24,16},{28,24},{20,28},{12,20},{4,12},{0,4},{9,1},{1... | collective-permute-start | bytes 1081352 | tf_op jit(solution)/shard_map/ppermute | solution.py:757
  20.5 20.5 %copy-start.30 = (s32[2]{0:T(128)S(1)}, s32[2]{0:T(128)}, u32[]{:S(2)}) copy-start(s32[2]{0:T(128)} %refs_0_.1) | copy-start | bytes 28
  30.4 23.6 %copy-start.46 = (bf16[128,1408]{1,0:T(8,128)(2,1)}, bf16[128,1408]{1,0:T(8,128)(2,1)S(1)}, u32[]{:S(2)}) copy-start(bf16[128,1408]{1,0:T(8,128)(2,1)S(1)} %collective-permute-done.2.refs_3_) | copy-start | bytes 1081348
  30.4 23.6 %copy-start.47 = (bf16[128,1408]{1,0:T(8,128)(2,1)}, bf16[128,1408]{1,0:T(8,128)(2,1)S(1)}, u32[]{:S(2)}) copy-start(bf16[128,1408]{1,0:T(8,128)(2,1)S(1)} %collective-permute-done.3.refs_4_) | copy-start | bytes 1081348
  30.4 8.6 %collective-permute-start.4 = (bf16[128,1408]{1,0:T(8,128)(2,1)S(1)}, bf16[128,1408]{1,0:T(8,128)(2,1)S(1)}, u32[]{:S(2)}, u32[]{:S(2)}) collective-permute-start(bf16[128,1408]{1,0:T(8,128)(2,1)S(1)} %collective-permute-done.2.refs_3_), channel_id=1, source_target_pairs={{0,8},{8,16},{16,24},{24,28},{28,20},{20,12},{12,4},{4,0},{1,9},{9... | collective-permute-start | bytes 1081352 | tf_op jit(solution)/shard_map/ppermute | solution.py:756
  32.1 9.0 %collective-permute-start.5 = (bf16[128,1408]{1,0:T(8,128)(2,1)S(1)}, bf16[128,1408]{1,0:T(8,128)(2,1)S(1)}, u32[]{:S(2)}, u32[]{:S(2)}) collective-permute-start(bf16[128,1408]{1,0:T(8,128)(2,1)S(1)} %collective-permute-done.3.refs_4_), channel_id=1, source_target_pairs={{8,0},{16,8},{24,16},{28,24},{20,28},{12,20},{4,12},{0,4},{9,1},{1... | collective-permute-start | bytes 1081352 | tf_op jit(solution)/shard_map/ppermute | solution.py:757
  39.0 18.7 %collective-permute-start.8 = (bf16[128,2048]{1,0:T(8,128)(2,1)S(1)}, bf16[128,2048]{1,0:T(8,128)(2,1)}, u32[]{:S(2)}, u32[]{:S(2)}) collective-permute-start(bf16[128,2048]{1,0:T(8,128)(2,1)S(1)} %get-tuple-element.159.refs_0_), channel_id=1, source_target_pairs={{0,8},{8,16},{16,24},{24,28},{28,20},{20,12},{12,4},{4,0},{1,9},{9... | collective-permute-start | bytes 1572872 | tf_op jit(solution)/shard_map/ppermute | solution.py:756
  40.6 17.1 %collective-permute-start.9 = (bf16[128,2048]{1,0:T(8,128)(2,1)S(1)}, bf16[128,2048]{1,0:T(8,128)(2,1)}, u32[]{:S(2)}, u32[]{:S(2)}) collective-permute-start(bf16[128,2048]{1,0:T(8,128)(2,1)S(1)} %get-tuple-element.159.refs_0_), channel_id=1, source_target_pairs={{8,0},{16,8},{24,16},{28,24},{20,28},{12,20},{4,12},{0,4},{9,1},{1... | collective-permute-start | bytes 1572872 | tf_op jit(solution)/shard_map/ppermute | solution.py:757
  41.1 12.8 %collective-permute-start.6 = (bf16[64,1408]{1,0:T(8,128)(2,1)S(1)}, bf16[64,1408]{1,0:T(8,128)(2,1)S(1)}, u32[]{:S(2)}, u32[]{:S(2)}) collective-permute-start(bf16[64,1408]{1,0:T(8,128)(2,1)S(1)} %slice.139), channel_id=1, source_target_pairs={{0,8},{8,16},{16,24},{24,28},{28,20},{20,12},{12,4},{4,0},{1,9},{9... | collective-permute-start | bytes 540680 | tf_op jit(solution)/shard_map/ppermute | solution.py:762
  42.8 12.6 %collective-permute-start.7 = (bf16[64,1408]{1,0:T(8,128)(2,1)S(1)}, bf16[64,1408]{1,0:T(8,128)(2,1)}, u32[]{:S(2)}, u32[]{:S(2)}) collective-permute-start(bf16[64,1408]{1,0:T(8,128)(2,1)S(1)} %slice.140), channel_id=1, source_target_pairs={{8,0},{16,8},{24,16},{28,24},{20,28},{12,20},{4,12},{0,4},{9,1},{1... | collective-permute-start | bytes 540680 | tf_op jit(solution)/shard_map/ppermute | solution.py:763
  57.7 170.2 %copy-start = (bf16[1024,1408]{1,0:T(8,128)(2,1)}, bf16[1024,1408]{1,0:T(8,128)(2,1)S(1)}, u32[]{:S(2)}) copy-start(bf16[1024,1408]{1,0:T(8,128)(2,1)S(1)} %assemble.2.refs_4_.refs_3_) | copy-start | bytes 8650756
  57.8 18.3 %collective-permute-start.12 = (bf16[128,2048]{1,0:T(8,128)(2,1)}, bf16[128,2048]{1,0:T(8,128)(2,1)}, u32[]{:S(2)}, u32[]{:S(2)}) collective-permute-start(bf16[128,2048]{1,0:T(8,128)(2,1)} %collective-permute-done.8.refs_6_.refs_1_), channel_id=1, source_target_pairs={{0,8},{8,16},{16,24},{24,28},{28,20},{20,12},{12,4},{4,0},{1,9},{9... | collective-permute-start | bytes 1572872 | tf_op jit(solution)/shard_map/ppermute | solution.py:756
  59.4 16.7 %collective-permute-start.13 = (bf16[128,2048]{1,0:T(8,128)(2,1)}, bf16[128,2048]{1,0:T(8,128)(2,1)}, u32[]{:S(2)}, u32[]{:S(2)}) collective-permute-start(bf16[128,2048]{1,0:T(8,128)(2,1)} %collective-permute-done.9.refs_7_.refs_2_), channel_id=1, source_target_pairs={{8,0},{16,8},{24,16},{28,24},{20,28},{12,20},{4,12},{0,4},{9,1},{1... | collective-permute-start | bytes 1572872 | tf_op jit(solution)/shard_map/ppermute | solution.py:757
  60.4 20.0 %collective-permute-start.11 = (bf16[1024,256]{1,0:T(8,128)(2,1)S(1)}, bf16[1024,256]{1,0:T(8,128)(2,1)}, u32[]{:S(2)}, u32[]{:S(2)}) collective-permute-start(bf16[1024,256]{1,0:T(8,128)(2,1)S(1)} %get-tuple-element.332.refs_3_), channel_id=1, source_target_pairs={{0,2},{1,3},{2,0},{3,1},{4,6},{5,7},{6,4},{7,5},{8,10},{9,11},{10,... | collective-permute-start | bytes 1572872 | tf_op jit(solution)/shard_map/ppermute | solution.py:810
  75.6 17.9 %collective-permute-start.10 = (bf16[1024,256]{1,0:T(8,128)(2,1)}, bf16[1024,256]{1,0:T(8,128)(2,1)}, u32[]{:S(2)}, u32[]{:S(2)}) collective-permute-start(bf16[1024,256]{1,0:T(8,128)(2,1)} %get-tuple-element.160.refs_1_.refs_5_), channel_id=1, source_target_pairs={{0,2},{1,3},{2,0},{3,1},{4,6},{5,7},{6,4},{7,5},{8,10},{9,11},{10,... | collective-permute-start | bytes 1572872 | tf_op jit(solution)/shard_map/ppermute | solution.py:810
  76.1 17.4 %collective-permute-start.14 = (bf16[128,2048]{1,0:T(8,128)(2,1)}, bf16[128,2048]{1,0:T(8,128)(2,1)}, u32[]{:S(2)}, u32[]{:S(2)}) collective-permute-start(bf16[128,2048]{1,0:T(8,128)(2,1)} %collective-permute-done.12.refs_6_.refs_3_), channel_id=1, source_target_pairs={{0,8},{8,16},{16,24},{24,28},{28,20},{20,12},{12,4},{4,0},{1,9},{9... | collective-permute-start | bytes 1572872 | tf_op jit(solution)/shard_map/ppermute | solution.py:756
  79.3 14.2 %collective-permute-start.15 = (bf16[128,2048]{1,0:T(8,128)(2,1)}, bf16[128,2048]{1,0:T(8,128)(2,1)}, u32[]{:S(2)}, u32[]{:S(2)}) collective-permute-start(bf16[128,2048]{1,0:T(8,128)(2,1)} %collective-permute-done.13.refs_7_.refs_4_), channel_id=1, source_target_pairs={{8,0},{16,8},{24,16},{28,24},{20,28},{12,20},{4,12},{0,4},{9,1},{1... | collective-permute-start | bytes 1572872 | tf_op jit(solution)/shard_map/ppermute | solution.py:757
  96.4 18.6 %copy-start.17 = (f32[512,1024]{1,0:T(8,128)S(1)}, f32[512,1024]{1,0:T(8,128)}, u32[]{:S(2)}) copy-start(f32[512,1024]{1,0:T(8,128)} %get-tuple-element.152.refs_1_) | copy-start | bytes 6291460
  96.4 18.6 %collective-permute-start.16 = (bf16[512,1024]{1,0:T(8,128)(2,1)S(1)}, bf16[512,1024]{1,0:T(8,128)(2,1)S(1)}, u32[]{:S(2)}, u32[]{:S(2)}) collective-permute-start(bf16[512,1024]{1,0:T(8,128)(2,1)S(1)} %get-tuple-element.175), channel_id=1, source_target_pairs={{0,1},{1,0},{2,3},{3,2},{4,5},{5,4},{6,7},{7,6},{8,9},{9,8},{10,11... | collective-permute-start | bytes 3145736 | tf_op jit(solution)/shard_map/ppermute | solution.py:810
  96.5 14.3 %collective-permute-start.17 = (bf16[1024,256]{1,0:T(8,128)(2,1)S(1)}, bf16[1024,256]{1,0:T(8,128)(2,1)S(1)}, u32[]{:S(2)}, u32[]{:S(2)}) collective-permute-start(bf16[1024,256]{1,0:T(8,128)(2,1)S(1)} %get-tuple-element.176.refs_1_.refs_5_), channel_id=1, source_target_pairs={{0,2},{1,3},{2,0},{3,1},{4,6},{5,7},{6,4},{7,5},{8,10},{9,11},{10,... | collective-permute-start | bytes 1572872 | tf_op jit(solution)/shard_map/ppermute | solution.py:810
  99.0 15.9 %collective-permute-start.18 = (bf16[64,2048]{1,0:T(8,128)(2,1)S(1)}, bf16[64,2048]{1,0:T(8,128)(2,1)S(1)}, u32[]{:S(2)}, u32[]{:S(2)}) collective-permute-start(bf16[64,2048]{1,0:T(8,128)(2,1)S(1)} %slice.147), channel_id=1, source_target_pairs={{0,8},{8,16},{16,24},{24,28},{28,20},{20,12},{12,4},{4,0},{1,9},{9... | collective-permute-start | bytes 786440 | tf_op jit(solution)/shard_map/ppermute | solution.py:762
  103.6 11.3 %collective-permute-start.19 = (bf16[64,2048]{1,0:T(8,128)(2,1)S(1)}, bf16[64,2048]{1,0:T(8,128)(2,1)S(1)}, u32[]{:S(2)}, u32[]{:S(2)}) collective-permute-start(bf16[64,2048]{1,0:T(8,128)(2,1)S(1)} %slice.148), channel_id=1, source_target_pairs={{8,0},{16,8},{24,16},{28,24},{20,28},{12,20},{4,12},{0,4},{9,1},{1... | collective-permute-start | bytes 786440 | tf_op jit(solution)/shard_map/ppermute | solution.py:763
  115.0 7.0 %collective-permute-start.21 = (bf16[512,1024]{1,0:T(8,128)(2,1)}, bf16[512,1024]{1,0:T(8,128)(2,1)}, u32[]{:S(2)}, u32[]{:S(2)}) collective-permute-start(bf16[512,1024]{1,0:T(8,128)(2,1)} %get-tuple-element.194), channel_id=1, source_target_pairs={{0,1},{1,0},{2,3},{3,2},{4,5},{5,4},{6,7},{7,6},{8,9},{9,8},{10,11... | collective-permute-start | bytes 3145736 | tf_op jit(solution)/shard_map/ppermute | solution.py:810
  118.3 7.0 %collective-permute-start.20 = (bf16[512,1024]{1,0:T(8,128)(2,1)}, bf16[512,1024]{1,0:T(8,128)(2,1)}, u32[]{:S(2)}, u32[]{:S(2)}) collective-permute-start(bf16[512,1024]{1,0:T(8,128)(2,1)} %get-tuple-element.181.refs_1_.refs_3_), channel_id=1, source_target_pairs={{0,1},{1,0},{2,3},{3,2},{4,5},{5,4},{6,7},{7,6},{8,9},{9,8},{10,11... | collective-permute-start | bytes 3145736 | tf_op jit(solution)/shard_map/ppermute | solution.py:810
  125.3 26.1 %copy-start.13 = (bf16[512,1024]{1,0:T(8,128)(2,1)}, bf16[512,1024]{1,0:T(8,128)(2,1)S(1)}, u32[]{:S(2)}) copy-start(bf16[512,1024]{1,0:T(8,128)(2,1)S(1)} %get-tuple-element.205.refs_1_.refs_3_) | copy-start | bytes 3145732
  135.1 2.7 collective-permute-start.22
  135.2 16.1 %collective-permute-start.24 = (bf16[512,1024]{1,0:T(8,128)(2,1)S(1)}, bf16[512,1024]{1,0:T(8,128)(2,1)S(1)}, u32[]{:S(2)}, u32[]{:S(2)}) collective-permute-start(bf16[512,1024]{1,0:T(8,128)(2,1)S(1)} %get-tuple-element.205.refs_1_.refs_3_), channel_id=1, source_target_pairs={{0,1},{1,0},{2,3},{3,2},{4,5},{5,4},{6,7},{7,6},{8,9},{9,8},{10,11... | collective-permute-start | bytes 3145736 | tf_op jit(solution)/shard_map/ppermute | solution.py:810
  139.2 30.4 %collective-permute-start.27 = (bf16[512,1024]{1,0:T(8,128)(2,1)}, bf16[512,1024]{1,0:T(8,128)(2,1)}, u32[]{:S(2)}, u32[]{:S(2)}) collective-permute-start(bf16[512,1024]{1,0:T(8,128)(2,1)} %add_convert_fusion.1.refs_8_.refs_1_), channel_id=1, source_target_pairs={{0,2},{1,3},{2,0},{3,1},{4,6},{5,7},{6,4},{7,5},{8,10},{9,11},{10,... | collective-permute-start | bytes 3145736 | tf_op jit(solution)/shard_map/ppermute | solution.py:810
  169.1 6.4 %collective-permute-start.25 = (bf16[512,1024]{1,0:T(8,128)(2,1)}, bf16[512,1024]{1,0:T(8,128)(2,1)}, u32[]{:S(2)}, u32[]{:S(2)}) collective-permute-start(bf16[512,1024]{1,0:T(8,128)(2,1)} %get-tuple-element.210), channel_id=1, source_target_pairs={{0,1},{1,0},{2,3},{3,2},{4,5},{5,4},{6,7},{7,6},{8,9},{9,8},{10,11... | collective-permute-start | bytes 3145736 | tf_op jit(solution)/shard_map/ppermute | solution.py:810
  169.1 44.4 %collective-permute-start.30 = (bf16[2,1024,256]{2,1,0:T(8,128)(2,1)}, bf16[2,1024,256]{2,1,0:T(8,128)(2,1)S(1)}, u32[]{:S(2)}, u32[]{:S(2)}) collective-permute-start(bf16[2,1024,256]{2,1,0:T(8,128)(2,1)} %get-tuple-element.225), channel_id=1, source_target_pairs={{0,1},{1,0},{2,3},{3,2},{4,5},{5,4},{6,7},{7,6},{8,9},{9,8},{10,11... | collective-permute-start | bytes 3145736 | tf_op jit(solution)/shard_map/ppermute | solution.py:810
  175.4 15.5 %collective-permute-start.28 = (bf16[512,1024]{1,0:T(8,128)(2,1)S(1)}, bf16[512,1024]{1,0:T(8,128)(2,1)S(1)}, u32[]{:S(2)}, u32[]{:S(2)}) collective-permute-start(bf16[512,1024]{1,0:T(8,128)(2,1)S(1)} %get-tuple-element.216.refs_1_), channel_id=1, source_target_pairs={{0,1},{1,0},{2,3},{3,2},{4,5},{5,4},{6,7},{7,6},{8,9},{9,8},{10,11... | collective-permute-start | bytes 3145736 | tf_op jit(solution)/shard_map/ppermute | solution.py:810
  176.8 9.8 %collective-permute-start.47 = (bf16[64,2048]{1,0:T(8,128)(2,1)S(1)}, bf16[64,2048]{1,0:T(8,128)(2,1)S(1)}, u32[]{:S(2)}, u32[]{:S(2)}) collective-permute-start(bf16[64,2048]{1,0:T(8,128)(2,1)S(1)} %get-tuple-element.319), channel_id=1, source_target_pairs={{0,8},{8,16},{16,24},{24,28},{28,20},{20,12},{12,4},{4,0},{1,9},{9... | collective-permute-start | bytes 786440 | tf_op jit(solution)/shard_map/ppermute | solution.py:787
  180.4 8.4 %collective-permute-start.48 = (bf16[64,2048]{1,0:T(8,128)(2,1)S(1)}, bf16[64,2048]{1,0:T(8,128)(2,1)S(1)}, u32[]{:S(2)}, u32[]{:S(2)}) collective-permute-start(bf16[64,2048]{1,0:T(8,128)(2,1)S(1)} %get-tuple-element.318), channel_id=1, source_target_pairs={{8,0},{16,8},{24,16},{28,24},{20,28},{12,20},{4,12},{0,4},{9,1},{1... | collective-permute-start | bytes 786440 | tf_op jit(solution)/shard_map/ppermute | solution.py:788
  182.0 29.3 %collective-permute-start.26 = (bf16[512,1024]{1,0:T(8,128)(2,1)S(1)}, bf16[512,1024]{1,0:T(8,128)(2,1)S(1)}, u32[]{:S(2)}, u32[]{:S(2)}) collective-permute-start(bf16[512,1024]{1,0:T(8,128)(2,1)S(1)} %add_convert_fusion.refs_12_.refs_1_), channel_id=1, source_target_pairs={{0,2},{1,3},{2,0},{3,1},{4,6},{5,7},{6,4},{7,5},{8,10},{9,11},{10,... | collective-permute-start | bytes 3145736 | tf_op jit(solution)/shard_map/ppermute | solution.py:810
  186.6 29.2 %collective-permute-start.23 = (bf16[2,1024,256]{2,1,0:T(8,128)(2,1)S(1)}, bf16[2,1024,256]{2,1,0:T(8,128)(2,1)S(1)}, u32[]{:S(2)}, u32[]{:S(2)}) collective-permute-start(bf16[2,1024,256]{2,1,0:T(8,128)(2,1)S(1)} %copy-done.51), channel_id=1, source_target_pairs={{0,1},{1,0},{2,3},{3,2},{4,5},{5,4},{6,7},{7,6},{8,9},{9,8},{10,11... | collective-permute-start | bytes 3145736 | tf_op jit(solution)/shard_map/ppermute | solution.py:810
  190.4 27.1 %collective-permute-start.50 = (bf16[128,2048]{1,0:T(8,128)(2,1)S(1)}, bf16[128,2048]{1,0:T(8,128)(2,1)S(1)}, u32[]{:S(2)}, u32[]{:S(2)}) collective-permute-start(bf16[128,2048]{1,0:T(8,128)(2,1)S(1)} %pad_maximum_fusion.1), channel_id=1, source_target_pairs={{8,0},{16,8},{24,16},{28,24},{20,28},{12,20},{4,12},{0,4},{9,1},{1... | collective-permute-start | bytes 1572872 | tf_op jit(solution)/shard_map/ppermute | solution.py:788
  190.8 28.2 %collective-permute-start.49 = (bf16[128,2048]{1,0:T(8,128)(2,1)S(1)}, bf16[128,2048]{1,0:T(8,128)(2,1)S(1)}, u32[]{:S(2)}, u32[]{:S(2)}) collective-permute-start(bf16[128,2048]{1,0:T(8,128)(2,1)S(1)} %pad_maximum_fusion), channel_id=1, source_target_pairs={{0,8},{8,16},{16,24},{24,28},{28,20},{20,12},{12,4},{4,0},{1,9},{9... | collective-permute-start | bytes 1572872 | tf_op jit(solution)/shard_map/ppermute | solution.py:787
  213.4 14.5 %collective-permute-start.32 = (bf16[512,1024]{1,0:T(8,128)(2,1)S(1)}, bf16[512,1024]{1,0:T(8,128)(2,1)S(1)}, u32[]{:S(2)}, u32[]{:S(2)}) collective-permute-start(bf16[512,1024]{1,0:T(8,128)(2,1)S(1)} %get-tuple-element.229.refs_1_), channel_id=1, source_target_pairs={{0,1},{1,0},{2,3},{3,2},{4,5},{5,4},{6,7},{7,6},{8,9},{9,8},{10,11... | collective-permute-start | bytes 3145736 | tf_op jit(solution)/shard_map/ppermute | solution.py:810
  213.5 34.4 %collective-permute-start.35 = (bf16[2,1024,256]{2,1,0:T(8,128)(2,1)S(1)}, bf16[2,1024,256]{2,1,0:T(8,128)(2,1)S(1)}, u32[]{:S(2)}, u32[]{:S(2)}) collective-permute-start(bf16[2,1024,256]{2,1,0:T(8,128)(2,1)S(1)} %copy-done.52), channel_id=1, source_target_pairs={{0,1},{1,0},{2,3},{3,2},{4,5},{5,4},{6,7},{7,6},{8,9},{9,8},{10,11... | collective-permute-start | bytes 3145736 | tf_op jit(solution)/shard_map/ppermute | solution.py:810
  215.8 35.4 %collective-permute-start.31 = (bf16[1,1024,256]{2,1,0:T(8,128)(2,1)}, bf16[1,1024,256]{2,1,0:T(8,128)(2,1)}, u32[]{:S(2)}, u32[]{:S(2)}) collective-permute-start(bf16[1,1024,256]{2,1,0:T(8,128)(2,1)} %dynamic-slice_convert_fusion.2), channel_id=1, source_target_pairs={{0,2},{1,3},{2,0},{3,1},{4,6},{5,7},{6,4},{7,5},{8,10},{9,11},{10,... | collective-permute-start | bytes 1572872 | tf_op jit(solution)/shard_map/ppermute | solution.py:810
  217.5 33.7 %collective-permute-start.29 = (bf16[1,1024,256]{2,1,0:T(8,128)(2,1)}, bf16[1,1024,256]{2,1,0:T(8,128)(2,1)}, u32[]{:S(2)}, u32[]{:S(2)}) collective-permute-start(bf16[1,1024,256]{2,1,0:T(8,128)(2,1)} %dynamic-slice_convert_fusion.3), channel_id=1, source_target_pairs={{0,2},{1,3},{2,0},{3,1},{4,6},{5,7},{6,4},{7,5},{8,10},{9,11},{10,... | collective-permute-start | bytes 1572872 | tf_op jit(solution)/shard_map/ppermute | solution.py:810
  221.8 34.3 %collective-permute-start.51 = (bf16[128,2048]{1,0:T(8,128)(2,1)}, bf16[128,2048]{1,0:T(8,128)(2,1)}, u32[]{:S(2)}, u32[]{:S(2)}) collective-permute-start(bf16[128,2048]{1,0:T(8,128)(2,1)} %get-tuple-element.313), channel_id=1, source_target_pairs={{0,8},{8,16},{16,24},{24,28},{28,20},{20,12},{12,4},{4,0},{1,9},{9... | collective-permute-start | bytes 1572872 | tf_op jit(solution)/shard_map/ppermute | solution.py:787
  227.9 29.7 %collective-permute-start.52 = (bf16[128,2048]{1,0:T(8,128)(2,1)}, bf16[128,2048]{1,0:T(8,128)(2,1)}, u32[]{:S(2)}, u32[]{:S(2)}) collective-permute-start(bf16[128,2048]{1,0:T(8,128)(2,1)} %get-tuple-element.312), channel_id=1, source_target_pairs={{8,0},{16,8},{24,16},{28,24},{20,28},{12,20},{4,12},{0,4},{9,1},{1... | collective-permute-start | bytes 1572872 | tf_op jit(solution)/shard_map/ppermute | solution.py:788
  250.8 13.8 %collective-permute-start.36 = (bf16[1,512,256]{2,1,0:T(8,128)(2,1)S(1)}, bf16[1,512,256]{2,1,0:T(8,128)(2,1)S(1)}, u32[]{:S(2)}, u32[]{:S(2)}) collective-permute-start(bf16[1,512,256]{2,1,0:T(8,128)(2,1)S(1)} %get-tuple-element.351), channel_id=1, source_target_pairs={{0,2},{1,3},{2,0},{3,1},{4,6},{5,7},{6,4},{7,5},{8,10},{9,11},{10,... | collective-permute-start | bytes 786440 | tf_op jit(solution)/shard_map/ppermute | solution.py:810
  252.4 10.9 %collective-permute-start.33 = (bf16[64,1152]{1,0:T(8,128)(2,1)S(1)}, bf16[64,1152]{1,0:T(8,128)(2,1)S(1)}, u32[]{:S(2)}, u32[]{:S(2)}) collective-permute-start(bf16[64,1152]{1,0:T(8,128)(2,1)S(1)} %get-tuple-element.329), channel_id=1, source_target_pairs={{0,8},{8,16},{16,24},{24,28},{28,20},{20,12},{12,4},{4,0},{1,9},{9... | collective-permute-start | bytes 442376 | tf_op jit(solution)/shard_map/ppermute | solution.py:787
  255.9 7.5 %collective-permute-start.34 = (bf16[64,1152]{1,0:T(8,128)(2,1)S(1)}, bf16[64,1152]{1,0:T(8,128)(2,1)S(1)}, u32[]{:S(2)}, u32[]{:S(2)}) collective-permute-start(bf16[64,1152]{1,0:T(8,128)(2,1)S(1)} %get-tuple-element.328), channel_id=1, source_target_pairs={{8,0},{16,8},{24,16},{28,24},{20,28},{12,20},{4,12},{0,4},{9,1},{1... | collective-permute-start | bytes 442376 | tf_op jit(solution)/shard_map/ppermute | solution.py:788
  256.0 14.7 %collective-permute-start.37 = (bf16[1,512,256]{2,1,0:T(8,128)(2,1)S(1)}, bf16[1,512,256]{2,1,0:T(8,128)(2,1)S(1)}, u32[]{:S(2)}, u32[]{:S(2)}) collective-permute-start(bf16[1,512,256]{2,1,0:T(8,128)(2,1)S(1)} %get-tuple-element.350), channel_id=1, source_target_pairs={{0,2},{1,3},{2,0},{3,1},{4,6},{5,7},{6,4},{7,5},{8,10},{9,11},{10,... | collective-permute-start | bytes 786440 | tf_op jit(solution)/shard_map/ppermute | solution.py:810
  260.2 23.1 %collective-permute-start.53 = (bf16[128,2048]{1,0:T(8,128)(2,1)S(1)}, bf16[128,2048]{1,0:T(8,128)(2,1)S(1)}, u32[]{:S(2)}, u32[]{:S(2)}) collective-permute-start(bf16[128,2048]{1,0:T(8,128)(2,1)S(1)} %get-tuple-element.311), channel_id=1, source_target_pairs={{0,8},{8,16},{16,24},{24,28},{28,20},{20,12},{12,4},{4,0},{1,9},{9... | collective-permute-start | bytes 1572872 | tf_op jit(solution)/shard_map/ppermute | solution.py:787
  263.4 19.9 %collective-permute-start.54 = (bf16[128,2048]{1,0:T(8,128)(2,1)S(1)}, bf16[128,2048]{1,0:T(8,128)(2,1)S(1)}, u32[]{:S(2)}, u32[]{:S(2)}) collective-permute-start(bf16[128,2048]{1,0:T(8,128)(2,1)S(1)} %get-tuple-element.310), channel_id=1, source_target_pairs={{8,0},{16,8},{24,16},{28,24},{20,28},{12,20},{4,12},{0,4},{9,1},{1... | collective-permute-start | bytes 1572872 | tf_op jit(solution)/shard_map/ppermute | solution.py:788
  264.8 16.1 %collective-permute-start.39 = (bf16[128,1152]{1,0:T(8,128)(2,1)S(1)}, bf16[128,1152]{1,0:T(8,128)(2,1)S(1)}, u32[]{:S(2)}, u32[]{:S(2)}) collective-permute-start(bf16[128,1152]{1,0:T(8,128)(2,1)S(1)} %pad_maximum_fusion.3), channel_id=1, source_target_pairs={{8,0},{16,8},{24,16},{28,24},{20,28},{12,20},{4,12},{0,4},{9,1},{1... | collective-permute-start | bytes 884744 | tf_op jit(solution)/shard_map/ppermute | solution.py:788
  265.7 15.2 %collective-permute-start.38 = (bf16[128,1152]{1,0:T(8,128)(2,1)S(1)}, bf16[128,1152]{1,0:T(8,128)(2,1)S(1)}, u32[]{:S(2)}, u32[]{:S(2)}) collective-permute-start(bf16[128,1152]{1,0:T(8,128)(2,1)S(1)} %pad_maximum_fusion.2), channel_id=1, source_target_pairs={{0,8},{8,16},{16,24},{24,28},{28,20},{20,12},{12,4},{4,0},{1,9},{9... | collective-permute-start | bytes 884744 | tf_op jit(solution)/shard_map/ppermute | solution.py:787
  270.7 22.4 %collective-permute-start.42 = (bf16[2,1024,256]{2,1,0:T(8,128)(2,1)}, bf16[2,1024,256]{2,1,0:T(8,128)(2,1)}, u32[]{:S(2)}, u32[]{:S(2)}) collective-permute-start(bf16[2,1024,256]{2,1,0:T(8,128)(2,1)} %get-tuple-element.253), channel_id=1, source_target_pairs={{0,1},{1,0},{2,3},{3,2},{4,5},{5,4},{6,7},{7,6},{8,9},{9,8},{10,11... | collective-permute-start | bytes 3145736 | tf_op jit(solution)/shard_map/ppermute | solution.py:810
  281.2 7.0 %collective-permute-start.40 = (bf16[128,1152]{1,0:T(8,128)(2,1)S(1)}, bf16[128,1152]{1,0:T(8,128)(2,1)S(1)}, u32[]{:S(2)}, u32[]{:S(2)}) collective-permute-start(bf16[128,1152]{1,0:T(8,128)(2,1)S(1)} %get-tuple-element.323), channel_id=1, source_target_pairs={{0,8},{8,16},{16,24},{24,28},{28,20},{20,12},{12,4},{4,0},{1,9},{9... | collective-permute-start | bytes 884744 | tf_op jit(solution)/shard_map/ppermute | solution.py:787
  282.1 7.3 %collective-permute-start.41 = (bf16[128,1152]{1,0:T(8,128)(2,1)S(1)}, bf16[128,1152]{1,0:T(8,128)(2,1)S(1)}, u32[]{:S(2)}, u32[]{:S(2)}) collective-permute-start(bf16[128,1152]{1,0:T(8,128)(2,1)S(1)} %get-tuple-element.322), channel_id=1, source_target_pairs={{8,0},{16,8},{24,16},{28,24},{20,28},{12,20},{4,12},{0,4},{9,1},{1... | collective-permute-start | bytes 884744 | tf_op jit(solution)/shard_map/ppermute | solution.py:788
  290.9 6.8 %collective-permute-start.45 = (bf16[128,1152]{1,0:T(8,128)(2,1)S(1)}, bf16[128,1152]{1,0:T(8,128)(2,1)S(1)}, u32[]{:S(2)}, u32[]{:S(2)}) collective-permute-start(bf16[128,1152]{1,0:T(8,128)(2,1)S(1)} %get-tuple-element.321), channel_id=1, source_target_pairs={{0,8},{8,16},{16,24},{24,28},{28,20},{20,12},{12,4},{4,0},{1,9},{9... | collective-permute-start | bytes 884744 | tf_op jit(solution)/shard_map/ppermute | solution.py:787
  291.4 6.7 %collective-permute-start.46 = (bf16[128,1152]{1,0:T(8,128)(2,1)S(1)}, bf16[128,1152]{1,0:T(8,128)(2,1)S(1)}, u32[]{:S(2)}, u32[]{:S(2)}) collective-permute-start(bf16[128,1152]{1,0:T(8,128)(2,1)S(1)} %get-tuple-element.320), channel_id=1, source_target_pairs={{8,0},{16,8},{24,16},{28,24},{20,28},{12,20},{4,12},{0,4},{9,1},{1... | collective-permute-start | bytes 884744 | tf_op jit(solution)/shard_map/ppermute | solution.py:788
  295.6 13.1 %collective-permute-start.43 = (bf16[1,512,256]{2,1,0:T(8,128)(2,1)}, bf16[1,512,256]{2,1,0:T(8,128)(2,1)}, u32[]{:S(2)}, u32[]{:S(2)}) collective-permute-start(bf16[1,512,256]{2,1,0:T(8,128)(2,1)} %get-tuple-element.348), channel_id=1, source_target_pairs={{0,2},{1,3},{2,0},{3,1},{4,6},{5,7},{6,4},{7,5},{8,10},{9,11},{10,... | collective-permute-start | bytes 786440 | tf_op jit(solution)/shard_map/ppermute | solution.py:810
  295.8 12.9 %collective-permute-start.44 = (bf16[1,512,256]{2,1,0:T(8,128)(2,1)}, bf16[1,512,256]{2,1,0:T(8,128)(2,1)}, u32[]{:S(2)}, u32[]{:S(2)}) collective-permute-start(bf16[1,512,256]{2,1,0:T(8,128)(2,1)} %get-tuple-element.349), channel_id=1, source_target_pairs={{0,2},{1,3},{2,0},{3,1},{4,6},{5,7},{6,4},{7,5},{8,10},{9,11},{10,... | collective-permute-start | bytes 786440 | tf_op jit(solution)/shard_map/ppermute | solution.py:810
  300.0 1.6 collective-permute-start.55
  302.5 4.4 %collective-permute-start.56 = (f32[128,128]{1,0:T(8,128)S(1)}, f32[128,128]{1,0:T(8,128)S(1)}, u32[]{:S(2)}, u32[]{:S(2)}) collective-permute-start(f32[128,128]{1,0:T(8,128)S(1)} %slice_add_fusion), channel_id=1, source_target_pairs={{0,2},{1,3},{2,0},{3,1},{4,6},{5,7},{6,4},{7,5},{8,10},{9,11},{10,... | collective-permute-start | bytes 196616 | tf_op jit(solution)/shard_map/ppermute | solution.py:802
  (47 other events, 248.0 us)

commit v2 on v1

--- a/solution.py
+++ b/solution.py
@@ -1010,7 +1010,6 @@
     token = middle_back_of(0, (token,))
     if final:
         token = sum_of(final, (token,))
-    hops2 = sum2.send((token,))
     grad1 = []
     for i in seqs:
         grad, keep, send, token = attended_back(
@@ -1047,7 +1046,7 @@
         window += 1
         if window == 1:
             block_out, _ = gate(block_out, latest)
-        if window == 2:
+        if window in (2, 3) and not isinstance(hops2, jax.Array):
             hops2 = sum2.send(latest)
         if window == 3:
             side[0], _ = gate(side[0], latest)

time: 317 us -> 317 us (level)
  Pallas kernels: 133 us -> 140 us
  starting transfers between devices: 57.5 us -> 51.7 us
    pallas_call x17, Pallas kernels: 127 us -> 135 us  [call(): pl.pallas_call(body, out_shape=(*(pltpu.HBM(o.shape, o.dtype) if k in sto...]
    ppermute x8, starting transfers between devices: 18 us -> 11.2 us  [scatter(): right = lax.ppermute(right, 'dp', self.right)]
    ppermute x8, waiting for transfers between devices: 14.1 us -> 10.8 us  [scatter(): left = lax.ppermute(left, 'dp', self.left)]
    unnamed x108 -> x98, local copies, waits for them, and re-layouts: 13.7 us -> 12.9 us
  transfers between devices with their start and end apart: 57 -> 57, of which waited for: 15 -> 12; matrix products, arithmetic and copies ran while one was open for 17% -> 17% of each run, Pallas kernels for 38% -> 40%
where the time goes in v2:
time: 317 us; the launch traced here: 311 us
  Pallas kernels  140 us (44%)
  starting transfers between devices  51.7 us (16%)
  waiting for transfers between devices  50 us (16%)
  other arithmetic  33.6 us (11%)
  local copies, waits for them, and re-layouts  32.3 us (10%)
    pallas_call x17, Pallas kernels, call(): pl.pallas_call(body, out_shape=(*(pltpu.HBM(o.shape, o.dtype) if k in sto...  135 us
    ppermute x23, starting transfers between devices, swap(): return lax.ppermute(value, 'tensor', [(i, i ^ bit) for i in range(n)])  15.1 us
    unnamed x98, local copies, waits for them, and re-layouts  12.9 us
    ppermute x8, starting transfers between devices, scatter(): right = lax.ppermute(right, 'dp', self.right)  11.2 us
    ppermute x6, starting transfers between devices, gather(): from_left = lax.ppermute(from_left, 'dp', self.right)  11.1 us
    ppermute x8, waiting for transfers between devices, scatter(): left = lax.ppermute(left, 'dp', self.left)  10.8 us
    ppermute x23, waiting for transfers between devices, swap(): return lax.ppermute(value, 'tensor', [(i, i ^ bit) for i in range(n)])  10.7 us
    ppermute x2, waiting for transfers between devices, gather(): come.append(lax.ppermute(from_left[:rows // 2], 'dp', self.right))  9.42 us
  transfers between devices with their start and end apart: 57, of which 12 were waited for; matrix products, arithmetic and copies ran while one was open for 17% of the time, Pallas kernels for 40%

profile of v2, /device:TPU:0, one launch (start us, length us, event | category | flops | bytes accessed | tf_op | source)
XLA Modules:
  0.0 311.1 jit_solution(10119910499510697135)
XLA Ops:
  2.5 2.6 pack.1
  5.1 3.1 collective-permute-start
  10.7 4.7 %slice_bitcast_fusion = (bf16[1024,1024]{1,0:T(8,128)(2,1)}, bf16[1024,1024]{1,0:T(8,128)(2,1)}) fusion(bf16[2,1024,1024]{2,1,0:T(8,128)(2,1)} %param.23), kind=kLoop, calls=%fused_computation.18 | loop fusion | bytes 8388608 | tf_op jit(solution)/shard_map/squeeze | solution.py:881
  16.5 1.5 collective-permute-done.1.refs_2_
  18.1 1.6 collective-permute-start.2
  20.6 9.8 %embed.1 = (f32[1024,1024]{1,0:T(8,128)}, f32[1024,1024]{1,0:T(8,128)}, f32[8,128]{1,0:T(8,128)}) custom-call(s32[10]{0:T(128)S(1)} %get-tuple-element.142.refs_0_, bf16[2,1024,1024]{2,1,0:T(8,128)(2,1)} %refs_1_.3, s32[2,1024,1]{2,1,0:T(8,128)S(1)} %copy.30.refs_2_, f32[1,512]{1,0:T(1,128)S(1)} %multiply_exponential_fusion.refs_3_), custom_call_target="tpu_custom_call" | custom-call | flops 409600 | bytes 12298 | tf_op jit(solution)/shard_map/embed/pallas_call | solution.py:114
  30.5 1.6 collective-permute-start.4
  32.5 6.5 %collective-permute-done.4.refs_5_ = bf16[128,1408]{1,0:T(8,128)(2,1)S(1)} collective-permute-done((bf16[128,1408]{1,0:T(8,128)(2,1)S(1)}, bf16[128,1408]{1,0:T(8,128)(2,1)S(1)}, u32[]{:S(2)}, u32[]{:S(2)}) %collective-permute-start.4) | collective-permute-done | bytes 360480 | tf_op jit(solution)/shard_map/ppermute | solution.py:756
  39.1 1.6 collective-permute-start.8
  41.2 1.6 collective-permute-start.6
  44.6 9.4 %collective-permute-done.6.refs_7_ = bf16[64,1408]{1,0:T(8,128)(2,1)S(1)} collective-permute-done((bf16[64,1408]{1,0:T(8,128)(2,1)S(1)}, bf16[64,1408]{1,0:T(8,128)(2,1)S(1)}, u32[]{:S(2)}, u32[]{:S(2)}) %collective-permute-start.6) | collective-permute-done | bytes 180256 | tf_op jit(solution)/shard_map/ppermute | solution.py:762
  55.4 2.4 assemble.2.refs_4_.refs_3_
  57.8 1.6 collective-permute-start.12
  60.5 1.6 collective-permute-start.11
  62.8 3.4 %project.2 = (f32[512,1024]{1,0:T(8,128)}, bf16[1024,1024]{1,0:T(8,128)(2,1)}, bf16[1024,768]{1,0:T(8,128)(2,1)S(1)}, f32[1024,128]{1,0:T(8,128)S(1)}, f32[8,128]{1,0:T(8,128)S(1)}) custom-call(s32[10]{0:T(128)S(1)} %get-tuple-element.142.refs_0_, f32[1024,1024]{1,0:T(8,128)S(1)} %copy-done.11, f32[1,1024]{1,0:T(1,128)S(1)} %get-tuple-element.353.refs_2_, ...), custom_call_target="tpu_custom_call" | custom-call | flops 1572864 | bytes 13064 | tf_op jit(solution)/shard_map/project/pallas_call | solution.py:114
  66.3 9.0 %attend.2 = (bf16[1024,256]{1,0:T(8,128)(2,1)}, f32[1024,128]{1,0:T(8,128)S(1)}, f32[8,128]{1,0:T(8,128)S(1)}) custom-call(s32[10]{0:T(128)S(1)} %get-tuple-element.142.refs_0_, bf16[1024,768]{1,0:T(8,128)(2,1)S(1)} %get-tuple-element.153.refs_1_.refs_4_, f32[1024,128]{1,0:T(8,128)S(1)} %get-tuple-element.154.refs_2_, s32[1024,1]{1,0:T(8,128)S(1)} %copy-done.8, ...), custom_call_target="tpu_custom_call" | custom-call | flops 2097152 | bytes 3080 | tf_op jit(solution)/shard_map/attend/pallas_call | solution.py:114
  77.8 1.6 collective-permute-start.14
  81.0 2.2 copy-done.10
  83.2 3.4 %project.3 = (f32[512,1024]{1,0:T(8,128)}, bf16[1024,1024]{1,0:T(8,128)(2,1)}, bf16[1024,768]{1,0:T(8,128)(2,1)S(1)}, f32[1024,128]{1,0:T(8,128)S(1)}, f32[8,128]{1,0:T(8,128)S(1)}) custom-call(s32[10]{0:T(128)S(1)} %get-tuple-element.161.refs_0_, f32[1024,1024]{1,0:T(8,128)S(1)} %copy-done.10, f32[1,1024]{1,0:T(1,128)S(1)} %get-tuple-element.352.refs_2_, ...), custom_call_target="tpu_custom_call" | custom-call | flops 1572864 | bytes 13064 | tf_op jit(solution)/shard_map/project/pallas_call | solution.py:114
  86.6 8.1 %attend.3 = (bf16[1024,256]{1,0:T(8,128)(2,1)S(1)}, f32[1024,128]{1,0:T(8,128)S(1)}, f32[8,128]{1,0:T(8,128)S(1)}) custom-call(s32[10]{0:T(128)S(1)} %get-tuple-element.161.refs_0_, bf16[1024,768]{1,0:T(8,128)(2,1)S(1)} %get-tuple-element.164.refs_1_.refs_4_, f32[1024,128]{1,0:T(8,128)S(1)} %get-tuple-element.165.refs_2_, s32[1024,1]{1,0:T(8,128)S(1)} %copy-done.6, ...), custom_call_target="tpu_custom_call" | custom-call | flops 2097152 | bytes 3080 | tf_op jit(solution)/shard_map/attend/pallas_call | solution.py:114
  95.6 2.9 project_out.2
  98.6 1.6 collective-permute-start.17
  101.2 1.7 collective-permute-start.18
  104.5 8.5 %collective-permute-done.17.refs_2_ = bf16[1024,256]{1,0:T(8,128)(2,1)S(1)} collective-permute-done((bf16[1024,256]{1,0:T(8,128)(2,1)S(1)}, bf16[1024,256]{1,0:T(8,128)(2,1)S(1)}, u32[]{:S(2)}, u32[]{:S(2)}) %collective-permute-start.17) | collective-permute-done | bytes 524320 | tf_op jit(solution)/shard_map/ppermute | solution.py:810
  112.9 3.1 %project_out.3 = (bf16[512,1024]{1,0:T(8,128)(2,1)S(1)}, bf16[512,1024]{1,0:T(8,128)(2,1)}, f32[8,128]{1,0:T(8,128)S(1)}) custom-call(s32[10]{0:T(128)S(1)} %get-tuple-element.161.refs_0_, bf16[1024,256]{1,0:T(8,128)(2,1)S(1)} %get-tuple-element.176.refs_1_.refs_5_, bf16[1024,256]{1,0:T(8,128)(2,1)S(1)} %collective-permute-done.17.refs_2_, ...), custom_call_target="tpu_custom_call" | custom-call | flops 1048576 | bytes 4096 | tf_op jit(solution)/shard_map/project_out/pallas_call | solution.py:114
  117.1 3.3 %middle.2 = (f32[512,1024]{1,0:T(8,128)}, bf16[512,1024]{1,0:T(8,128)(2,1)}, f32[512,128]{1,0:T(8,128)S(1)}, f32[8,128]{1,0:T(8,128)S(1)}) custom-call(s32[10]{0:T(128)S(1)} %get-tuple-element.142.refs_0_, f32[512,1024]{1,0:T(8,128)S(1)} %copy-done.16, bf16[512,1024]{1,0:T(8,128)(2,1)S(1)} %get-tuple-element.174.refs_2_, ...), custom_call_target="tpu_custom_call" | custom-call | flops 10240 | bytes 7428 | tf_op jit(solution)/shard_map/middle/pallas_call | solution.py:114
  121.1 3.0 assemble.3.refs_4_
  124.2 3.1 %middle.3 = (f32[512,1024]{1,0:T(8,128)}, bf16[512,1024]{1,0:T(8,128)(2,1)S(1)}, f32[512,128]{1,0:T(8,128)S(1)}, f32[8,128]{1,0:T(8,128)S(1)}) custom-call(s32[10]{0:T(128)S(1)} %get-tuple-element.161.refs_0_, f32[512,1024]{1,0:T(8,128)S(1)} %copy-done.17, bf16[512,1024]{1,0:T(8,128)(2,1)S(1)} %copy-done.19, ...), custom_call_target="tpu_custom_call" | custom-call | flops 10240 | bytes 7428 | tf_op jit(solution)/shard_map/middle/pallas_call | solution.py:114
  128.1 9.9 %hidden_start.1 = (bf16[512,1024]{1,0:T(8,128)(2,1)S(1)}, bf16[512,1024]{1,0:T(8,128)(2,1)S(1)}, bf16[1024,1024]{1,0:T(8,128)(2,1)S(1)}, bf16[1024,1024]{1,0:T(8,128)(2,1)S(1)}, f32[8,128]{1,0:T(8,128)}) custom-call(s32[10]{0:T(128)S(1)} %get-tuple-element.142.refs_0_, bf16[512,1024]{1,0:T(8,128)(2,1)} %get-tuple-element.181.refs_1_.refs_3_, ...), custom_call_target="tpu_custom_call" | custom-call | flops 6291456 | bytes 14336 | tf_op jit(solution)/shard_map/hidden_start/pallas_call | solution.py:114
  138.6 2.1 collective-permute-done.22
  141.1 1.6 collective-permute-start.27
  142.7 10.6 %hidden_end.1 = (bf16[1024,2048]{1,0:T(8,128)(2,1)}, bf16[2,1024,256]{2,1,0:T(8,128)(2,1)}, bf16[2,1024,256]{2,1,0:T(8,128)(2,1)}, f32[8,128]{1,0:T(8,128)S(1)}) custom-call(s32[10]{0:T(128)S(1)} %get-tuple-element.142.refs_0_, bf16[512,1024]{1,0:T(8,128)(2,1)} %get-tuple-element.181.refs_1_.refs_3_, bf16[512,1024]{1,0:T(8,128)(2,1)} %collective-permute-done.20.refs_2_, ...), custom_call_target="tpu_custom_call" | custom-call | flops 6291456 | bytes 20480 | tf_op jit(solution)/shard_map/hidden_end/pallas_call | solution.py:114
  153.3 15.8 %hidden_layer.1 = (bf16[512,1024]{1,0:T(8,128)(2,1)S(1)}, bf16[512,1024]{1,0:T(8,128)(2,1)S(1)}, bf16[1024,2048]{1,0:T(8,128)(2,1)}, bf16[2,1024,256]{2,1,0:T(8,...) custom-call(s32[10]{0:T(128)S(1)} %get-tuple-element.161.refs_0_, ...), custom_call_target="tpu_custom_call" | custom-call | flops 12582912 | bytes 18432 | tf_op jit(solution)/shard_map/hidden_layer/pallas_call | solution.py:114
  169.3 3.8 %middle_back.2 = (bf16[512,1024]{1,0:T(8,128)(2,1)}, f32[1,1024]{1,0:T(1,128)S(1)}, f32[8,128]{1,0:T(8,128)}) custom-call(s32[10]{0:T(128)S(1)} %get-tuple-element.142.refs_0_, bf16[512,1024]{1,0:T(8,128)(2,1)S(1)} %add_convert_fusion.1.refs_8_.refs_1_, bf16[512,1024]{1,0:T(8,128)(2,1)S(1)} %collective-permute-done.27.refs_2_, ...), custom_call_target="tpu_custom_call" | custom-call | flops 15360 | bytes 6408 | tf_op jit(solution)/shard_map/middle_back/pallas_call | solution.py:114
  173.6 1.4 add_convert_fusion.refs_12_.refs_1_
  176.0 1.3 add_convert_fusion.16
  177.3 1.6 collective-permute-start.47
  179.7 21.5 %attend_back.2 = (bf16[1024,1152]{1,0:T(8,128)(2,1)}, bf16[2,1024,256]{2,1,0:T(8,128)(2,1)}, bf16[2,1024,256]{2,1,0:T(8,128)(2,1)}, f32[8,128]{1,0:T(8,128)S(1)}) custom-call(s32[10]{0:T(128)S(1)} %get-tuple-element.142.refs_0_, bf16[512,1024]{1,0:T(8,128)(2,1)} %get-tuple-element.216.refs_1_, bf16[512,1024]{1,0:T(8,128)(2,1)} %collective-permute-done.28.refs_2_, ...), custom_call_target="tpu_custom_call" | custom-call | flops 9437184 | bytes 13840 | tf_op jit(solution)/shard_map/attend_back/pallas_call | solution.py:114
  201.3 3.2 %middle_back.3 = (bf16[512,1024]{1,0:T(8,128)(2,1)S(1)}, f32[1,1024]{1,0:T(1,128)S(1)}, f32[8,128]{1,0:T(8,128)S(1)}) custom-call(s32[10]{0:T(128)S(1)} %get-tuple-element.161.refs_0_, bf16[512,1024]{1,0:T(8,128)(2,1)} %add_convert_fusion.refs_12_.refs_1_, bf16[512,1024]{1,0:T(8,128)(2,1)} %collective-permute-done.26.refs_2_, ...), custom_call_target="tpu_custom_call" | custom-call | flops 15360 | bytes 6408 | tf_op jit(solution)/shard_map/middle_back/pallas_call | solution.py:114
  205.1 1.3 fusion.18
  207.5 1.5 collective-permute-start.31
  210.8 1.9 add_convert_fusion.13
  216.9 1.6 collective-permute-start.49
  218.5 21.3 %attend_back.3 = (bf16[1024,1152]{1,0:T(8,128)(2,1)}, bf16[2,1024,256]{2,1,0:T(8,128)(2,1)}, bf16[2,1024,256]{2,1,0:T(8,128)(2,1)}, f32[8,128]{1,0:T(8,128)}) custom-call(s32[10]{0:T(128)S(1)} %get-tuple-element.161.refs_0_, bf16[512,1024]{1,0:T(8,128)(2,1)S(1)} %get-tuple-element.229.refs_1_, bf16[512,1024]{1,0:T(8,128)(2,1)S(1)} %collective-permute-done.32.refs_2_, ...), custom_call_target="tpu_custom_call" | custom-call | flops 9437184 | bytes 13840 | tf_op jit(solution)/shard_map/attend_back/pallas_call | solution.py:114
  242.6 1.5 collective-permute-start.36
  245.4 1.7 collective-permute-start.33
  248.2 2.5 add_convert_fusion.4
  250.7 1.6 collective-permute-start.51
  254.9 1.6 collective-permute-start.38
  257.7 2.6 fusion.4
  260.3 10.2 %collective-permute-done.39 = bf16[128,1152]{1,0:T(8,128)(2,1)S(1)} collective-permute-done((bf16[128,1152]{1,0:T(8,128)(2,1)S(1)}, bf16[128,1152]{1,0:T(8,128)(2,1)S(1)}, u32[]{:S(2)}, u32[]{:S(2)}) %collective-permute-start.39) | collective-permute-done | bytes 294944 | tf_op jit(solution)/shard_map/ppermute | solution.py:788
  271.3 1.4 collective-permute-start.41
  272.8 2.0 add_convert_fusion.2
  275.5 1.4 collective-permute-start.54
  276.9 3.6 %collective-permute-done.40 = bf16[128,1152]{1,0:T(8,128)(2,1)S(1)} collective-permute-done((bf16[128,1152]{1,0:T(8,128)(2,1)S(1)}, bf16[128,1152]{1,0:T(8,128)(2,1)S(1)}, u32[]{:S(2)}, u32[]{:S(2)}) %collective-permute-start.40) | collective-permute-done | bytes 294944 | tf_op jit(solution)/shard_map/ppermute | solution.py:787
  282.1 1.8 collective-permute-start.45
  286.2 1.3 collective-permute-start.43
  287.6 3.8 %collective-permute-done.53 = bf16[128,2048]{1,0:T(8,128)(2,1)S(1)} collective-permute-done((bf16[128,2048]{1,0:T(8,128)(2,1)S(1)}, bf16[128,2048]{1,0:T(8,128)(2,1)S(1)}, u32[]{:S(2)}, u32[]{:S(2)}) %collective-permute-start.53) | collective-permute-done | bytes 524320 | tf_op jit(solution)/shard_map/ppermute | solution.py:787
  292.4 1.5 convert_add_fusion.4
  295.0 2.0 copy.36
  297.0 1.4 convert_add_fusion.7
  302.6 1.7 maximum_multiply_fusion
  304.3 1.7 collective-permute-done.56
  308.9 2.0 fusion.1
  (259 shorter events, 56.6 us)
Async XLA Ops:
  5.1 35.5 %copy-start.22 = (bf16[128,2048]{1,0:T(8,128)(2,1)}, bf16[128,2048]{1,0:T(8,128)(2,1)S(1)}, u32[]{:S(2)}) copy-start(bf16[128,2048]{1,0:T(8,128)(2,1)S(1)} %get-tuple-element.159.refs_0_) | copy-start | bytes 1572868
  5.1 11.4 %collective-permute-start = (bf16[128,1408]{1,0:T(8,128)(2,1)S(1)}, bf16[128,1408]{1,0:T(8,128)(2,1)S(1)}, u32[]{:S(2)}, u32[]{:S(2)}) collective-permute-start(bf16[128,1408]{1,0:T(8,128)(2,1)S(1)} %get-tuple-element.141.refs_0_), channel_id=1, source_target_pairs={{0,8},{8,16},{16,24},{24,28},{28,20},{20,12},{12,4},{4,0},{1,9},{9... | collective-permute-start | bytes 1081352 | tf_op jit(solution)/shard_map/ppermute | solution.py:756
  8.2 9.9 %collective-permute-start.1 = (bf16[128,1408]{1,0:T(8,128)(2,1)S(1)}, bf16[128,1408]{1,0:T(8,128)(2,1)S(1)}, u32[]{:S(2)}, u32[]{:S(2)}) collective-permute-start(bf16[128,1408]{1,0:T(8,128)(2,1)S(1)} %get-tuple-element.141.refs_0_), channel_id=1, source_target_pairs={{8,0},{16,8},{24,16},{28,24},{20,28},{12,20},{4,12},{0,4},{9,1},{1... | collective-permute-start | bytes 1081352 | tf_op jit(solution)/shard_map/ppermute | solution.py:757
  18.1 12.3 %collective-permute-start.2 = (bf16[128,1408]{1,0:T(8,128)(2,1)S(1)}, bf16[128,1408]{1,0:T(8,128)(2,1)S(1)}, u32[]{:S(2)}, u32[]{:S(2)}) collective-permute-start(bf16[128,1408]{1,0:T(8,128)(2,1)S(1)} %collective-permute-done.refs_1_), channel_id=1, source_target_pairs={{0,8},{8,16},{16,24},{24,28},{28,20},{20,12},{12,4},{4,0},{1,9},{9... | collective-permute-start | bytes 1081352 | tf_op jit(solution)/shard_map/ppermute | solution.py:756
  19.7 10.8 %collective-permute-start.3 = (bf16[128,1408]{1,0:T(8,128)(2,1)S(1)}, bf16[128,1408]{1,0:T(8,128)(2,1)S(1)}, u32[]{:S(2)}, u32[]{:S(2)}) collective-permute-start(bf16[128,1408]{1,0:T(8,128)(2,1)S(1)} %collective-permute-done.1.refs_2_), channel_id=1, source_target_pairs={{8,0},{16,8},{24,16},{28,24},{20,28},{12,20},{4,12},{0,4},{9,1},{1... | collective-permute-start | bytes 1081352 | tf_op jit(solution)/shard_map/ppermute | solution.py:757
  30.4 23.6 %copy-start.43 = (bf16[128,1408]{1,0:T(8,128)(2,1)}, bf16[128,1408]{1,0:T(8,128)(2,1)S(1)}, u32[]{:S(2)}) copy-start(bf16[128,1408]{1,0:T(8,128)(2,1)S(1)} %collective-permute-done.2.refs_3_) | copy-start | bytes 1081348
  30.4 23.6 %copy-start.44 = (bf16[128,1408]{1,0:T(8,128)(2,1)}, bf16[128,1408]{1,0:T(8,128)(2,1)S(1)}, u32[]{:S(2)}) copy-start(bf16[128,1408]{1,0:T(8,128)(2,1)S(1)} %collective-permute-done.3.refs_4_) | copy-start | bytes 1081348
  30.5 8.6 %collective-permute-start.4 = (bf16[128,1408]{1,0:T(8,128)(2,1)S(1)}, bf16[128,1408]{1,0:T(8,128)(2,1)S(1)}, u32[]{:S(2)}, u32[]{:S(2)}) collective-permute-start(bf16[128,1408]{1,0:T(8,128)(2,1)S(1)} %collective-permute-done.2.refs_3_), channel_id=1, source_target_pairs={{0,8},{8,16},{16,24},{24,28},{28,20},{20,12},{12,4},{4,0},{1,9},{9... | collective-permute-start | bytes 1081352 | tf_op jit(solution)/shard_map/ppermute | solution.py:756
  32.1 9.0 %collective-permute-start.5 = (bf16[128,1408]{1,0:T(8,128)(2,1)S(1)}, bf16[128,1408]{1,0:T(8,128)(2,1)S(1)}, u32[]{:S(2)}, u32[]{:S(2)}) collective-permute-start(bf16[128,1408]{1,0:T(8,128)(2,1)S(1)} %collective-permute-done.3.refs_4_), channel_id=1, source_target_pairs={{8,0},{16,8},{24,16},{28,24},{20,28},{12,20},{4,12},{0,4},{9,1},{1... | collective-permute-start | bytes 1081352 | tf_op jit(solution)/shard_map/ppermute | solution.py:757
  39.1 18.7 %collective-permute-start.8 = (bf16[128,2048]{1,0:T(8,128)(2,1)S(1)}, bf16[128,2048]{1,0:T(8,128)(2,1)}, u32[]{:S(2)}, u32[]{:S(2)}) collective-permute-start(bf16[128,2048]{1,0:T(8,128)(2,1)S(1)} %get-tuple-element.159.refs_0_), channel_id=1, source_target_pairs={{0,8},{8,16},{16,24},{24,28},{28,20},{20,12},{12,4},{4,0},{1,9},{9... | collective-permute-start | bytes 1572872 | tf_op jit(solution)/shard_map/ppermute | solution.py:756
  40.7 17.1 %collective-permute-start.9 = (bf16[128,2048]{1,0:T(8,128)(2,1)S(1)}, bf16[128,2048]{1,0:T(8,128)(2,1)}, u32[]{:S(2)}, u32[]{:S(2)}) collective-permute-start(bf16[128,2048]{1,0:T(8,128)(2,1)S(1)} %get-tuple-element.159.refs_0_), channel_id=1, source_target_pairs={{8,0},{16,8},{24,16},{28,24},{20,28},{12,20},{4,12},{0,4},{9,1},{1... | collective-permute-start | bytes 1572872 | tf_op jit(solution)/shard_map/ppermute | solution.py:757
  41.2 12.8 %collective-permute-start.6 = (bf16[64,1408]{1,0:T(8,128)(2,1)S(1)}, bf16[64,1408]{1,0:T(8,128)(2,1)S(1)}, u32[]{:S(2)}, u32[]{:S(2)}) collective-permute-start(bf16[64,1408]{1,0:T(8,128)(2,1)S(1)} %slice.139), channel_id=1, source_target_pairs={{0,8},{8,16},{16,24},{24,28},{28,20},{20,12},{12,4},{4,0},{1,9},{9... | collective-permute-start | bytes 540680 | tf_op jit(solution)/shard_map/ppermute | solution.py:762
  42.8 12.6 %collective-permute-start.7 = (bf16[64,1408]{1,0:T(8,128)(2,1)S(1)}, bf16[64,1408]{1,0:T(8,128)(2,1)}, u32[]{:S(2)}, u32[]{:S(2)}) collective-permute-start(bf16[64,1408]{1,0:T(8,128)(2,1)S(1)} %slice.140), channel_id=1, source_target_pairs={{8,0},{16,8},{24,16},{28,24},{20,28},{12,20},{4,12},{0,4},{9,1},{1... | collective-permute-start | bytes 540680 | tf_op jit(solution)/shard_map/ppermute | solution.py:763
  57.8 160.7 %copy-start = (bf16[1024,1408]{1,0:T(8,128)(2,1)}, bf16[1024,1408]{1,0:T(8,128)(2,1)S(1)}, u32[]{:S(2)}) copy-start(bf16[1024,1408]{1,0:T(8,128)(2,1)S(1)} %assemble.2.refs_4_.refs_3_) | copy-start | bytes 8650756
  57.8 19.9 %collective-permute-start.12 = (bf16[128,2048]{1,0:T(8,128)(2,1)}, bf16[128,2048]{1,0:T(8,128)(2,1)}, u32[]{:S(2)}, u32[]{:S(2)}) collective-permute-start(bf16[128,2048]{1,0:T(8,128)(2,1)} %collective-permute-done.8.refs_6_.refs_1_), channel_id=1, source_target_pairs={{0,8},{8,16},{16,24},{24,28},{28,20},{20,12},{12,4},{4,0},{1,9},{9... | collective-permute-start | bytes 1572872 | tf_op jit(solution)/shard_map/ppermute | solution.py:756
  59.4 18.3 %collective-permute-start.13 = (bf16[128,2048]{1,0:T(8,128)(2,1)}, bf16[128,2048]{1,0:T(8,128)(2,1)}, u32[]{:S(2)}, u32[]{:S(2)}) collective-permute-start(bf16[128,2048]{1,0:T(8,128)(2,1)} %collective-permute-done.9.refs_7_.refs_2_), channel_id=1, source_target_pairs={{8,0},{16,8},{24,16},{28,24},{20,28},{12,20},{4,12},{0,4},{9,1},{1... | collective-permute-start | bytes 1572872 | tf_op jit(solution)/shard_map/ppermute | solution.py:757
  60.5 20.5 %collective-permute-start.11 = (bf16[1024,256]{1,0:T(8,128)(2,1)S(1)}, bf16[1024,256]{1,0:T(8,128)(2,1)}, u32[]{:S(2)}, u32[]{:S(2)}) collective-permute-start(bf16[1024,256]{1,0:T(8,128)(2,1)S(1)} %get-tuple-element.332.refs_3_), channel_id=1, source_target_pairs={{0,2},{1,3},{2,0},{3,1},{4,6},{5,7},{6,4},{7,5},{8,10},{9,11},{10,... | collective-permute-start | bytes 1572872 | tf_op jit(solution)/shard_map/ppermute | solution.py:810
  77.2 18.3 %collective-permute-start.10 = (bf16[1024,256]{1,0:T(8,128)(2,1)}, bf16[1024,256]{1,0:T(8,128)(2,1)}, u32[]{:S(2)}, u32[]{:S(2)}) collective-permute-start(bf16[1024,256]{1,0:T(8,128)(2,1)} %get-tuple-element.160.refs_1_.refs_5_), channel_id=1, source_target_pairs={{0,2},{1,3},{2,0},{3,1},{4,6},{5,7},{6,4},{7,5},{8,10},{9,11},{10,... | collective-permute-start | bytes 1572872 | tf_op jit(solution)/shard_map/ppermute | solution.py:810
  77.8 17.8 %collective-permute-start.14 = (bf16[128,2048]{1,0:T(8,128)(2,1)}, bf16[128,2048]{1,0:T(8,128)(2,1)}, u32[]{:S(2)}, u32[]{:S(2)}) collective-permute-start(bf16[128,2048]{1,0:T(8,128)(2,1)} %collective-permute-done.12.refs_6_.refs_3_), channel_id=1, source_target_pairs={{0,8},{8,16},{16,24},{24,28},{28,20},{20,12},{12,4},{4,0},{1,9},{9... | collective-permute-start | bytes 1572872 | tf_op jit(solution)/shard_map/ppermute | solution.py:756
  79.3 16.2 %collective-permute-start.15 = (bf16[128,2048]{1,0:T(8,128)(2,1)}, bf16[128,2048]{1,0:T(8,128)(2,1)}, u32[]{:S(2)}, u32[]{:S(2)}) collective-permute-start(bf16[128,2048]{1,0:T(8,128)(2,1)} %collective-permute-done.13.refs_7_.refs_4_), channel_id=1, source_target_pairs={{8,0},{16,8},{24,16},{28,24},{20,28},{12,20},{4,12},{0,4},{9,1},{1... | collective-permute-start | bytes 1572872 | tf_op jit(solution)/shard_map/ppermute | solution.py:757
  98.5 18.6 %collective-permute-start.16 = (bf16[512,1024]{1,0:T(8,128)(2,1)S(1)}, bf16[512,1024]{1,0:T(8,128)(2,1)S(1)}, u32[]{:S(2)}, u32[]{:S(2)}) collective-permute-start(bf16[512,1024]{1,0:T(8,128)(2,1)S(1)} %get-tuple-element.175), channel_id=1, source_target_pairs={{0,1},{1,0},{2,3},{3,2},{4,5},{5,4},{6,7},{7,6},{8,9},{9,8},{10,11... | collective-permute-start | bytes 3145736 | tf_op jit(solution)/shard_map/ppermute | solution.py:810
  98.6 14.3 %collective-permute-start.17 = (bf16[1024,256]{1,0:T(8,128)(2,1)S(1)}, bf16[1024,256]{1,0:T(8,128)(2,1)S(1)}, u32[]{:S(2)}, u32[]{:S(2)}) collective-permute-start(bf16[1024,256]{1,0:T(8,128)(2,1)S(1)} %get-tuple-element.176.refs_1_.refs_5_), channel_id=1, source_target_pairs={{0,2},{1,3},{2,0},{3,1},{4,6},{5,7},{6,4},{7,5},{8,10},{9,11},{10,... | collective-permute-start | bytes 1572872 | tf_op jit(solution)/shard_map/ppermute | solution.py:810
  101.2 15.9 %collective-permute-start.18 = (bf16[64,2048]{1,0:T(8,128)(2,1)S(1)}, bf16[64,2048]{1,0:T(8,128)(2,1)S(1)}, u32[]{:S(2)}, u32[]{:S(2)}) collective-permute-start(bf16[64,2048]{1,0:T(8,128)(2,1)S(1)} %slice.147), channel_id=1, source_target_pairs={{0,8},{8,16},{16,24},{24,28},{28,20},{20,12},{12,4},{4,0},{1,9},{9... | collective-permute-start | bytes 786440 | tf_op jit(solution)/shard_map/ppermute | solution.py:762
  103.8 13.3 %collective-permute-start.19 = (bf16[64,2048]{1,0:T(8,128)(2,1)S(1)}, bf16[64,2048]{1,0:T(8,128)(2,1)S(1)}, u32[]{:S(2)}, u32[]{:S(2)}) collective-permute-start(bf16[64,2048]{1,0:T(8,128)(2,1)S(1)} %slice.148), channel_id=1, source_target_pairs={{8,0},{16,8},{24,16},{28,24},{20,28},{12,20},{4,12},{0,4},{9,1},{1... | collective-permute-start | bytes 786440 | tf_op jit(solution)/shard_map/ppermute | solution.py:763
  117.1 7.1 %collective-permute-start.21 = (bf16[512,1024]{1,0:T(8,128)(2,1)}, bf16[512,1024]{1,0:T(8,128)(2,1)}, u32[]{:S(2)}, u32[]{:S(2)}) collective-permute-start(bf16[512,1024]{1,0:T(8,128)(2,1)} %get-tuple-element.194), channel_id=1, source_target_pairs={{0,1},{1,0},{2,3},{3,2},{4,5},{5,4},{6,7},{7,6},{8,9},{9,8},{10,11... | collective-permute-start | bytes 3145736 | tf_op jit(solution)/shard_map/ppermute | solution.py:810
  120.5 7.6 %collective-permute-start.20 = (bf16[512,1024]{1,0:T(8,128)(2,1)}, bf16[512,1024]{1,0:T(8,128)(2,1)}, u32[]{:S(2)}, u32[]{:S(2)}) collective-permute-start(bf16[512,1024]{1,0:T(8,128)(2,1)} %get-tuple-element.181.refs_1_.refs_3_), channel_id=1, source_target_pairs={{0,1},{1,0},{2,3},{3,2},{4,5},{5,4},{6,7},{7,6},{8,9},{9,8},{10,11... | collective-permute-start | bytes 3145736 | tf_op jit(solution)/shard_map/ppermute | solution.py:810
  128.1 25.2 %copy-start.12 = (bf16[512,1024]{1,0:T(8,128)(2,1)}, bf16[512,1024]{1,0:T(8,128)(2,1)S(1)}, u32[]{:S(2)}) copy-start(bf16[512,1024]{1,0:T(8,128)(2,1)S(1)} %get-tuple-element.205.refs_1_.refs_3_) | copy-start | bytes 3145732
  138.0 2.7 collective-permute-start.22
  138.1 15.2 %collective-permute-start.24 = (bf16[512,1024]{1,0:T(8,128)(2,1)S(1)}, bf16[512,1024]{1,0:T(8,128)(2,1)S(1)}, u32[]{:S(2)}, u32[]{:S(2)}) collective-permute-start(bf16[512,1024]{1,0:T(8,128)(2,1)S(1)} %get-tuple-element.205.refs_1_.refs_3_), channel_id=1, source_target_pairs={{0,1},{1,0},{2,3},{3,2},{4,5},{5,4},{6,7},{7,6},{8,9},{9,8},{10,11... | collective-permute-start | bytes 3145736 | tf_op jit(solution)/shard_map/ppermute | solution.py:810
  141.1 28.1 %collective-permute-start.27 = (bf16[512,1024]{1,0:T(8,128)(2,1)S(1)}, bf16[512,1024]{1,0:T(8,128)(2,1)S(1)}, u32[]{:S(2)}, u32[]{:S(2)}) collective-permute-start(bf16[512,1024]{1,0:T(8,128)(2,1)S(1)} %add_convert_fusion.1.refs_8_.refs_1_), channel_id=1, source_target_pairs={{0,2},{1,3},{2,0},{3,1},{4,6},{5,7},{6,4},{7,5},{8,10},{9,11},{10,... | collective-permute-start | bytes 3145736 | tf_op jit(solution)/shard_map/ppermute | solution.py:810
  169.2 4.4 %collective-permute-start.25 = (bf16[512,1024]{1,0:T(8,128)(2,1)S(1)}, bf16[512,1024]{1,0:T(8,128)(2,1)S(1)}, u32[]{:S(2)}, u32[]{:S(2)}) collective-permute-start(bf16[512,1024]{1,0:T(8,128)(2,1)S(1)} %get-tuple-element.210), channel_id=1, source_target_pairs={{0,1},{1,0},{2,3},{3,2},{4,5},{5,4},{6,7},{7,6},{8,9},{9,8},{10,11... | collective-permute-start | bytes 3145736 | tf_op jit(solution)/shard_map/ppermute | solution.py:810
  173.0 5.9 %collective-permute-start.28 = (bf16[512,1024]{1,0:T(8,128)(2,1)}, bf16[512,1024]{1,0:T(8,128)(2,1)}, u32[]{:S(2)}, u32[]{:S(2)}) collective-permute-start(bf16[512,1024]{1,0:T(8,128)(2,1)} %get-tuple-element.216.refs_1_), channel_id=1, source_target_pairs={{0,1},{1,0},{2,3},{3,2},{4,5},{5,4},{6,7},{7,6},{8,9},{9,8},{10,11... | collective-permute-start | bytes 3145736 | tf_op jit(solution)/shard_map/ppermute | solution.py:810
  175.0 26.2 %collective-permute-start.26 = (bf16[512,1024]{1,0:T(8,128)(2,1)}, bf16[512,1024]{1,0:T(8,128)(2,1)}, u32[]{:S(2)}, u32[]{:S(2)}) collective-permute-start(bf16[512,1024]{1,0:T(8,128)(2,1)} %add_convert_fusion.refs_12_.refs_1_), channel_id=1, source_target_pairs={{0,2},{1,3},{2,0},{3,1},{4,6},{5,7},{6,4},{7,5},{8,10},{9,11},{10,... | collective-permute-start | bytes 3145736 | tf_op jit(solution)/shard_map/ppermute | solution.py:810
  175.5 29.1 %collective-permute-start.30 = (bf16[2,1024,256]{2,1,0:T(8,128)(2,1)}, bf16[2,1024,256]{2,1,0:T(8,128)(2,1)}, u32[]{:S(2)}, u32[]{:S(2)}) collective-permute-start(bf16[2,1024,256]{2,1,0:T(8,128)(2,1)} %get-tuple-element.225), channel_id=1, source_target_pairs={{0,1},{1,0},{2,3},{3,2},{4,5},{5,4},{6,7},{7,6},{8,9},{9,8},{10,11... | collective-permute-start | bytes 3145736 | tf_op jit(solution)/shard_map/ppermute | solution.py:810
  175.5 32.0 %collective-permute-start.23 = (bf16[2,1024,256]{2,1,0:T(8,128)(2,1)}, bf16[2,1024,256]{2,1,0:T(8,128)(2,1)S(1)}, u32[]{:S(2)}, u32[]{:S(2)}) collective-permute-start(bf16[2,1024,256]{2,1,0:T(8,128)(2,1)} %get-tuple-element.204), channel_id=1, source_target_pairs={{0,1},{1,0},{2,3},{3,2},{4,5},{5,4},{6,7},{7,6},{8,9},{9,8},{10,11... | collective-permute-start | bytes 3145736 | tf_op jit(solution)/shard_map/ppermute | solution.py:810
  177.3 32.9 %collective-permute-start.47 = (bf16[64,2048]{1,0:T(8,128)(2,1)S(1)}, bf16[64,2048]{1,0:T(8,128)(2,1)S(1)}, u32[]{:S(2)}, u32[]{:S(2)}) collective-permute-start(bf16[64,2048]{1,0:T(8,128)(2,1)S(1)} %get-tuple-element.319), channel_id=1, source_target_pairs={{0,8},{8,16},{16,24},{24,28},{28,20},{20,12},{12,4},{4,0},{1,9},{9... | collective-permute-start | bytes 786440 | tf_op jit(solution)/shard_map/ppermute | solution.py:787
  179.0 31.8 %collective-permute-start.48 = (bf16[64,2048]{1,0:T(8,128)(2,1)S(1)}, bf16[64,2048]{1,0:T(8,128)(2,1)S(1)}, u32[]{:S(2)}, u32[]{:S(2)}) collective-permute-start(bf16[64,2048]{1,0:T(8,128)(2,1)S(1)} %get-tuple-element.318), channel_id=1, source_target_pairs={{8,0},{16,8},{24,16},{28,24},{20,28},{12,20},{4,12},{0,4},{9,1},{1... | collective-permute-start | bytes 786440 | tf_op jit(solution)/shard_map/ppermute | solution.py:788
  179.7 21.6 %copy-start.13 = (bf16[512,1024]{1,0:T(8,128)(2,1)S(1)}, bf16[512,1024]{1,0:T(8,128)(2,1)}, u32[]{:S(2)}) copy-start(bf16[512,1024]{1,0:T(8,128)(2,1)} %copy-done.12) | copy-start | bytes 3145732
  179.7 21.6 %copy-start.27 = (f32[512,128]{1,0:T(8,128)S(1)}, f32[512,128]{1,0:T(8,128)}, u32[]{:S(2)}) copy-start(f32[512,128]{1,0:T(8,128)} %copy-done.26) | copy-start | bytes 786436
  204.5 12.4 %collective-permute-start.32 = (bf16[512,1024]{1,0:T(8,128)(2,1)S(1)}, bf16[512,1024]{1,0:T(8,128)(2,1)S(1)}, u32[]{:S(2)}, u32[]{:S(2)}) collective-permute-start(bf16[512,1024]{1,0:T(8,128)(2,1)S(1)} %get-tuple-element.229.refs_1_), channel_id=1, source_target_pairs={{0,1},{1,0},{2,3},{3,2},{4,5},{5,4},{6,7},{7,6},{8,9},{9,8},{10,11... | collective-permute-start | bytes 3145736 | tf_op jit(solution)/shard_map/ppermute | solution.py:810
  204.6 35.2 %collective-permute-start.35 = (bf16[2,1024,256]{2,1,0:T(8,128)(2,1)S(1)}, bf16[2,1024,256]{2,1,0:T(8,128)(2,1)S(1)}, u32[]{:S(2)}, u32[]{:S(2)}) collective-permute-start(bf16[2,1024,256]{2,1,0:T(8,128)(2,1)S(1)} %copy-done.47), channel_id=1, source_target_pairs={{0,1},{1,0},{2,3},{3,2},{4,5},{5,4},{6,7},{7,6},{8,9},{9,8},{10,11... | collective-permute-start | bytes 3145736 | tf_op jit(solution)/shard_map/ppermute | solution.py:810
  207.5 36.7 %collective-permute-start.31 = (bf16[1,1024,256]{2,1,0:T(8,128)(2,1)}, bf16[1,1024,256]{2,1,0:T(8,128)(2,1)}, u32[]{:S(2)}, u32[]{:S(2)}) collective-permute-start(bf16[1,1024,256]{2,1,0:T(8,128)(2,1)} %dynamic-slice_convert_fusion.2), channel_id=1, source_target_pairs={{0,2},{1,3},{2,0},{3,1},{4,6},{5,7},{6,4},{7,5},{8,10},{9,11},{10,... | collective-permute-start | bytes 1572872 | tf_op jit(solution)/shard_map/ppermute | solution.py:810
  210.2 33.9 %collective-permute-start.29 = (bf16[1,1024,256]{2,1,0:T(8,128)(2,1)}, bf16[1,1024,256]{2,1,0:T(8,128)(2,1)}, u32[]{:S(2)}, u32[]{:S(2)}) collective-permute-start(bf16[1,1024,256]{2,1,0:T(8,128)(2,1)} %dynamic-slice_convert_fusion.3), channel_id=1, source_target_pairs={{0,2},{1,3},{2,0},{3,1},{4,6},{5,7},{6,4},{7,5},{8,10},{9,11},{10,... | collective-permute-start | bytes 1572872 | tf_op jit(solution)/shard_map/ppermute | solution.py:810
  213.5 34.0 %collective-permute-start.50 = (bf16[128,2048]{1,0:T(8,128)(2,1)}, bf16[128,2048]{1,0:T(8,128)(2,1)}, u32[]{:S(2)}, u32[]{:S(2)}) collective-permute-start(bf16[128,2048]{1,0:T(8,128)(2,1)} %pad_maximum_fusion.1), channel_id=1, source_target_pairs={{8,0},{16,8},{24,16},{28,24},{20,28},{12,20},{4,12},{0,4},{9,1},{1... | collective-permute-start | bytes 1572872 | tf_op jit(solution)/shard_map/ppermute | solution.py:788
  216.9 31.3 %collective-permute-start.49 = (bf16[128,2048]{1,0:T(8,128)(2,1)}, bf16[128,2048]{1,0:T(8,128)(2,1)}, u32[]{:S(2)}, u32[]{:S(2)}) collective-permute-start(bf16[128,2048]{1,0:T(8,128)(2,1)} %pad_maximum_fusion), channel_id=1, source_target_pairs={{0,8},{8,16},{16,24},{24,28},{28,20},{20,12},{12,4},{4,0},{1,9},{9... | collective-permute-start | bytes 1572872 | tf_op jit(solution)/shard_map/ppermute | solution.py:787
  242.6 11.4 %collective-permute-start.36 = (bf16[1,512,256]{2,1,0:T(8,128)(2,1)S(1)}, bf16[1,512,256]{2,1,0:T(8,128)(2,1)S(1)}, u32[]{:S(2)}, u32[]{:S(2)}) collective-permute-start(bf16[1,512,256]{2,1,0:T(8,128)(2,1)S(1)} %get-tuple-element.351), channel_id=1, source_target_pairs={{0,2},{1,3},{2,0},{3,1},{4,6},{5,7},{6,4},{7,5},{8,10},{9,11},{10,... | collective-permute-start | bytes 786440 | tf_op jit(solution)/shard_map/ppermute | solution.py:810
  245.4 7.0 %collective-permute-start.33 = (bf16[64,1152]{1,0:T(8,128)(2,1)S(1)}, bf16[64,1152]{1,0:T(8,128)(2,1)S(1)}, u32[]{:S(2)}, u32[]{:S(2)}) collective-permute-start(bf16[64,1152]{1,0:T(8,128)(2,1)S(1)} %get-tuple-element.329), channel_id=1, source_target_pairs={{0,8},{8,16},{16,24},{24,28},{28,20},{20,12},{12,4},{4,0},{1,9},{9... | collective-permute-start | bytes 442376 | tf_op jit(solution)/shard_map/ppermute | solution.py:787
  247.0 5.9 %collective-permute-start.34 = (bf16[64,1152]{1,0:T(8,128)(2,1)S(1)}, bf16[64,1152]{1,0:T(8,128)(2,1)S(1)}, u32[]{:S(2)}, u32[]{:S(2)}) collective-permute-start(bf16[64,1152]{1,0:T(8,128)(2,1)S(1)} %get-tuple-element.328), channel_id=1, source_target_pairs={{8,0},{16,8},{24,16},{28,24},{20,28},{12,20},{4,12},{0,4},{9,1},{1... | collective-permute-start | bytes 442376 | tf_op jit(solution)/shard_map/ppermute | solution.py:788
  247.6 12.7 %collective-permute-start.37 = (bf16[1,512,256]{2,1,0:T(8,128)(2,1)S(1)}, bf16[1,512,256]{2,1,0:T(8,128)(2,1)S(1)}, u32[]{:S(2)}, u32[]{:S(2)}) collective-permute-start(bf16[1,512,256]{2,1,0:T(8,128)(2,1)S(1)} %get-tuple-element.350), channel_id=1, source_target_pairs={{0,2},{1,3},{2,0},{3,1},{4,6},{5,7},{6,4},{7,5},{8,10},{9,11},{10,... | collective-permute-start | bytes 786440 | tf_op jit(solution)/shard_map/ppermute | solution.py:810
  250.7 22.1 %collective-permute-start.51 = (bf16[128,2048]{1,0:T(8,128)(2,1)S(1)}, bf16[128,2048]{1,0:T(8,128)(2,1)S(1)}, u32[]{:S(2)}, u32[]{:S(2)}) collective-permute-start(bf16[128,2048]{1,0:T(8,128)(2,1)S(1)} %get-tuple-element.313), channel_id=1, source_target_pairs={{0,8},{8,16},{16,24},{24,28},{28,20},{20,12},{12,4},{4,0},{1,9},{9... | collective-permute-start | bytes 1572872 | tf_op jit(solution)/shard_map/ppermute | solution.py:787
  252.4 20.4 %collective-permute-start.52 = (bf16[128,2048]{1,0:T(8,128)(2,1)S(1)}, bf16[128,2048]{1,0:T(8,128)(2,1)S(1)}, u32[]{:S(2)}, u32[]{:S(2)}) collective-permute-start(bf16[128,2048]{1,0:T(8,128)(2,1)S(1)} %get-tuple-element.312), channel_id=1, source_target_pairs={{8,0},{16,8},{24,16},{28,24},{20,28},{12,20},{4,12},{0,4},{9,1},{1... | collective-permute-start | bytes 1572872 | tf_op jit(solution)/shard_map/ppermute | solution.py:788
  254.4 16.1 %collective-permute-start.39 = (bf16[128,1152]{1,0:T(8,128)(2,1)S(1)}, bf16[128,1152]{1,0:T(8,128)(2,1)S(1)}, u32[]{:S(2)}, u32[]{:S(2)}) collective-permute-start(bf16[128,1152]{1,0:T(8,128)(2,1)S(1)} %pad_maximum_fusion.3), channel_id=1, source_target_pairs={{8,0},{16,8},{24,16},{28,24},{20,28},{12,20},{4,12},{0,4},{9,1},{1... | collective-permute-start | bytes 884744 | tf_op jit(solution)/shard_map/ppermute | solution.py:788
  254.9 15.5 %collective-permute-start.38 = (bf16[128,1152]{1,0:T(8,128)(2,1)S(1)}, bf16[128,1152]{1,0:T(8,128)(2,1)S(1)}, u32[]{:S(2)}, u32[]{:S(2)}) collective-permute-start(bf16[128,1152]{1,0:T(8,128)(2,1)S(1)} %pad_maximum_fusion.2), channel_id=1, source_target_pairs={{0,8},{8,16},{16,24},{24,28},{28,20},{20,12},{12,4},{4,0},{1,9},{9... | collective-permute-start | bytes 884744 | tf_op jit(solution)/shard_map/ppermute | solution.py:787
  260.3 24.1 %collective-permute-start.42 = (bf16[2,1024,256]{2,1,0:T(8,128)(2,1)S(1)}, bf16[2,1024,256]{2,1,0:T(8,128)(2,1)S(1)}, u32[]{:S(2)}, u32[]{:S(2)}) collective-permute-start(bf16[2,1024,256]{2,1,0:T(8,128)(2,1)S(1)} %copy-done.46), channel_id=1, source_target_pairs={{0,1},{1,0},{2,3},{3,2},{4,5},{5,4},{6,7},{7,6},{8,9},{9,8},{10,11... | collective-permute-start | bytes 3145736 | tf_op jit(solution)/shard_map/ppermute | solution.py:810
  270.7 9.9 %collective-permute-start.40 = (bf16[128,1152]{1,0:T(8,128)(2,1)S(1)}, bf16[128,1152]{1,0:T(8,128)(2,1)S(1)}, u32[]{:S(2)}, u32[]{:S(2)}) collective-permute-start(bf16[128,1152]{1,0:T(8,128)(2,1)S(1)} %get-tuple-element.323), channel_id=1, source_target_pairs={{0,8},{8,16},{16,24},{24,28},{28,20},{20,12},{12,4},{4,0},{1,9},{9... | collective-permute-start | bytes 884744 | tf_op jit(solution)/shard_map/ppermute | solution.py:787
  271.3 9.8 %collective-permute-start.41 = (bf16[128,1152]{1,0:T(8,128)(2,1)S(1)}, bf16[128,1152]{1,0:T(8,128)(2,1)S(1)}, u32[]{:S(2)}, u32[]{:S(2)}) collective-permute-start(bf16[128,1152]{1,0:T(8,128)(2,1)S(1)} %get-tuple-element.322), channel_id=1, source_target_pairs={{8,0},{16,8},{24,16},{28,24},{20,28},{12,20},{4,12},{0,4},{9,1},{1... | collective-permute-start | bytes 884744 | tf_op jit(solution)/shard_map/ppermute | solution.py:788
  274.8 16.6 %collective-permute-start.53 = (bf16[128,2048]{1,0:T(8,128)(2,1)S(1)}, bf16[128,2048]{1,0:T(8,128)(2,1)S(1)}, u32[]{:S(2)}, u32[]{:S(2)}) collective-permute-start(bf16[128,2048]{1,0:T(8,128)(2,1)S(1)} %get-tuple-element.311), channel_id=1, source_target_pairs={{0,8},{8,16},{16,24},{24,28},{28,20},{20,12},{12,4},{4,0},{1,9},{9... | collective-permute-start | bytes 1572872 | tf_op jit(solution)/shard_map/ppermute | solution.py:787
  275.5 16.9 %collective-permute-start.54 = (bf16[128,2048]{1,0:T(8,128)(2,1)S(1)}, bf16[128,2048]{1,0:T(8,128)(2,1)S(1)}, u32[]{:S(2)}, u32[]{:S(2)}) collective-permute-start(bf16[128,2048]{1,0:T(8,128)(2,1)S(1)} %get-tuple-element.310), channel_id=1, source_target_pairs={{8,0},{16,8},{24,16},{28,24},{20,28},{12,20},{4,12},{0,4},{9,1},{1... | collective-permute-start | bytes 1572872 | tf_op jit(solution)/shard_map/ppermute | solution.py:788
  282.1 14.9 %collective-permute-start.45 = (bf16[128,1152]{1,0:T(8,128)(2,1)}, bf16[128,1152]{1,0:T(8,128)(2,1)}, u32[]{:S(2)}, u32[]{:S(2)}) collective-permute-start(bf16[128,1152]{1,0:T(8,128)(2,1)} %get-tuple-element.321), channel_id=1, source_target_pairs={{0,8},{8,16},{16,24},{24,28},{28,20},{20,12},{12,4},{4,0},{1,9},{9... | collective-permute-start | bytes 884744 | tf_op jit(solution)/shard_map/ppermute | solution.py:787
  283.9 13.1 %collective-permute-start.46 = (bf16[128,1152]{1,0:T(8,128)(2,1)S(1)}, bf16[128,1152]{1,0:T(8,128)(2,1)}, u32[]{:S(2)}, u32[]{:S(2)}) collective-permute-start(bf16[128,1152]{1,0:T(8,128)(2,1)S(1)} %get-tuple-element.320), channel_id=1, source_target_pairs={{8,0},{16,8},{24,16},{28,24},{20,28},{12,20},{4,12},{0,4},{9,1},{1... | collective-permute-start | bytes 884744 | tf_op jit(solution)/shard_map/ppermute | solution.py:788
  286.2 21.5 %collective-permute-start.43 = (bf16[1,512,256]{2,1,0:T(8,128)(2,1)}, bf16[1,512,256]{2,1,0:T(8,128)(2,1)}, u32[]{:S(2)}, u32[]{:S(2)}) collective-permute-start(bf16[1,512,256]{2,1,0:T(8,128)(2,1)} %get-tuple-element.348), channel_id=1, source_target_pairs={{0,2},{1,3},{2,0},{3,1},{4,6},{5,7},{6,4},{7,5},{8,10},{9,11},{10,... | collective-permute-start | bytes 786440 | tf_op jit(solution)/shard_map/ppermute | solution.py:810
  291.4 16.4 %collective-permute-start.44 = (bf16[1,512,256]{2,1,0:T(8,128)(2,1)}, bf16[1,512,256]{2,1,0:T(8,128)(2,1)}, u32[]{:S(2)}, u32[]{:S(2)}) collective-permute-start(bf16[1,512,256]{2,1,0:T(8,128)(2,1)} %get-tuple-element.349), channel_id=1, source_target_pairs={{0,2},{1,3},{2,0},{3,1},{4,6},{5,7},{6,4},{7,5},{8,10},{9,11},{10,... | collective-permute-start | bytes 786440 | tf_op jit(solution)/shard_map/ppermute | solution.py:810
  299.1 1.6 collective-permute-start.55
  301.5 4.4 %collective-permute-start.56 = (f32[128,128]{1,0:T(8,128)S(1)}, f32[128,128]{1,0:T(8,128)S(1)}, u32[]{:S(2)}, u32[]{:S(2)}) collective-permute-start(f32[128,128]{1,0:T(8,128)S(1)} %slice_add_fusion), channel_id=1, source_target_pairs={{0,2},{1,3},{2,0},{3,1},{4,6},{5,7},{6,4},{7,5},{8,10},{9,11},{10,... | collective-permute-start | bytes 196616 | tf_op jit(solution)/shard_map/ppermute | solution.py:802
  (42 other events, 220.7 us)
